TPU v7x, 256 devices: a whole 4x4x8 slice. The times are simulated.
256 devices in a mesh: dp: 8 (over y, x_lo), seq: 32 (over x_hi, z, core).
Axes of the slice: x: 4 (x_hi: 2, x_lo: 2; x = x_hi * 2 + x_lo), y: 4, z: 8, core: 2. Of those that a mesh axis runs over, the one named last changes fastest.
Arguments:
- query_rows: bfloat16 [8, 6144, 512], P('dp', 'seq'), may hold values from -6 to 6
- key_rows: bfloat16 [8, 6144, 512], P('dp', 'seq'), may hold values from -6 to 6
- value_rows: bfloat16 [8, 6144, 512], P('dp', 'seq'), may hold values from -6 to 6
- attention_out: bfloat16 [8, 6144, 512], P('dp', 'seq'), may hold values from -6 to 6
- softmax_log: bfloat16 [8, 6144, 8], P('dp', 'seq'), as said below
- valid_lengths: int32 [8], replicated, may hold values from 3072 to 6144, as said below
- mixer_input: bfloat16 [8, 6144, 1024], P('dp', 'seq'), may hold values from -6 to 6
- upstream_grad: bfloat16 [8, 6144, 1024], P('dp', 'seq'), may hold values from -6 to 6
- output_proj: bfloat16 [512, 1024], replicated, may hold values from -0.25 to 0.25
- depth_kernel: float32 [31, 1024], replicated, may hold values from -1 to 1
Outputs:
- grad_queries: bfloat16 [8, 6144, 512], P('dp', 'seq')
- grad_keys: bfloat16 [8, 6144, 512], P('dp', 'seq')
- grad_values: bfloat16 [8, 6144, 512], P('dp', 'seq')
- grad_state: bfloat16 [8, 6144, 1024], P('dp', 'seq')
- grad_proj: float32 [512, 1024], replicated
- grad_kernel: float32 [31, 1024], replicated
Inputs may be any that keep to these rules, and one draw needn't show every extreme that they name: `valid_lengths`: at least one recording has all 6144 frames valid. `softmax_log`: values lie between the logarithm of 6144 and that plus 1.5.
All inputs are finite; a program needn't handle non-finite values.
Results may differ from a plain program's by a relative error of at most 0.03.
Values may be sent and summed in bfloat16 or wider, within the bound.
No kernel may reach another device: no remote copies, remote signals or barrier semaphores. Data moves between devices by JAX's collectives and lax.ppermute only.
A program may use at most 192 MiB of HBM per device.

v0:
```python
import jax
import jax.numpy as jnp
from jax import lax
from jax.sharding import PartitionSpec as P


def padded_2(array, sides, width):
    for axis, dim in sides:
        devices, length = (lax.axis_size(axis), array.shape[dim])
        up = [(i, (i + 1) % devices) for i in range(devices - 1)]
        down = [(j, i) for i, j in up]
        last = lax.slice_in_dim(array, length - width, length, axis=dim)
        first = lax.slice_in_dim(array, 0, width, axis=dim)
        before = lax.ppermute(last, axis, up)
        after = lax.ppermute(first, axis, down)
        array = jnp.concatenate([before, array, after], axis=dim)
    return array


def taps_forward(padded, tap_weights, row_count):

    def add_tap(tap_index, running_sum):
        window = lax.dynamic_slice_in_dim(padded, tap_index, row_count, 0).astype(jnp.float32)
        return running_sum + tap_weights[tap_index] * window

    return lax.fori_loop(
        0, tap_weights.shape[0], add_tap, jnp.zeros((row_count, padded.shape[1]), jnp.float32)
    )


def taps_backward(padded_grad, tap_weights, row_count):
    last_tap = tap_weights.shape[0] - 1

    def add_tap(tap_index, running_sum):
        window = lax.dynamic_slice_in_dim(padded_grad, last_tap - tap_index, row_count, 0).astype(
            jnp.float32
        )
        return running_sum + tap_weights[tap_index] * window

    return lax.fori_loop(
        0, tap_weights.shape[0], add_tap, jnp.zeros((row_count, padded_grad.shape[1]), jnp.float32)
    )


def taps_product(padded, grad_rows, row_count, tap_count):
    grad_float = grad_rows.astype(jnp.float32)

    def one_tap(tap_index):
        window = lax.dynamic_slice_in_dim(padded, tap_index, row_count, 0).astype(jnp.float32)
        return jnp.sum(window * grad_float, axis=0)

    return lax.map(one_tap, jnp.arange(tap_count, dtype=jnp.int32))


def swish_grad(conv_pre, masked_grad):
    sigmoid_pre = jax.nn.sigmoid(conv_pre)
    return (
        masked_grad.astype(jnp.float32) * sigmoid_pre * (1.0 + conv_pre * (1.0 - sigmoid_pre))
    ).astype(jnp.bfloat16)


def score_parts(query_heads, key_heads, value_heads, grad_heads, log_rows, delta_rows, key_mask):
    scores = (
        jnp.einsum("thd,uhd->htu", query_heads, key_heads, preferred_element_type=jnp.float32)
        * 0.125
    )
    soft_probs = jnp.exp(scores - log_rows[:, :, None]) * key_mask[None, None, :]
    grad_probs = jnp.einsum(
        "thd,uhd->htu", grad_heads, value_heads, preferred_element_type=jnp.float32
    )
    grad_scores = (soft_probs * (grad_probs - delta_rows[:, :, None])).astype(jnp.bfloat16)
    return (soft_probs.astype(jnp.bfloat16), grad_scores)


def shards(
    query_rows,
    key_rows,
    value_rows,
    attention_out,
    softmax_log,
    valid_lengths,
    mixer_input,
    upstream_grad,
    output_proj,
    depth_kernel,
):
    shard_rows = query_rows.shape[1]
    proj_width = query_rows.shape[2]
    head_count = softmax_log.shape[2]
    head_size = proj_width // head_count
    tap_count = depth_kernel.shape[0]
    rim_width = tap_count // 2
    shard_index = lax.axis_index("seq")
    first_row = shard_index * shard_rows
    rec_length = lax.dynamic_index_in_dim(valid_lengths, lax.axis_index("dp"), 0, keepdims=False)
    row_offsets = jnp.arange(shard_rows, dtype=jnp.int32)
    keep_mask = (first_row + row_offsets < rec_length).astype(jnp.float32)
    keep_half = keep_mask.astype(jnp.bfloat16)[:, None]
    masked_in = mixer_input[0] * keep_half
    masked_grad = upstream_grad[0] * keep_half
    padded_in = padded_2(masked_in, (("seq", 0),), rim_width)
    conv_pre = taps_forward(padded_in, depth_kernel, shard_rows)
    grad_pre = swish_grad(conv_pre, masked_grad)
    padded_grad = padded_2(grad_pre, (("seq", 0),), rim_width)
    conv_back = taps_backward(padded_grad, depth_kernel, shard_rows)
    kernel_grad = taps_product(padded_in, grad_pre, shard_rows, tap_count)
    grad_state = (masked_grad.astype(jnp.float32) + keep_mask[:, None] * conv_back).astype(
        jnp.bfloat16
    )
    grad_out = lax.dot_general(
        grad_state, output_proj, (((1,), (1,)), ((), ())), preferred_element_type=jnp.float32
    ).astype(jnp.bfloat16)
    proj_part = lax.dot_general(
        attention_out[0], grad_state, (((0,), (0,)), ((), ())), preferred_element_type=jnp.float32
    )
    proj_sum, kernel_sum = lax.psum((proj_part, kernel_grad), ("dp", "seq"))
    grad_scale = 1.0 / jnp.sqrt(jnp.sum(valid_lengths).astype(jnp.float32))
    query_heads = query_rows[0].reshape(shard_rows, head_count, head_size)
    key_heads = key_rows[0].reshape(shard_rows, head_count, head_size)
    value_heads = value_rows[0].reshape(shard_rows, head_count, head_size)
    grad_heads = grad_out.reshape(shard_rows, head_count, head_size)
    out_heads = attention_out[0].reshape(shard_rows, head_count, head_size)
    log_half = softmax_log[0]
    log_rows = log_half.astype(jnp.float32).T
    delta_half = jnp.sum(
        grad_heads.astype(jnp.float32) * out_heads.astype(jnp.float32), axis=-1
    ).astype(jnp.bfloat16)
    delta_rows = delta_half.astype(jnp.float32).T
    key_piece = lax.all_gather(key_rows[0], "seq", axis=0, tiled=True)
    value_piece = lax.all_gather(value_rows[0], "seq", axis=0, tiled=True)
    piece_rows = key_piece.shape[0]
    key_mask = (jnp.arange(piece_rows, dtype=jnp.int32) < rec_length).astype(jnp.float32)
    piece_keys = key_piece.reshape(piece_rows, head_count, head_size)
    piece_values = value_piece.reshape(piece_rows, head_count, head_size)
    unused_probs, grad_scores = score_parts(
        query_heads, piece_keys, piece_values, grad_heads, log_rows, delta_rows, key_mask
    )
    grad_q = jnp.einsum("htu,uhd->thd", grad_scores, piece_keys, preferred_element_type=jnp.float32)
    query_piece = lax.all_gather(query_rows[0], "seq", axis=0, tiled=True)
    grad_piece = lax.all_gather(grad_out, "seq", axis=0, tiled=True)
    delta_piece = lax.all_gather(delta_half, "seq", axis=0, tiled=True)
    log_piece = lax.all_gather(log_half, "seq", axis=0, tiled=True)
    piece_rows = query_piece.shape[0]
    piece_queries = query_piece.reshape(piece_rows, head_count, head_size)
    piece_grads = grad_piece.reshape(piece_rows, head_count, head_size)
    probs_half, grad_scores = score_parts(
        piece_queries,
        key_heads,
        value_heads,
        piece_grads,
        log_piece.astype(jnp.float32).T,
        delta_piece.astype(jnp.float32).T,
        keep_mask,
    )
    key_sum = jnp.einsum(
        "htu,thd->uhd", grad_scores, piece_queries, preferred_element_type=jnp.float32
    )
    value_sum = jnp.einsum(
        "htu,thd->uhd", probs_half, piece_grads, preferred_element_type=jnp.float32
    )
    grad_queries = (grad_q * 0.125).reshape(1, shard_rows, proj_width).astype(jnp.bfloat16)
    grad_keys = (key_sum * 0.125).reshape(1, shard_rows, proj_width).astype(jnp.bfloat16)
    grad_values = value_sum.reshape(1, shard_rows, proj_width).astype(jnp.bfloat16)
    return (
        grad_queries,
        grad_keys,
        grad_values,
        grad_state[None],
        proj_sum * grad_scale,
        kernel_sum * grad_scale,
    )


def solution(mesh):
    in_specs = (
        P("dp", "seq", None),
        P("dp", "seq", None),
        P("dp", "seq", None),
        P("dp", "seq", None),
        P("dp", "seq", None),
        P(),
        P("dp", "seq", None),
        P("dp", "seq", None),
        P(),
        P(),
    )
    out_specs = (
        P("dp", "seq", None),
        P("dp", "seq", None),
        P("dp", "seq", None),
        P("dp", "seq", None),
        P(),
        P(),
    )
    return jax.shard_map(shards, mesh=mesh, in_specs=in_specs, out_specs=out_specs, check_vma=False)
```

profile of v0, /device:TPU:1, one launch (start us, length us, event | category | flops | bytes accessed | tf_op | source)
XLA Modules:
  0.0 708.4 jit_solution(3300434665411013344)
XLA Ops:
  11.3 5.1 collective-permute-start.1
  16.4 1.9 collective-permute-start
  19.7 35.5 %while.41 = (s32[]{:T(128)}, f32[192,1024]{1,0:T(8,128)S(1)}, f32[31,1024]{1,0:T(8,128)}, bf16[222,1024]{1,0:T(8,128)(2,1)S(1)}, s32[]{:T(128)}, /*index=5*/s32[]{:T(128)}) while((s32[]{:T(128)}, f32[192,1024]{1,0:T(8,128)S(1)}, f32[31,1024]{1,0:T(8,128)}, bf16[222,1024]{1,0:T(8,128)(2,1)S(1)}, s32[]{:T(128)}, ...), condition=%wide.region_1.2_spmd.clone, body=%wide.region_0.1_spmd.clone.sunk | while | flops 786435 | bytes 1978463 | solution.py:26
  55.1 2.2 fusion.26
  57.3 2.2 collective-permute-start.3
  59.6 3.9 collective-permute-start.2
  63.5 161.5 %while.40 = (s32[]{:T(128)}, f32[31,1024]{1,0:T(8,128)}, s32[31]{0:T(128)S(1)}, bf16[222,1024]{1,0:T(8,128)(2,1)S(1)}, f32[192,1024]{1,0:T(8,128)}, /*index=5*/s32[]{:T(128)}, s32[]{:T(128)}, s32[]{:T(128)}) while((s32[]{:T(128)}, f32[31,1024]{1,0:T(8,128)}, s32[31]{0:T(128)S(1)}, bf16[222,1024]{1,0:T(8,128)(2,1)S(1)}, ...), condition=%wide.region_9.10_spmd, body=%wide.region_7.9_spmd.sunk | while | flops 588805 | bytes 1192083 | solution.py:52
  225.1 35.6 %while.42 = (s32[]{:T(128)}, f32[192,1024]{1,0:T(8,128)S(1)}, f32[31,1024]{1,0:T(8,128)}, bf16[222,1024]{1,0:T(8,128)(2,1)S(1)}, s32[]{:T(128)}, /*index=5*/s32[]{:T(128)}, s32[]{:T(128)}, s32[]{:T(128)}) while((s32[]{:T(128)}, f32[192,1024]{1,0:T(8,128)S(1)}, f32[31,1024]{1,0:T(8,128)}, bf16[222,1024]{1,0:T(8,128)(2,1)S(1)}, ...), condition=%wide.region_3.4_spmd.clone, body=%wide.region_2.3_spmd.clone.sunk | while | flops 786439 | bytes 1978525 | solution.py:40
  271.6 55.6 %all-gather.3 = bf16[1,6144,8]{2,0,1:T(2,128)(2,1)S(1)} all-gather(bf16[1,192,8]{2,0,1:T(2,128)(2,1)S(1)} %copy.61), channel_id=5, replica_groups=mesh['dp'=8,'seq'=32] {'seq'}, dimensions={1}, use_global_device_ids=true | all-gather | bytes 101376 | tf_op jit(solution)/shard_map/all_gather | solution.py:142
  327.2 4.6 transpose.84
  331.8 3.0 copy.62
  338.0 37.2 %all-gather.4 = bf16[32,192,8]{1,2,0:T(8,128)(2,1)S(1)} all-gather(bf16[1,192,8]{1,2,0:T(8,128)(2,1)S(1)} %bitcast.99), channel_id=1, replica_groups=mesh['dp'=8,'seq'=32] {'seq'}, dimensions={0}, use_global_device_ids=true | all-gather | bytes 101376 | tf_op jit(solution)/shard_map/all_gather | solution.py:141
  376.1 188.1 %all-reduce.3.cloned.1.call-done = (f32[512,1024]{0,1:T(8,128)}, f32[31,1024]{1,0:T(8,128)}) async-done(((f32[512,1024]{0,1:T(8,128)}, f32[31,1024]{1,0:T(8,128)}), (f32[512,1024]{0,1:T(8,128)}, f32[31,1024]{1,0:T(8,128)})) %all-reduce.3.cloned.1.call-update) | async-done | bytes 2224144 | tf_op jit(solution)/shard_map/psum | solution.py:116
  564.2 1.8 broadcast_multiply_fusion
  566.1 1.8 copy.69
  569.4 8.7 %copy.55 = bf16[1,6144,512]{1,2,0:T(8,128)(2,1)} copy(bf16[1,6144,512]{2,1,0:T(8,128)(2,1)} %all-gather.12.cloned.1.call-done) | data formatting | bytes 12582912 | tf_op jit(solution)/shard_map/all_gather | solution.py:129
  578.1 8.7 %copy.57 = bf16[1,6144,512]{1,2,0:T(8,128)(2,1)} copy(bf16[1,6144,512]{2,1,0:T(8,128)(2,1)} %all-gather.14.cloned.1.call-done) | data formatting | bytes 12582912 | tf_op jit(solution)/shard_map/all_gather | solution.py:130
  586.8 16.7 %fusion.30 = f32[8,192,6144]{2,1,0:T(8,128)} fusion(bf16[192,8,64]{0,2,1:T(8,128)(2,1)S(1)} %bitcast.88, bf16[6144,8,64]{0,2,1:T(8,128)(2,1)} %bitcast.80), kind=kOutput, calls=%fused_computation.48 | convolution fusion | flops 1207959552 | bytes 44236800 | tf_op jit(solution)/shard_map/thd,uhd->htu/dot_general | solution.py:64
  603.5 22.0 %fusion.11 = bf16[8,192,64]{1,2,0:T(8,128)(2,1)S(1)} fusion(bf16[6144,8,64]{0,2,1:T(8,128)(2,1)} %bitcast.81, f32[8,192,6144]{2,1,0:T(8,128)} %fusion.30, f32[8,192]{1,0:T(8,128)S(1)} %convert_bitcast_fusion.1, f32[6144]{0:T(1024)S(1)} %copy-done.7, f32[8,192]{1,0:T(8,128)S(1)} %convert_bitcast_fusion, bf16[192,8,64]{0,2,1:T(8,128)(2,1)S(1)} %bitcast.89, ...), kind=kOutput, calls=%fused_computation.17 | convolution fusion | flops 2472738816 | bytes 50761728 | tf_op jit(solution)/shard_map/htu,uhd->thd/dot_general | solution.py:138
  626.3 8.7 %copy.59 = bf16[1,6144,512]{1,2,0:T(8,128)(2,1)} copy(bf16[1,6144,512]{2,1,0:T(8,128)(2,1)} %all-gather.16.cloned.1.call-done) | data formatting | bytes 12582912 | tf_op jit(solution)/shard_map/all_gather | solution.py:139
  635.0 17.1 %fusion.31 = f32[8,6144,192]{1,2,0:T(8,128)} fusion(bf16[6144,8,64]{0,2,1:T(8,128)(2,1)} %bitcast.78, bf16[192,8,64]{0,2,1:T(8,128)(2,1)S(1)} %bitcast.87), kind=kOutput, calls=%fused_computation.49 | convolution fusion | flops 1207959552 | bytes 44236800 | tf_op jit(solution)/shard_map/thd,uhd->htu/dot_general | solution.py:64
  652.1 8.7 %copy.63 = bf16[6144,512]{0,1:T(8,128)(2,1)} copy(bf16[6144,512]{1,0:T(8,128)(2,1)} %all-gather.10.cloned.1.call-done) | data formatting | bytes 12582912 | tf_op jit(solution)/shard_map/all_gather | solution.py:140
  660.7 16.8 %fusion.13 = bf16[8,64,192]{2,1,0:T(8,128)(2,1)S(1)} fusion(bf16[6144,8,64]{0,2,1:T(8,128)(2,1)} %bitcast.84, f32[8,6144,192]{1,2,0:T(8,128)} %fusion.31, f32[192]{0:T(256)S(1)} %get-tuple-element.313, f32[8,6144]{1,0:T(8,128)S(1)} %copy-done.5), kind=kOutput, calls=%fused_computation.19 | convolution fusion | flops 1245806592 | bytes 44434176 | tf_op jit(solution)/shard_map/htu,thd->uhd/dot_general | solution.py:158
  677.6 21.6 %fusion.12 = bf16[8,192,64]{1,2,0:T(8,128)(2,1)S(1)} fusion(bf16[6144,8,64]{0,2,1:T(8,128)(2,1)} %bitcast.79, f32[8,6144,192]{1,2,0:T(8,128)} %fusion.31, f32[8,6144]{1,0:T(8,128)S(1)} %bitcast.98, f32[192]{0:T(256)S(1)} %get-tuple-element.313, f32[8,6144]{1,0:T(8,128)S(1)} %copy-done.5, bf16[6144,8,64]{0,2,1:T(8,128)(2,1)} %bitcast.85, ...), kind=kOutput, calls=%fused_computation.18 | convolution fusion | flops 2472738816 | bytes 51118848 | tf_op jit(solution)/shard_map/htu,thd->uhd/dot_general | solution.py:155
  (286 shorter events, 193.6 us)
Async XLA Ops:
  8.0 257.6 %copy-start = (bf16[512,1024]{1,0:T(8,128)(2,1)S(1)}, bf16[512,1024]{1,0:T(8,128)(2,1)}, u32[]{:S(2)}) copy-start(bf16[512,1024]{1,0:T(8,128)(2,1)} %param.24) | copy-start | bytes 3145732
  8.0 556.2 %all-reduce.3.cloned.1.call-start = ((), (), s32[]{:S(2)}) async-start(), calls=%async_computation.4 | async-start | bytes 4456448 | tf_op jit(solution)/shard_map/psum | solution.py:116
  11.3 7.1 %collective-permute-start.1 = (bf16[15,1024]{1,0:T(8,128)(2,1)S(1)}, bf16[15,1024]{1,0:T(8,128)(2,1)S(1)}, u32[]{:S(2)}, u32[]{:S(2)}) collective-permute-start(bf16[15,1024]{1,0:T(8,128)(2,1)S(1)} %get-tuple-element.312), channel_id=1, source_target_pairs={{1,0},{2,1},{3,2},{4,3},{5,4},{6,5},{7,6},{8,7},{9,8},{10,9},{11,1... | collective-permute-start | bytes 92168 | tf_op jit(solution)/shard_map/ppermute | solution.py:15
  16.4 3.1 collective-permute-start
  19.6 251.2 %copy-start.9 = (s32[8]{0:T(128)S(1)}, s32[8]{0:T(128)}, u32[]{:S(2)}) copy-start(s32[8]{0:T(128)} %param.21) | copy-start | bytes 100
  19.7 251.8 %copy-start.8 = (bf16[1,192,8]{1,2,0:T(8,128)(2,1)S(1)}, bf16[1,192,8]{1,2,0:T(8,128)(2,1)}, u32[]{:S(2)}) copy-start(bf16[1,192,8]{1,2,0:T(8,128)(2,1)} %param.20) | copy-start | bytes 9220
  57.3 204.6 %copy-start.3 = (bf16[1,192,512]{2,1,0:T(8,128)(2,1)S(1)}, bf16[1,192,512]{2,1,0:T(8,128)(2,1)}, u32[]{:S(2)}) copy-start(bf16[1,192,512]{2,1,0:T(8,128)(2,1)} %param.19) | copy-start | bytes 589828
  57.3 167.7 %collective-permute-start.3 = (bf16[15,1024]{1,0:T(8,128)(2,1)S(1)}, bf16[15,1024]{1,0:T(8,128)(2,1)S(1)}, u32[]{:S(2)}, u32[]{:S(2)}) collective-permute-start(bf16[15,1024]{1,0:T(8,128)(2,1)S(1)} %get-tuple-element.310), channel_id=1, source_target_pairs={{1,0},{2,1},{3,2},{4,3},{5,4},{6,5},{7,6},{8,7},{9,8},{10,9},{11,1... | collective-permute-start | bytes 92168 | tf_op jit(solution)/shard_map/ppermute | solution.py:15
  59.6 165.5 %collective-permute-start.2 = (bf16[15,1024]{1,0:T(8,128)(2,1)S(1)}, bf16[15,1024]{1,0:T(8,128)(2,1)S(1)}, u32[]{:S(2)}, u32[]{:S(2)}) collective-permute-start(bf16[15,1024]{1,0:T(8,128)(2,1)S(1)} %get-tuple-element.309), channel_id=1, source_target_pairs={{0,1},{1,2},{2,3},{3,4},{4,5},{5,6},{6,7},{7,8},{8,9},{9,10},{10,1... | collective-permute-start | bytes 92168 | tf_op jit(solution)/shard_map/ppermute | solution.py:14
  262.0 316.2 %copy-start.2 = (bf16[192,1024]{1,0:T(8,128)(2,1)}, bf16[192,1024]{1,0:T(8,128)(2,1)S(1)}, u32[]{:S(2)}) copy-start(bf16[192,1024]{1,0:T(8,128)(2,1)S(1)} %fusion.18) | copy-start | bytes 1179652
  263.8 305.7 %all-gather.12.cloned.1.call-start = ((), (), s32[]{:S(2)}) async-start(), calls=%async_computation.1 | async-start | bytes 6488064 | tf_op jit(solution)/shard_map/all_gather | solution.py:129
  264.4 313.8 %all-gather.14.cloned.1.call-start = ((), (), s32[]{:S(2)}) async-start(), calls=%async_computation.2 | async-start | bytes 6488064 | tf_op jit(solution)/shard_map/all_gather | solution.py:130
  264.9 361.4 %all-gather.16.cloned.1.call-start = ((), (), s32[]{:S(2)}) async-start(), calls=%async_computation.3 | async-start | bytes 6488064 | tf_op jit(solution)/shard_map/all_gather | solution.py:139
  265.5 386.5 %all-gather.10.cloned.1.call-start = ((), (), s32[]{:S(2)}) async-start(), calls=%async_computation | async-start | bytes 6488064 | tf_op jit(solution)/shard_map/all_gather | solution.py:140
  586.8 16.7 %copy-start.7 = (f32[6144]{0:T(1024)S(1)}, f32[6144]{0:T(1024)}, u32[]{:S(2)}) copy-start(f32[6144]{0:T(1024)} %fusion.21) | copy-start | bytes 73732
  635.0 25.8 %copy-start.5 = (f32[8,6144]{1,0:T(8,128)S(1)}, f32[8,6144]{1,0:T(8,128)}, u32[]{:S(2)}) copy-start(f32[8,6144]{1,0:T(8,128)} %copy.62) | copy-start | bytes 589828
  660.7 16.9 %copy-start.4 = (bf16[1,192,512]{1,2,0:T(8,128)(2,1)S(1)}, bf16[1,192,512]{1,2,0:T(8,128)(2,1)}, u32[]{:S(2)}) copy-start(bf16[1,192,512]{1,2,0:T(8,128)(2,1)} %copy.64) | copy-start | bytes 589828
  660.7 16.9 %copy-start.6 = (f32[6144,8]{0,1:T(8,128)S(1)}, f32[6144,8]{0,1:T(8,128)}, u32[]{:S(2)}) copy-start(f32[6144,8]{0,1:T(8,128)} %reshape.112) | copy-start | bytes 589828
  677.6 23.2 %copy-start.1 = (bf16[512,1024]{1,0:T(8,128)(2,1)S(1)}, bf16[512,1024]{1,0:T(8,128)(2,1)}, u32[]{:S(2)}) copy-start(bf16[512,1024]{1,0:T(8,128)(2,1)} %param.24) | copy-start | bytes 3145732
Sparse Core Ops, SparseCore 0:
  263.9 300.2 all-reduce.2
Sparse Core Ops, SparseCore 1:
  267.0 101.6 all-gather.11
  371.3 91.1 all-gather.13
  465.2 91.5 all-gather.15
  560.1 90.5 all-gather.9
where the time goes:
time: 719 us; the launch traced here: 708 us
  waiting for transfers between devices  191 us (27%)
  local copies, waits for them, and re-layouts  158 us (22%)
  matrix products  97.2 us (14%)
  blocking collectives  92.8 us (13%)
  other arithmetic  77.4 us (11%)
  loops' own time  61.6 us (9%)
  between operations  16.7 us (2%)
  starting transfers between devices  13.4 us (2%)
    psum x1, waiting for transfers between devices, shards(): proj_sum, kernel_sum = lax.psum((proj_part, kernel_grad), ('dp', 'seq'))  188 us
    another operation x1, loops' own time, taps_product(): return lax.map(one_tap, jnp.arange(tap_count, dtype=jnp.int32))  60.3 us
    all_gather x1, blocking collectives, shards(): log_piece = lax.all_gather(log_half, 'seq', axis=0, tiled=True)  55.6 us
    dynamic_slice x62, local copies, waits for them, and re-layouts, add_tap(): return running_sum + tap_weights[tap_index] * window  47.6 us
    dynamic_update_slice x31, local copies, waits for them, and re-layouts, taps_product(): return lax.map(one_tap, jnp.arange(tap_count, dtype=jnp.int32))  43.3 us
    reduce_sum x31, other arithmetic, one_tap(): return jnp.sum(window * grad_float, axis=0)  39.9 us
    all_gather x1, blocking collectives, shards(): delta_piece = lax.all_gather(delta_half, 'seq', axis=0, tiled=True)  37.2 us
    dot_general x2, matrix products, score_parts(): jnp.einsum('thd,uhd->htu', query_heads, key_heads, preferred_element_type...  33.8 us
  transfers between devices with their start and end apart: 9, of which 2 were waited for; matrix products, arithmetic and copies ran while one was open for 29% of the time, Pallas kernels for 0%

commit v1 on v0

v1 whole, which is shorter than its diff:
```python
import functools

import jax
import jax.numpy as jnp
from jax import lax
from jax.experimental import pallas as pl
from jax.experimental.pallas import tpu as pltpu
from jax.sharding import Mesh, PartitionSpec as P

BF = jnp.bfloat16
F32 = jnp.float32
NT = (((1,), (1,)), ((), ()))
NN = (((1,), (0,)), ((), ()))
TN = (((0,), (0,)), ((), ()))
ROWS = 192
HALF = 96
HEADS = 8
HSIZE = 64
TAPS = 31
ALL = ("dp", "xh", "z", "core")
SEQ = ("xh", "z", "core")
VMEM_LIMIT = 56 << 20


def call(kernel, out_shape, cost=None, **kw):
    return pl.pallas_call(
        kernel,
        out_shape=out_shape,
        compiler_params=pltpu.CompilerParams(vmem_limit_bytes=VMEM_LIMIT),
        cost_estimate=cost,
        **kw,
    )


def sds(shape, dtype=BF):
    return jax.ShapeDtypeStruct(shape, dtype)


def pack_early(q_ref, k_ref, v_ref, o_ref):
    for h in range(HEADS):
        cols = slice(h * HSIZE, (h + 1) * HSIZE)
        o_ref[h, 0:ROWS, 0:HSIZE] = k_ref[0, :, cols]
        o_ref[h, 0:ROWS, HSIZE:128] = v_ref[0, :, cols]
        q = q_ref[0, :, cols] * BF(0.125)
        o_ref[h, ROWS : ROWS + HALF, 0:HSIZE] = q[:HALF]
        o_ref[h, ROWS : ROWS + HALF, HSIZE:128] = q[HALF:]


def conv_kernel(
    pos_ref,
    x_ref,
    g_ref,
    lo_ref,
    hi_ref,
    w_ref,
    proj_ref,
    attn_ref,
    log_ref,
    gs_ref,
    pk_ref,
    late_ref,
    xs,
    gm,
    gp,
    out_acc,
    attn_t,
    tmp,
):
    step = pl.program_id(0)
    first_row = pos_ref[0]
    length = pos_ref[1]

    @pl.when(step == 0)
    def _():
        out_acc[...] = jnp.zeros_like(out_acc)
        attn_t[...] = attn_ref[0].T

    def mask(rows, offset):
        at = first_row + offset + lax.broadcasted_iota(jnp.int32, (rows, 128), 0)
        return jnp.where((at >= 0) & (at < length), 1.0, 0.0).astype(F32)

    mask_x = mask(256, -32)
    mask_g = mask(224, -16)
    for half in range(2):
        cols = slice(half * 128, half * 128 + 128)
        xs[0:32, :] = lo_ref[0:32, cols].astype(F32) * mask_x[0:32]
        xs[32:224, :] = x_ref[0, :, cols].astype(F32) * mask_x[32:224]
        xs[224:256, :] = hi_ref[0:32, cols].astype(F32) * mask_x[224:256]
        gm[0:16, :] = lo_ref[32:48, cols].astype(F32) * mask_g[0:16]
        gm[16:208, :] = g_ref[0, :, cols].astype(F32) * mask_g[16:208]
        gm[208:224, :] = hi_ref[32:48, cols].astype(F32) * mask_g[208:224]
        pre = jnp.zeros((224, 128), F32)
        for j in range(TAPS):
            pre = pre + w_ref[j : j + 1, cols] * xs[1 + j : 225 + j, :]
        s = jax.nn.sigmoid(pre)
        gp[...] = (gm[...] * s * (1.0 + pre * (1.0 - s))).astype(BF).astype(F32)
        back = jnp.zeros((ROWS, 128), F32)
        for j in range(TAPS):
            back = back + w_ref[j : j + 1, cols] * gp[31 - j : 223 - j, :]
        gs = (gm[16:208, :] + mask_g[16:208] * back).astype(BF)
        gs_ref[0, :, cols] = gs
        out_acc[...] += lax.dot_general(
            gs, proj_ref[:, cols], NT, preferred_element_type=F32
        )
        pk_ref[half, 0:512, :] = lax.dot_general(
            attn_t[...], gs, NN, preferred_element_type=F32
        ).astype(BF)
        own = gp[16:208, :]
        rows = [
            jnp.sum(xs[17 + j : 209 + j, :] * own, axis=0, keepdims=True) for j in range(TAPS)
        ]
        rows.append(jnp.zeros((1, 128), F32))
        pk_ref[half, 512:544, :] = jnp.concatenate(rows, axis=0).astype(BF)

    @pl.when(step == pl.num_programs(0) - 1)
    def _():
        grad = out_acc[...].astype(BF)
        tmp[0:ROWS, :] = grad.astype(F32) * attn_ref[0].astype(F32)
        tmp[ROWS:256, :] = jnp.zeros((256 - ROWS, 512), F32)
        turned = tmp[...].T
        tmp[0:ROWS, 0:128] = jnp.concatenate(
            [log_ref[0].astype(F32), jnp.zeros((ROWS, 120), F32)], axis=1
        )
        logs = tmp[:, 0:128].T
        for h in range(HEADS):
            delta = jnp.sum(turned[h * HSIZE : (h + 1) * HSIZE], axis=0, keepdims=True)
            log_row = logs[h : h + 1]
            part = grad[:, h * HSIZE : (h + 1) * HSIZE]
            late_ref[h, 0:HALF, 0:HSIZE] = part[:HALF]
            late_ref[h, 0:HALF, HSIZE:128] = part[HALF:]
            late_ref[h, HALF : HALF + 16, :] = jnp.concatenate(
                [
                    delta[:, 0:128],
                    delta[:, 128:256],
                    log_row[:, 0:128],
                    log_row[:, 128:256],
                    jnp.zeros((12, 128), F32),
                ],
                axis=0,
            ).astype(BF)


def conv_call(pos, x, g, lo, hi, w, proj, attn, log):
    chunk = lambda i, *_: (0, 0, i)
    flat = lambda i, *_: (0, i)
    full3 = lambda i, *_: (0, 0, 0)
    return pl.pallas_call(
        conv_kernel,
        out_shape=(
            sds((1, ROWS, 1024)),
            sds((8, 544, 128)),
            sds((HEADS, HALF + 16, 128)),
        ),
        grid_spec=pltpu.PrefetchScalarGridSpec(
            num_scalar_prefetch=1,
            grid=(4,),
            in_specs=[
                pl.BlockSpec((1, ROWS, 256), chunk),
                pl.BlockSpec((1, ROWS, 256), chunk),
                pl.BlockSpec((48, 256), flat),
                pl.BlockSpec((48, 256), flat),
                pl.BlockSpec((TAPS, 256), flat),
                pl.BlockSpec((512, 256), flat),
                pl.BlockSpec((1, ROWS, 512), full3),
                pl.BlockSpec((1, ROWS, HEADS), full3),
            ],
            out_specs=[
                pl.BlockSpec((1, ROWS, 256), chunk),
                pl.BlockSpec((2, 544, 128), lambda i, *_: (i, 0, 0)),
                pl.BlockSpec((HEADS, HALF + 16, 128), full3),
            ],
            scratch_shapes=[
                pltpu.VMEM((256, 128), F32),
                pltpu.VMEM((224, 128), F32),
                pltpu.VMEM((224, 128), F32),
                pltpu.VMEM((ROWS, 512), F32),
                pltpu.VMEM((512, ROWS), BF),
                pltpu.VMEM((256, 512), F32),
            ],
        ),
        compiler_params=pltpu.CompilerParams(vmem_limit_bytes=VMEM_LIMIT),
    )(pos, x, g, lo, hi, w, proj, attn, log)


CALLS = 8
CHUNK = HEADS * ROWS
KEYS = 2 * CHUNK // CALLS
BT = 1024


def unpack_rows(x, blk, dst):
    left, right = x[:, 0:HSIZE], x[:, HSIZE:128]
    dst[blk * 128 : blk * 128 + 96, :] = left
    dst[blk * 128 + 96 : blk * 128 + 128, :] = right[0:32]
    dst[2048 + blk * 64 : 2048 + blk * 64 + 64, :] = right[32:96]


def prep_early(pos_ref, own_ref, qc_ref, kvx_ref, q_ref, k_ref, v_ref, kt_ref, kf):
    length = pos_ref[0]
    for z in range(8):
        unpack_rows(own_ref[z, ROWS : ROWS + HALF, :], z, q_ref)
        unpack_rows(qc_ref[z], 8 + z, q_ref)
    for c in range(2):
        for z in range(8):
            kv = kvx_ref[z] if c == 0 else own_ref[z, 0:ROWS, :]
            at = c * CHUNK + z * ROWS
            k_ref[at : at + ROWS, :] = kv[:, 0:HSIZE]
            v_ref[at : at + ROWS, :] = kv[:, HSIZE:128]
            row = pos_ref[1 + c] + z * 2 * ROWS
            row = row + lax.broadcasted_iota(jnp.int32, (ROWS, 128), 0)
            kf[at : at + ROWS, :] = jnp.where(row < length, kv.astype(F32) * 0.125, 0.0)
    for b in range(2 * CHUNK // 512):
        turned = kf[b * 512 : b * 512 + 512, :].T
        kt_ref[:, b * 512 : b * 512 + 512] = turned[0:HSIZE].astype(BF)


def prep_late(own_ref, core_ref, do_ref, st_ref):
    stats = []
    for c, ref in enumerate((own_ref, core_ref)):
        for z in range(8):
            blk = c * 8 + z
            unpack_rows(ref[z, 0:HALF, :], blk, do_ref)
            st = ref[z, HALF : HALF + 16, :].astype(F32)
            st_ref[0:1, blk * 128 : blk * 128 + 128] = st[0:1]
            st_ref[1:2, blk * 128 : blk * 128 + 128] = st[2:3]
            stats.append(st)
    lane = lax.broadcasted_iota(jnp.int32, (1, 128), 1)
    for m in range(8):
        a, b = stats[2 * m], stats[2 * m + 1]
        at = 2048 + m * 128
        for row in range(2):
            src = 2 * row + 1
            st_ref[row : row + 1, at : at + 128] = jnp.where(
                lane < 64, a[src : src + 1], pltpu.roll(b[src : src + 1], 64, 1)
            )


def attn_kernel(first, part, pos_ref, q, do, st, k, v, kt, *rest):
    dqt = rest[-1]
    dkv_ref = rest[-2]
    if first:
        dqt[...] = jnp.zeros_like(dqt)
    else:
        dqt[...] = rest[0][...]
    kb, vb, ktb = k[...], v[...], kt[...]

    def query_block(ti, carry):
        dk, dv = carry
        t0 = pl.multiple_of(ti * BT, BT)
        qb = q[pl.ds(t0, BT), :]
        dob = do[pl.ds(t0, BT), :]
        s = lax.dot_general(kb, qb, NT, preferred_element_type=F32)
        p = jnp.exp(s - st[1:2, pl.ds(t0, BT)])
        dp = lax.dot_general(vb, dob, NT, preferred_element_type=F32)
        ds = (p * (dp - st[0:1, pl.ds(t0, BT)])).astype(BF)
        dv = dv + lax.dot_general(p.astype(BF), dob, NN, preferred_element_type=F32)
        dk = dk + lax.dot_general(ds, qb, NN, preferred_element_type=F32)
        dqt[:, pl.ds(t0, BT)] += lax.dot_general(ktb, ds, NN, preferred_element_type=F32)
        return dk, dv

    zero = jnp.zeros((KEYS, HSIZE), F32)
    dk, dv = lax.fori_loop(0, 2 * CHUNK // BT, query_block, (zero, zero))
    c, z0 = divmod(part * KEYS // ROWS, 8)
    for i in range(KEYS // ROWS):
        row = pos_ref[1 + c] + (z0 + i) * 2 * ROWS
        row = row + lax.broadcasted_iota(jnp.int32, (ROWS, HSIZE), 0)
        keep = row < pos_ref[0]
        rows = slice(i * ROWS, i * ROWS + ROWS)
        dkv_ref[i, :, 0:HSIZE] = jnp.where(keep, dk[rows], 0.0).astype(BF)
        dkv_ref[i, :, HSIZE:128] = jnp.where(keep, dv[rows], 0.0).astype(BF)


def attn_call(part, pos, q, do, st, k, v, kt, dqt):
    first = dqt is None
    full = lambda *_: (0, 0)
    rows = lambda *_: (part, 0)
    specs = [
        pl.BlockSpec((2 * CHUNK, HSIZE), full),
        pl.BlockSpec((2 * CHUNK, HSIZE), full),
        pl.BlockSpec((8, 2 * CHUNK), full),
        pl.BlockSpec((KEYS, HSIZE), rows),
        pl.BlockSpec((KEYS, HSIZE), rows),
        pl.BlockSpec((HSIZE, KEYS), lambda *_: (0, part)),
    ]
    args = [pos, q, do, st, k, v, kt]
    if not first:
        specs.append(pl.BlockSpec((HSIZE, 2 * CHUNK), full))
        args.append(dqt)
    scores = KEYS * 2 * CHUNK
    return pl.pallas_call(
        functools.partial(attn_kernel, first, part),
        out_shape=(sds((KEYS // ROWS, ROWS, 128)), sds((HSIZE, 2 * CHUNK), F32)),
        grid_spec=pltpu.PrefetchScalarGridSpec(
            num_scalar_prefetch=1,
            grid=(1,),
            in_specs=specs,
            out_specs=[
                pl.BlockSpec((KEYS // ROWS, ROWS, 128), lambda *_: (0, 0, 0)),
                pl.BlockSpec((HSIZE, 2 * CHUNK), full),
            ],
        ),
        input_output_aliases={} if first else {7: 1},
        compiler_params=pltpu.CompilerParams(vmem_limit_bytes=VMEM_LIMIT),
        cost_estimate=pl.CostEstimate(
            flops=10 * scores * 256, transcendentals=scores, bytes_accessed=4 << 20
        ),
    )(*args)


def turn_queries(dqt_ref, own_ref, core_ref, dq):
    for b in range(6):
        dq[b * 512 : b * 512 + 512, :] = dqt_ref[:, b * 512 : b * 512 + 512].T
    for c, ref in enumerate((own_ref, core_ref)):
        for z in range(8):
            blk = c * 8 + z
            ref[z, :, 0:HSIZE] = dq[blk * 128 : blk * 128 + 96, :].astype(BF)
            ref[z, 0:32, HSIZE:128] = dq[blk * 128 + 96 : blk * 128 + 128, :].astype(BF)
            ref[z, 32:96, HSIZE:128] = dq[2048 + blk * 64 : 2048 + blk * 64 + 64, :].astype(BF)


def unpack_final(x_ref, q_ref, k_ref, v_ref):
    for h in range(HEADS):
        cols = slice(h * HSIZE, (h + 1) * HSIZE)
        k_ref[0, :, cols] = x_ref[h, 0:ROWS, 0:HSIZE]
        v_ref[0, :, cols] = x_ref[h, 0:ROWS, HSIZE:128]
        q_ref[0, 0:HALF, cols] = x_ref[h, ROWS : ROWS + HALF, 0:HSIZE]
        q_ref[0, HALF:ROWS, cols] = x_ref[h, ROWS : ROWS + HALF, HSIZE:128]


def finish_sums(scale_ref, x_ref, proj_ref, taps_ref):
    scale = scale_ref[0]
    for c in range(8):
        cols = slice(c * 128, c * 128 + 128)
        proj_ref[:, cols] = x_ref[c, 0:512, :].astype(F32) * scale
        taps_ref[:, cols] = x_ref[c, 512:543, :].astype(F32) * scale


ROUNDS = (("core", 0), ("dp", 0), ("dp", 1), ("dp", 2), ("xh", 0), ("z", 0), ("z", 1), ("z", 2))


def partner(axis, bit):
    size = lax.axis_size(axis)
    return [(i, i ^ (1 << bit)) for i in range(size)]


def reduce_round(x, axis, bit):
    b = (lax.axis_index(axis) >> bit) & 1
    halves = x.reshape(2, x.shape[0] // 2, 128)
    send = lax.dynamic_index_in_dim(halves, 1 - b, 0, keepdims=False)
    keep = lax.dynamic_index_in_dim(halves, b, 0, keepdims=False)
    got = lax.ppermute(send, axis, partner(axis, bit))
    return (keep.astype(F32) + got.astype(F32)).astype(BF)


def gather_round(x, axis, bit):
    b = ((lax.axis_index(axis) >> bit) & 1) == 1
    got = lax.ppermute(x, axis, partner(axis, bit))
    return jnp.concatenate([jnp.where(b, got, x), jnp.where(b, x, got)], axis=0)


def swap(x, axis):
    return lax.ppermute(x, axis, [(0, 1), (1, 0)])


def shards(query, key, value, attn, log, lengths, x, g, proj, taps):
    xh, z, core = (lax.axis_index(a) for a in SEQ)
    index = (xh * 8 + z) * 2 + core
    length = lax.dynamic_index_in_dim(lengths, lax.axis_index("dp"), 0, keepdims=False)
    up = [(i, i + 1) for i in range(31)]
    down = [(i + 1, i) for i in range(31)]
    last = jnp.concatenate([x[0, 160:192], g[0, 176:192]], axis=0)
    first = jnp.concatenate([x[0, 0:32], g[0, 0:16]], axis=0)
    lo = lax.ppermute(last, SEQ, up)
    hi = lax.ppermute(first, SEQ, down)

    packed = call(pack_early, sds((HEADS, ROWS + HALF, 128)))(query, key, value)
    early = lax.all_to_all(packed, "z", 0, 0, tiled=True)
    qc = swap(early[:, ROWS:], "core")
    kvx = swap(early[:, :ROWS], "xh")
    own_row = (xh * 16 + core) * ROWS
    other_row = ((1 - xh) * 16 + core) * ROWS
    pos = jnp.stack([length, other_row, own_row]).astype(jnp.int32)
    smem = pl.BlockSpec(memory_space=pltpu.SMEM)
    vmem = pl.BlockSpec(memory_space=pltpu.VMEM)
    q, k, v, kt = call(
        prep_early,
        (sds((2 * CHUNK, HSIZE)),) * 3 + (sds((HSIZE, 2 * CHUNK)),),
        in_specs=[smem, vmem, vmem, vmem],
        scratch_shapes=[pltpu.VMEM((2 * CHUNK, 128), F32)],
    )(pos, early, qc, kvx)

    conv_pos = jnp.stack([index * ROWS, length]).astype(jnp.int32)
    grad_state, sums, late = conv_call(conv_pos, x, g, lo, hi, taps, proj, attn, log)
    late = lax.all_to_all(late, "z", 0, 0, tiled=True)
    late_core = swap(late, "core")
    do, st = call(prep_late, (sds((2 * CHUNK, HSIZE)), sds((8, 2 * CHUNK), F32)))(late, late_core)

    dqt = None
    dkv = []
    for part in range(CALLS):
        piece, dqt = attn_call(part, pos, q, do, st, k, v, kt, dqt)
        dkv.append(piece)
    dkv_other = swap(jnp.concatenate(dkv[: CALLS // 2], axis=0), "xh")
    dkv_own = jnp.concatenate(dkv[CALLS // 2 :], axis=0)
    dq_own, dq_core = call(
        turn_queries,
        (sds((8, HALF, 128)),) * 2,
        scratch_shapes=[pltpu.VMEM((2 * CHUNK, HSIZE), F32)],
    )(dqt)
    dq_core = swap(dq_core, "core")
    dkv_sum = (dkv_own.astype(F32) + dkv_other.astype(F32)).astype(BF)
    dq_sum = (dq_own.astype(F32) + dq_core.astype(F32)).astype(BF)
    back = lax.all_to_all(jnp.concatenate([dkv_sum, dq_sum], axis=1), "z", 0, 0, tiled=True)
    grad_q, grad_k, grad_v = call(unpack_final, (sds((1, ROWS, 512)),) * 3)(back)

    sums = sums.reshape(8 * 544, 128)
    for axis, bit in ROUNDS:
        sums = reduce_round(sums, axis, bit)
    for axis, bit in reversed(ROUNDS):
        sums = gather_round(sums, axis, bit)
    scale = 1.0 / jnp.sqrt(jnp.sum(lengths).astype(F32))
    grad_proj, grad_taps = call(
        finish_sums,
        (sds((512, 1024), F32), sds((TAPS, 1024), F32)),
        in_specs=[smem, vmem],
    )(scale.reshape(1), sums.reshape(8, 544, 128))
    return grad_q, grad_k, grad_v, grad_state, grad_proj, grad_taps


def solution(mesh):
    inner = Mesh(mesh.devices.reshape(8, 2, 8, 2), ALL)
    rows = P("dp", SEQ, None)
    in_specs = (rows,) * 5 + (P(), rows, rows, P(), P())
    out_specs = (rows,) * 4 + (P(), P())
    return jax.shard_map(
        shards, mesh=inner, in_specs=in_specs, out_specs=out_specs, check_vma=False
    )
```

time: 719 us -> 225 us (0.31); the launches traced: 708 us -> 224 us
  local copies, waits for them, and re-layouts: 158 us -> 9.92 us
  waiting for transfers between devices: 191 us -> 55 us
  matrix products: 97.2 us -> 0 us
  blocking collectives: 92.8 us -> 0 us
  Pallas kernels: 0 us -> 81.1 us
  other arithmetic: 77.4 us -> 6.26 us
  loops' own time: 61.6 us -> 0 us
  starting transfers between devices: 13.4 us -> 70 us
  between operations: 16.7 us -> 1.79 us
    psum x1 -> x0, waiting for transfers between devices: 188 us -> none  [shards(): proj_sum, kernel_sum = lax.psum((proj_part, kernel_grad), ('dp', 'seq'))]
    dot_general x7 -> x0, matrix products: 97.2 us -> none  [the longest x2 33.8 us: score_parts(): jnp.einsum('thd,uhd->htu', query_heads, key_heads, preferred_element_type...]
    all_gather x2 -> x0, blocking collectives: 92.8 us -> none  [the longest x1 55.6 us: shards(): log_piece = lax.all_gather(log_half, 'seq', axis=0, tiled=True)]
    pallas_call x0 -> x15, Pallas kernels: none -> 81.1 us  [the longest x8 54.2 us: attn_call(): pl.pallas_call(functools.partial(attn_kernel, first, part), out_shape=(sd...]
    dynamic_slice x94 -> x1, local copies, waits for them, and re-layouts: 67.1 us -> 1.24 us  [shards(): lax.dynamic_index_in_dim(lengths, lax.axis_index('dp'), 0, keepdims=False)]
    another operation x3 -> x0, loops' own time: 61.6 us -> none  [the longest x1 60.3 us: taps_product(): return lax.map(one_tap, jnp.arange(tap_count, dtype=jnp.int32))]
    dynamic_update_slice x31 -> x0, local copies, waits for them, and re-layouts: 43.3 us -> none  [taps_product(): return lax.map(one_tap, jnp.arange(tap_count, dtype=jnp.int32))]
    ppermute x4 -> x23, starting transfers between devices: 13.2 us -> 55.7 us  [the longest x8 19.2 us: reduce_round(): got = lax.ppermute(send, axis, partner(axis, bit))]
  transfers between devices with their start and end apart: 9 -> 26, of which waited for: 2 -> 13; matrix products, arithmetic and copies ran while one was open for 29% -> 4% of each run, Pallas kernels for 0% -> 30%
where the time goes in v1:
time: 225 us; the launch traced here: 224 us
  Pallas kernels  81.1 us (36%)
  starting transfers between devices  70 us (31%)
  waiting for transfers between devices  55 us (24%)
  local copies, waits for them, and re-layouts  9.92 us (4%)
  other arithmetic  6.26 us (3%)
    pallas_call x8, Pallas kernels, attn_call(): pl.pallas_call(functools.partial(attn_kernel, first, part), out_shape=(sd...  54.2 us
    ppermute x8, waiting for transfers between devices, reduce_round(): got = lax.ppermute(send, axis, partner(axis, bit))  21.3 us
    ppermute x8, starting transfers between devices, reduce_round(): got = lax.ppermute(send, axis, partner(axis, bit))  19.2 us
    ppermute x5, starting transfers between devices, swap(): return lax.ppermute(x, axis, [(0, 1), (1, 0)])  17.9 us
    all_to_all x1, waiting for transfers between devices, shards(): lax.all_to_all(jnp.concatenate([dkv_sum, dq_sum], axis=1), 'z', 0, 0, til...  15.1 us
    ppermute x8, starting transfers between devices, gather_round(): got = lax.ppermute(x, axis, partner(axis, bit))  11.9 us
    pallas_call x1, Pallas kernels, conv_call(): pl.pallas_call(conv_kernel, out_shape=(sds((1, ROWS, 1024)), sds((8, 544,...  11.5 us
    ppermute x5, waiting for transfers between devices, swap(): return lax.ppermute(x, axis, [(0, 1), (1, 0)])  9.89 us
  transfers between devices with their start and end apart: 26, of which 13 were waited for; matrix products, arithmetic and copies ran while one was open for 4% of the time, Pallas kernels for 30%

profile of v1, /device:TPU:1, one launch (start us, length us, event | category | flops | bytes accessed | tf_op | source)
XLA Modules:
  0.0 224.2 jit_solution(15492358694904270482)
XLA Ops:
  2.3 4.9 %collective-permute-start.2 = (bf16[48,1024]{1,0:T(8,128)(2,1)S(1)}, bf16[48,1024]{1,0:T(8,128)(2,1)S(1)}, u32[]{:S(2)}, u32[]{:S(2)}) collective-permute-start(bf16[48,1024]{1,0:T(8,128)(2,1)S(1)} %pad_maximum_fusion.6), channel_id=1, source_target_pairs={{0,1},{1,2},{2,3},{3,4},{4,5},{5,6},{6,7},{7,8},{8,9},{9,10},{10,1... | collective-permute-start | bytes 294920 | tf_op jit(solution)/shard_map/ppermute | solution.py:373
  14.4 11.5 %shard_map.147 = (bf16[1,192,1024]{2,1,0:T(8,128)(2,1)}, bf16[8,544,128]{2,1,0:T(8,128)(2,1)}, bf16[8,112,128]{2,1,0:T(8,128)(2,1)}) custom-call(s32[2]{0:T(128)} %pad_add_fusion.1.pos_ref, bf16[1,192,1024]{2,1,0:T(8,128)(2,1)} %x_ref.1, bf16[1,192,1024]{2,1,0:T(8,128)(2,1)} %g_ref.1, bf16[48,1024]{1,0:T(8,128)(2,1)} %copy-done.16, ...), custom_call_target="tpu_custom_call" | custom-call | tf_op jit(solution)/shard_map/pallas_call | solution.py:147
  30.7 6.9 %collective-permute-done.8 = bf16[1088,128]{1,0:T(8,128)(2,1)S(1)} collective-permute-done((bf16[1088,128]{1,0:T(8,128)(2,1)S(1)}, bf16[1088,128]{1,0:T(8,128)(2,1)S(1)}, u32[]{:S(2)}, u32[]{:S(2)}) %collective-permute-start.8) | collective-permute-done | bytes 278560 | tf_op jit(solution)/shard_map/ppermute | solution.py:351
  42.1 3.0 %collective-permute-start.10 = (bf16[272,128]{1,0:T(8,128)(2,1)S(1)}, bf16[272,128]{1,0:T(8,128)(2,1)S(1)}, u32[]{:S(2)}, u32[]{:S(2)}) collective-permute-start(bf16[272,128]{1,0:T(8,128)(2,1)S(1)} %dynamic-slice_bitcast_fusion.3), channel_id=1, source_target_pairs={{0,128},{32,160},{64,192},{96,224},{128,0},{160,32},{192,64},{224,... | collective-permute-start | bytes 208904 | tf_op jit(solution)/shard_map/ppermute | solution.py:351
  46.9 6.6 %collective-permute-start.11 = (bf16[136,128]{1,0:T(8,128)(2,1)S(1)}, bf16[136,128]{1,0:T(8,128)(2,1)S(1)}, u32[]{:S(2)}, u32[]{:S(2)}) collective-permute-start(bf16[136,128]{1,0:T(8,128)(2,1)S(1)} %dynamic-slice_bitcast_fusion.4), channel_id=1, source_target_pairs={{0,16},{16,0},{1,17},{17,1},{2,18},{18,2},{3,19},{19,3},{4,20},{20... | collective-permute-start | bytes 104456 | tf_op jit(solution)/shard_map/ppermute | solution.py:351
  59.2 5.2 %all-to-all-start.1 = ((bf16[8,112,128]{2,1,0:T(8,128)(2,1)}), bf16[8,112,128]{2,1,0:T(8,128)(2,1)S(1)}, u32[]{:S(2)}, u32[]{:S(2)}) async-start(bf16[8,112,128]{2,1,0:T(8,128)(2,1)} %get-tuple-element.39), calls=%async_computation.1 | async-start | bytes 458752 | tf_op jit(solution)/shard_map/all_to_all | solution.py:394
  64.4 5.4 %collective-permute-start.14 = (bf16[17,128]{1,0:T(8,128)(2,1)S(1)}, bf16[17,128]{1,0:T(8,128)(2,1)S(1)}, u32[]{:S(2)}, u32[]{:S(2)}) collective-permute-start(bf16[17,128]{1,0:T(8,128)(2,1)S(1)} %dynamic-slice_bitcast_fusion.7), channel_id=1, source_target_pairs={{0,8},{2,10},{4,12},{6,14},{8,0},{10,2},{12,4},{14,6},{1,9},{3,11}... | collective-permute-start | bytes 13064 | tf_op jit(solution)/shard_map/ppermute | solution.py:351
  69.8 3.5 %collective-permute-done.14 = bf16[17,128]{1,0:T(8,128)(2,1)S(1)} collective-permute-done((bf16[17,128]{1,0:T(8,128)(2,1)S(1)}, bf16[17,128]{1,0:T(8,128)(2,1)S(1)}, u32[]{:S(2)}, u32[]{:S(2)}) %collective-permute-start.14) | collective-permute-done | bytes 4384 | tf_op jit(solution)/shard_map/ppermute | solution.py:351
  78.6 3.8 %all-to-all-start = ((bf16[8,288,128]{2,1,0:T(8,128)(2,1)}), bf16[8,288,128]{2,1,0:T(8,128)(2,1)S(1)}, u32[]{:S(2)}, u32[]{:S(2)}) async-start(bf16[8,288,128]{2,1,0:T(8,128)(2,1)} %shard_map.145), calls=%async_computation | async-start | bytes 1179648 | tf_op jit(solution)/shard_map/all_to_all | solution.py:377
  84.8 6.1 %collective-permute-done.16 = bf16[34,128]{1,0:T(8,128)(2,1)S(1)} collective-permute-done((bf16[34,128]{1,0:T(8,128)(2,1)S(1)}, bf16[34,128]{1,0:T(8,128)(2,1)S(1)}, u32[]{:S(2)}, u32[]{:S(2)}) %collective-permute-start.16) | collective-permute-done | bytes 8736 | tf_op jit(solution)/shard_map/ppermute | solution.py:357
  95.0 11.6 %collective-permute-start.4 = (bf16[8,112,128]{2,1,0:T(8,128)(2,1)S(1)}, bf16[8,112,128]{2,1,0:T(8,128)(2,1)S(1)}, u32[]{:S(2)}, u32[]{:S(2)}) collective-permute-start(bf16[8,112,128]{2,1,0:T(8,128)(2,1)S(1)} %all-to-all-done.1.own_ref), channel_id=1, source_target_pairs={{0,1},{1,0},{2,3},{3,2},{4,5},{5,4},{6,7},{7,6},{8,9},{9,8},{10,11... | collective-permute-start | bytes 688136 | tf_op jit(solution)/shard_map/ppermute | solution.py:362
  107.8 3.1 %collective-permute-start.19 = (bf16[272,128]{1,0:T(8,128)(2,1)S(1)}, bf16[272,128]{1,0:T(8,128)(2,1)S(1)}, u32[]{:S(2)}, u32[]{:S(2)}) collective-permute-start(bf16[272,128]{1,0:T(8,128)(2,1)S(1)} %pad_maximum_fusion.8), channel_id=1, source_target_pairs={{0,128},{32,160},{64,192},{96,224},{128,0},{160,32},{192,64},{224,... | collective-permute-start | bytes 208904 | tf_op jit(solution)/shard_map/ppermute | solution.py:357
  121.2 3.1 %shard_map.146 = (bf16[3072,64]{1,0:T(8,128)(2,1)}, bf16[3072,64]{1,0:T(8,128)(2,1)}, bf16[3072,64]{1,0:T(8,128)(2,1)}, bf16[64,3072]{1,0:T(8,128)(2,1)}) custom-call(s32[3]{0:T(128)} %pad_add_fusion.pos_ref, bf16[8,288,128]{2,1,0:T(8,128)(2,1)} %copy-done, bf16[8,96,128]{2,1,0:T(8,128)(2,1)} %copy-done.7, bf16[8,192,128]{2,1,0:T(8,128)(2,1)} %copy-done.4), custom_call_target="tpu_custom_call" | custom-call | tf_op jit(solution)/shard_map/pallas_call | solution.py:385
  124.3 6.5 %shard_map.149 = (bf16[2,192,128]{2,1,0:T(8,128)(2,1)}, f32[64,3072]{1,0:T(8,128)}) custom-call(s32[3]{0:T(128)} %pad_add_fusion.pos_ref, bf16[3072,64]{1,0:T(8,128)(2,1)} %get-tuple-element.38.q, bf16[3072,64]{1,0:T(8,128)(2,1)} %get-tuple-element.40.do, f32[8,3072]{1,0:T(8,128)} %get-tuple-element.41.st, bf16[3072,64]{1,0:T(8,128)(2,1)} %get-tuple-element.42.k, ...), custom_call_target="tpu_custom_call" | custom-call | flops 3019898880 | bytes 4194304 | tf_op jit(solution)/shard_map/pallas_call | solution.py:290
  130.8 6.8 %shard_map.150 = (bf16[2,192,128]{2,1,0:T(8,128)(2,1)}, f32[64,3072]{1,0:T(8,128)}) custom-call(s32[3]{0:T(128)} %pad_add_fusion.pos_ref, bf16[3072,64]{1,0:T(8,128)(2,1)} %get-tuple-element.38.q, bf16[3072,64]{1,0:T(8,128)(2,1)} %get-tuple-element.40.do, f32[8,3072]{1,0:T(8,128)} %get-tuple-element.41.st, ...), custom_call_target="tpu_custom_call", output_to_operand_aliasing={{1}: (7, {})} | custom-call | flops 3019898880 | bytes 4194304 | tf_op jit(solution)/shard_map/pallas_call | solution.py:290
  137.6 6.8 %shard_map.151 = (bf16[2,192,128]{2,1,0:T(8,128)(2,1)}, f32[64,3072]{1,0:T(8,128)}) custom-call(s32[3]{0:T(128)} %pad_add_fusion.pos_ref, bf16[3072,64]{1,0:T(8,128)(2,1)} %get-tuple-element.38.q, bf16[3072,64]{1,0:T(8,128)(2,1)} %get-tuple-element.40.do, f32[8,3072]{1,0:T(8,128)} %get-tuple-element.41.st, ...), custom_call_target="tpu_custom_call", output_to_operand_aliasing={{1}: (7, {})} | custom-call | flops 3019898880 | bytes 4194304 | tf_op jit(solution)/shard_map/pallas_call | solution.py:290
  144.4 6.8 %shard_map.152 = (bf16[2,192,128]{2,1,0:T(8,128)(2,1)}, f32[64,3072]{1,0:T(8,128)}) custom-call(s32[3]{0:T(128)} %pad_add_fusion.pos_ref, bf16[3072,64]{1,0:T(8,128)(2,1)} %get-tuple-element.38.q, bf16[3072,64]{1,0:T(8,128)(2,1)} %get-tuple-element.40.do, f32[8,3072]{1,0:T(8,128)} %get-tuple-element.41.st, ...), custom_call_target="tpu_custom_call", output_to_operand_aliasing={{1}: (7, {})} | custom-call | flops 3019898880 | bytes 4194304 | tf_op jit(solution)/shard_map/pallas_call | solution.py:290
  151.2 6.8 %shard_map.153 = (bf16[2,192,128]{2,1,0:T(8,128)(2,1)}, f32[64,3072]{1,0:T(8,128)}) custom-call(s32[3]{0:T(128)} %pad_add_fusion.pos_ref, bf16[3072,64]{1,0:T(8,128)(2,1)} %get-tuple-element.38.q, bf16[3072,64]{1,0:T(8,128)(2,1)} %get-tuple-element.40.do, f32[8,3072]{1,0:T(8,128)} %get-tuple-element.41.st, ...), custom_call_target="tpu_custom_call", output_to_operand_aliasing={{1}: (7, {})} | custom-call | flops 3019898880 | bytes 4194304 | tf_op jit(solution)/shard_map/pallas_call | solution.py:290
  158.0 6.8 %shard_map.154 = (bf16[2,192,128]{2,1,0:T(8,128)(2,1)}, f32[64,3072]{1,0:T(8,128)}) custom-call(s32[3]{0:T(128)} %pad_add_fusion.pos_ref, bf16[3072,64]{1,0:T(8,128)(2,1)} %get-tuple-element.38.q, bf16[3072,64]{1,0:T(8,128)(2,1)} %get-tuple-element.40.do, f32[8,3072]{1,0:T(8,128)} %get-tuple-element.41.st, ...), custom_call_target="tpu_custom_call", output_to_operand_aliasing={{1}: (7, {})} | custom-call | flops 3019898880 | bytes 4194304 | tf_op jit(solution)/shard_map/pallas_call | solution.py:290
  164.8 6.8 %shard_map.155 = (bf16[2,192,128]{2,1,0:T(8,128)(2,1)}, f32[64,3072]{1,0:T(8,128)}) custom-call(s32[3]{0:T(128)} %pad_add_fusion.pos_ref, bf16[3072,64]{1,0:T(8,128)(2,1)} %get-tuple-element.38.q, bf16[3072,64]{1,0:T(8,128)(2,1)} %get-tuple-element.40.do, f32[8,3072]{1,0:T(8,128)} %get-tuple-element.41.st, ...), custom_call_target="tpu_custom_call", output_to_operand_aliasing={{1}: (7, {})} | custom-call | flops 3019898880 | bytes 4194304 | tf_op jit(solution)/shard_map/pallas_call | solution.py:290
  172.8 6.9 %shard_map.156 = (bf16[2,192,128]{2,1,0:T(8,128)(2,1)}, f32[64,3072]{1,0:T(8,128)}) custom-call(s32[3]{0:T(128)} %pad_add_fusion.pos_ref, bf16[3072,64]{1,0:T(8,128)(2,1)} %get-tuple-element.38.q, bf16[3072,64]{1,0:T(8,128)(2,1)} %get-tuple-element.40.do, f32[8,3072]{1,0:T(8,128)} %get-tuple-element.41.st, ...), custom_call_target="tpu_custom_call", output_to_operand_aliasing={{1}: (7, {})} | custom-call | flops 3019898880 | bytes 4194304 | tf_op jit(solution)/shard_map/pallas_call | solution.py:290
  186.0 9.4 %collective-permute-done.5 = bf16[8,192,128]{2,1,0:T(8,128)(2,1)S(1)} collective-permute-done((bf16[8,192,128]{2,1,0:T(8,128)(2,1)S(1)}, bf16[8,192,128]{2,1,0:T(8,128)(2,1)S(1)}, u32[]{:S(2)}, u32[]{:S(2)}) %collective-permute-start.5) | collective-permute-done | bytes 393248 | tf_op jit(solution)/shard_map/ppermute | solution.py:362
  196.4 5.3 %all-to-all-start.2 = ((bf16[8,288,128]{2,1,0:T(8,128)(2,1)}), bf16[8,288,128]{2,1,0:T(8,128)(2,1)S(1)}, u32[]{:S(2)}, u32[]{:S(2)}) async-start(bf16[8,288,128]{2,1,0:T(8,128)(2,1)} %pad_maximum_fusion.1), calls=%async_computation.2 | async-start | bytes 1179648 | tf_op jit(solution)/shard_map/all_to_all | solution.py:413
  206.0 15.1 %all-to-all-done.2.x_ref = bf16[8,288,128]{2,1,0:T(8,128)(2,1)S(1)} async-done(((bf16[8,288,128]{2,1,0:T(8,128)(2,1)}), bf16[8,288,128]{2,1,0:T(8,128)(2,1)S(1)}, u32[]{:S(2)}, u32[]{:S(2)}) %all-to-all-start.2) | async-done | bytes 589856 | tf_op jit(solution)/shard_map/all_to_all | solution.py:413
  (131 shorter events, 63.5 us)
Async XLA Ops:
  2.3 10.8 %collective-permute-start.2 = (bf16[48,1024]{1,0:T(8,128)(2,1)S(1)}, bf16[48,1024]{1,0:T(8,128)(2,1)S(1)}, u32[]{:S(2)}, u32[]{:S(2)}) collective-permute-start(bf16[48,1024]{1,0:T(8,128)(2,1)S(1)} %pad_maximum_fusion.6), channel_id=1, source_target_pairs={{0,1},{1,2},{2,3},{3,4},{4,5},{5,6},{6,7},{7,8},{8,9},{9,10},{10,1... | collective-permute-start | bytes 294920 | tf_op jit(solution)/shard_map/ppermute | solution.py:373
  7.3 5.9 %collective-permute-start.3 = (bf16[48,1024]{1,0:T(8,128)(2,1)S(1)}, bf16[48,1024]{1,0:T(8,128)(2,1)S(1)}, u32[]{:S(2)}, u32[]{:S(2)}) collective-permute-start(bf16[48,1024]{1,0:T(8,128)(2,1)S(1)} %pad_maximum_fusion.7), channel_id=1, source_target_pairs={{1,0},{2,1},{3,2},{4,3},{5,4},{6,5},{7,6},{8,7},{9,8},{10,9},{11,1... | collective-permute-start | bytes 294920 | tf_op jit(solution)/shard_map/ppermute | solution.py:374
  29.4 8.2 %collective-permute-start.8 = (bf16[1088,128]{1,0:T(8,128)(2,1)S(1)}, bf16[1088,128]{1,0:T(8,128)(2,1)S(1)}, u32[]{:S(2)}, u32[]{:S(2)}) collective-permute-start(bf16[1088,128]{1,0:T(8,128)(2,1)S(1)} %dynamic-slice_bitcast_fusion.1), channel_id=1, source_target_pairs={{0,32},{32,0},{64,96},{96,64},{128,160},{160,128},{192,224},{224,1... | collective-permute-start | bytes 835592 | tf_op jit(solution)/shard_map/ppermute | solution.py:351
  37.7 4.3 %collective-permute-start.9 = (bf16[544,128]{1,0:T(8,128)(2,1)S(1)}, bf16[544,128]{1,0:T(8,128)(2,1)S(1)}, u32[]{:S(2)}, u32[]{:S(2)}) collective-permute-start(bf16[544,128]{1,0:T(8,128)(2,1)S(1)} %dynamic-slice_bitcast_fusion.2), channel_id=1, source_target_pairs={{0,64},{32,96},{64,0},{96,32},{128,192},{160,224},{192,128},{224,1... | collective-permute-start | bytes 417800 | tf_op jit(solution)/shard_map/ppermute | solution.py:351
  42.1 4.8 %collective-permute-start.10 = (bf16[272,128]{1,0:T(8,128)(2,1)S(1)}, bf16[272,128]{1,0:T(8,128)(2,1)S(1)}, u32[]{:S(2)}, u32[]{:S(2)}) collective-permute-start(bf16[272,128]{1,0:T(8,128)(2,1)S(1)} %dynamic-slice_bitcast_fusion.3), channel_id=1, source_target_pairs={{0,128},{32,160},{64,192},{96,224},{128,0},{160,32},{192,64},{224,... | collective-permute-start | bytes 208904 | tf_op jit(solution)/shard_map/ppermute | solution.py:351
  46.9 7.9 %collective-permute-start.11 = (bf16[136,128]{1,0:T(8,128)(2,1)S(1)}, bf16[136,128]{1,0:T(8,128)(2,1)S(1)}, u32[]{:S(2)}, u32[]{:S(2)}) collective-permute-start(bf16[136,128]{1,0:T(8,128)(2,1)S(1)} %dynamic-slice_bitcast_fusion.4), channel_id=1, source_target_pairs={{0,16},{16,0},{1,17},{17,1},{2,18},{18,2},{3,19},{19,3},{4,20},{20... | collective-permute-start | bytes 104456 | tf_op jit(solution)/shard_map/ppermute | solution.py:351
  57.9 6.4 %collective-permute-start.13 = (bf16[34,128]{1,0:T(8,128)(2,1)S(1)}, bf16[34,128]{1,0:T(8,128)(2,1)S(1)}, u32[]{:S(2)}, u32[]{:S(2)}) collective-permute-start(bf16[34,128]{1,0:T(8,128)(2,1)S(1)} %dynamic-slice_bitcast_fusion.6), channel_id=1, source_target_pairs={{0,4},{2,6},{4,0},{6,2},{8,12},{10,14},{12,8},{14,10},{1,5},{3,7},... | collective-permute-start | bytes 26120 | tf_op jit(solution)/shard_map/ppermute | solution.py:351
  59.2 19.4 %all-to-all-start.1 = ((bf16[8,112,128]{2,1,0:T(8,128)(2,1)}), bf16[8,112,128]{2,1,0:T(8,128)(2,1)S(1)}, u32[]{:S(2)}, u32[]{:S(2)}) async-start(bf16[8,112,128]{2,1,0:T(8,128)(2,1)} %get-tuple-element.39), calls=%async_computation.1 | async-start | bytes 458752 | tf_op jit(solution)/shard_map/all_to_all | solution.py:394
  64.4 9.0 %collective-permute-start.14 = (bf16[17,128]{1,0:T(8,128)(2,1)S(1)}, bf16[17,128]{1,0:T(8,128)(2,1)S(1)}, u32[]{:S(2)}, u32[]{:S(2)}) collective-permute-start(bf16[17,128]{1,0:T(8,128)(2,1)S(1)} %dynamic-slice_bitcast_fusion.7), channel_id=1, source_target_pairs={{0,8},{2,10},{4,12},{6,14},{8,0},{10,2},{12,4},{14,6},{1,9},{3,11}... | collective-permute-start | bytes 13064 | tf_op jit(solution)/shard_map/ppermute | solution.py:351
  73.4 9.0 %collective-permute-start.15 = (bf16[17,128]{1,0:T(8,128)(2,1)S(1)}, bf16[17,128]{1,0:T(8,128)(2,1)S(1)}, u32[]{:S(2)}, u32[]{:S(2)}) collective-permute-start(bf16[17,128]{1,0:T(8,128)(2,1)S(1)} %fusion.7), channel_id=1, source_target_pairs={{0,8},{2,10},{4,12},{6,14},{8,0},{10,2},{12,4},{14,6},{1,9},{3,11}... | collective-permute-start | bytes 13064 | tf_op jit(solution)/shard_map/ppermute | solution.py:357
  78.6 28.1 %all-to-all-start = ((bf16[8,288,128]{2,1,0:T(8,128)(2,1)}), bf16[8,288,128]{2,1,0:T(8,128)(2,1)S(1)}, u32[]{:S(2)}, u32[]{:S(2)}) async-start(bf16[8,288,128]{2,1,0:T(8,128)(2,1)} %shard_map.145), calls=%async_computation | async-start | bytes 1179648 | tf_op jit(solution)/shard_map/all_to_all | solution.py:377
  82.4 8.5 %collective-permute-start.16 = (bf16[34,128]{1,0:T(8,128)(2,1)S(1)}, bf16[34,128]{1,0:T(8,128)(2,1)S(1)}, u32[]{:S(2)}, u32[]{:S(2)}) collective-permute-start(bf16[34,128]{1,0:T(8,128)(2,1)S(1)} %pad_maximum_fusion.11), channel_id=1, source_target_pairs={{0,4},{2,6},{4,0},{6,2},{8,12},{10,14},{12,8},{14,10},{1,5},{3,7},... | collective-permute-start | bytes 26120 | tf_op jit(solution)/shard_map/ppermute | solution.py:357
  90.9 3.0 %collective-permute-start.17 = (bf16[68,128]{1,0:T(8,128)(2,1)S(1)}, bf16[68,128]{1,0:T(8,128)(2,1)S(1)}, u32[]{:S(2)}, u32[]{:S(2)}) collective-permute-start(bf16[68,128]{1,0:T(8,128)(2,1)S(1)} %pad_maximum_fusion.10), channel_id=1, source_target_pairs={{0,2},{2,0},{4,6},{6,4},{8,10},{10,8},{12,14},{14,12},{1,3},{3,1},... | collective-permute-start | bytes 52232 | tf_op jit(solution)/shard_map/ppermute | solution.py:357
  94.0 13.8 %collective-permute-start.18 = (bf16[136,128]{1,0:T(8,128)(2,1)S(1)}, bf16[136,128]{1,0:T(8,128)(2,1)S(1)}, u32[]{:S(2)}, u32[]{:S(2)}) collective-permute-start(bf16[136,128]{1,0:T(8,128)(2,1)S(1)} %pad_maximum_fusion.9), channel_id=1, source_target_pairs={{0,16},{16,0},{1,17},{17,1},{2,18},{18,2},{3,19},{19,3},{4,20},{20... | collective-permute-start | bytes 104456 | tf_op jit(solution)/shard_map/ppermute | solution.py:357
  95.0 18.4 %collective-permute-start.4 = (bf16[8,112,128]{2,1,0:T(8,128)(2,1)S(1)}, bf16[8,112,128]{2,1,0:T(8,128)(2,1)S(1)}, u32[]{:S(2)}, u32[]{:S(2)}) collective-permute-start(bf16[8,112,128]{2,1,0:T(8,128)(2,1)S(1)} %all-to-all-done.1.own_ref), channel_id=1, source_target_pairs={{0,1},{1,0},{2,3},{3,2},{4,5},{5,4},{6,7},{7,6},{8,9},{9,8},{10,11... | collective-permute-start | bytes 688136 | tf_op jit(solution)/shard_map/ppermute | solution.py:362
  106.7 13.0 %collective-permute-start.1 = (bf16[8,192,128]{2,1,0:T(8,128)(2,1)S(1)}, bf16[8,192,128]{2,1,0:T(8,128)(2,1)S(1)}, u32[]{:S(2)}, u32[]{:S(2)}) collective-permute-start(bf16[8,192,128]{2,1,0:T(8,128)(2,1)S(1)} %slice.25), channel_id=1, source_target_pairs={{0,16},{16,0},{1,17},{17,1},{2,18},{18,2},{3,19},{19,3},{4,20},{20... | collective-permute-start | bytes 1179656 | tf_op jit(solution)/shard_map/ppermute | solution.py:362
  107.8 10.9 %collective-permute-start.19 = (bf16[272,128]{1,0:T(8,128)(2,1)S(1)}, bf16[272,128]{1,0:T(8,128)(2,1)S(1)}, u32[]{:S(2)}, u32[]{:S(2)}) collective-permute-start(bf16[272,128]{1,0:T(8,128)(2,1)S(1)} %pad_maximum_fusion.8), channel_id=1, source_target_pairs={{0,128},{32,160},{64,192},{96,224},{128,0},{160,32},{192,64},{224,... | collective-permute-start | bytes 208904 | tf_op jit(solution)/shard_map/ppermute | solution.py:357
  116.4 3.3 %collective-permute-start = (bf16[8,96,128]{2,1,0:T(8,128)(2,1)S(1)}, bf16[8,96,128]{2,1,0:T(8,128)(2,1)S(1)}, u32[]{:S(2)}, u32[]{:S(2)}) collective-permute-start(bf16[8,96,128]{2,1,0:T(8,128)(2,1)S(1)} %slice.24), channel_id=1, source_target_pairs={{0,1},{1,0},{2,3},{3,2},{4,5},{5,4},{6,7},{7,6},{8,9},{9,8},{10,11... | collective-permute-start | bytes 589832 | tf_op jit(solution)/shard_map/ppermute | solution.py:362
  118.8 52.9 %collective-permute-start.20 = (bf16[544,128]{1,0:T(8,128)(2,1)S(1)}, bf16[544,128]{1,0:T(8,128)(2,1)S(1)}, u32[]{:S(2)}, u32[]{:S(2)}) collective-permute-start(bf16[544,128]{1,0:T(8,128)(2,1)S(1)} %pad_maximum_fusion.5), channel_id=1, source_target_pairs={{0,64},{32,96},{64,0},{96,32},{128,192},{160,224},{192,128},{224,1... | collective-permute-start | bytes 417800 | tf_op jit(solution)/shard_map/ppermute | solution.py:357
  171.7 13.7 %collective-permute-start.21 = (bf16[1088,128]{1,0:T(8,128)(2,1)S(1)}, bf16[1088,128]{1,0:T(8,128)(2,1)S(1)}, u32[]{:S(2)}, u32[]{:S(2)}) collective-permute-start(bf16[1088,128]{1,0:T(8,128)(2,1)S(1)} %pad_maximum_fusion.4), channel_id=1, source_target_pairs={{0,32},{32,0},{64,96},{96,64},{128,160},{160,128},{192,224},{224,1... | collective-permute-start | bytes 835592 | tf_op jit(solution)/shard_map/ppermute | solution.py:357
  182.3 3.6 %collective-permute-start.6 = (bf16[8,96,128]{2,1,0:T(8,128)(2,1)}, bf16[8,96,128]{2,1,0:T(8,128)(2,1)S(1)}, u32[]{:S(2)}, u32[]{:S(2)}) collective-permute-start(bf16[8,96,128]{2,1,0:T(8,128)(2,1)} %get-tuple-element.62), channel_id=1, source_target_pairs={{0,1},{1,0},{2,3},{3,2},{4,5},{5,4},{6,7},{7,6},{8,9},{9,8},{10,11... | collective-permute-start | bytes 589832 | tf_op jit(solution)/shard_map/ppermute | solution.py:362
  183.1 12.3 %collective-permute-start.5 = (bf16[8,192,128]{2,1,0:T(8,128)(2,1)S(1)}, bf16[8,192,128]{2,1,0:T(8,128)(2,1)S(1)}, u32[]{:S(2)}, u32[]{:S(2)}) collective-permute-start(bf16[8,192,128]{2,1,0:T(8,128)(2,1)S(1)} %pad_maximum_fusion.3), channel_id=1, source_target_pairs={{0,16},{16,0},{1,17},{17,1},{2,18},{18,2},{3,19},{19,3},{4,20},{20... | collective-permute-start | bytes 1179656 | tf_op jit(solution)/shard_map/ppermute | solution.py:362
  185.6 16.2 %collective-permute-start.22 = (bf16[2176,128]{1,0:T(8,128)(2,1)S(1)}, bf16[2176,128]{1,0:T(8,128)(2,1)S(1)}, u32[]{:S(2)}, u32[]{:S(2)}) collective-permute-start(bf16[2176,128]{1,0:T(8,128)(2,1)S(1)} %pad_maximum_fusion.2), channel_id=1, source_target_pairs={{0,1},{1,0},{2,3},{3,2},{4,5},{5,4},{6,7},{7,6},{8,9},{9,8},{10,11... | collective-permute-start | bytes 1671176 | tf_op jit(solution)/shard_map/ppermute | solution.py:357
  196.4 24.7 %all-to-all-start.2 = ((bf16[8,288,128]{2,1,0:T(8,128)(2,1)}), bf16[8,288,128]{2,1,0:T(8,128)(2,1)S(1)}, u32[]{:S(2)}, u32[]{:S(2)}) async-start(bf16[8,288,128]{2,1,0:T(8,128)(2,1)} %pad_maximum_fusion.1), calls=%async_computation.2 | async-start | bytes 1179648 | tf_op jit(solution)/shard_map/all_to_all | solution.py:413
  (21 other events, 169.7 us)

commit v2 on v1

v2 whole, which is shorter than its diff:
```python
import functools

import jax
import jax.numpy as jnp
from jax import lax
from jax.experimental import pallas as pl
from jax.experimental.pallas import tpu as pltpu
from jax.sharding import Mesh, PartitionSpec as P

BF = jnp.bfloat16
F32 = jnp.float32
NT = (((1,), (1,)), ((), ()))
NN = (((1,), (0,)), ((), ()))
TN = (((0,), (0,)), ((), ()))
ROWS = 192
HALF = 96
HEADS = 8
HSIZE = 64
TAPS = 31
FREE = 60
WIDTH = 256
ALL = ("dp", "xh", "z", "core")
SEQ = ("xh", "z", "core")


def cost(micros):
    return pl.CostEstimate(flops=int(micros * 1.15e9), transcendentals=0, bytes_accessed=1 << 20)


def call(kernel, out_shape, micros, vmem, **kw):
    return pl.pallas_call(
        kernel,
        out_shape=out_shape,
        compiler_params=pltpu.CompilerParams(vmem_limit_bytes=vmem << 20),
        cost_estimate=cost(micros),
        **kw,
    )


def record_length(lengths_ref):
    return lengths_ref[lax.axis_index("dp")]


def sds(shape, dtype=BF):
    return jax.ShapeDtypeStruct(shape, dtype)


def pack_early(q_ref, k_ref, v_ref, xl_ref, xf_ref, gl_ref, gf_ref, o_ref, last_ref, first_ref):
    last_ref[0:32, :] = xl_ref[0]
    last_ref[32:48, :] = gl_ref[0]
    first_ref[0:32, :] = xf_ref[0]
    first_ref[32:48, :] = gf_ref[0]
    for h in range(HEADS):
        cols = slice(h * HSIZE, (h + 1) * HSIZE)
        o_ref[h, 0:ROWS, 0:HSIZE] = k_ref[0, :, cols]
        o_ref[h, 0:ROWS, HSIZE:128] = v_ref[0, :, cols]
        q = q_ref[0, :, cols] * BF(0.125)
        o_ref[h, ROWS : ROWS + HALF, 0:HSIZE] = q[:HALF]
        o_ref[h, ROWS : ROWS + HALF, HSIZE:128] = q[HALF:]


def pack_call(query, key, value, x, g):
    full = lambda i: (0, 0, 0)
    rows = pl.BlockSpec((1, ROWS, 512), full)
    rim = lambda n, at: pl.BlockSpec((1, n, 1024), lambda i: (0, at, 0))
    edge = pl.BlockSpec((48, 1024), lambda i: (0, 0))
    return call(
        pack_early,
        (sds((HEADS, ROWS + HALF, 128)), sds((48, 1024)), sds((48, 1024))),
        2,
        FREE,
        grid=(1,),
        in_specs=[rows, rows, rows, rim(32, 5), rim(32, 0), rim(16, 11), rim(16, 0)],
        out_specs=[pl.BlockSpec((HEADS, ROWS + HALF, 128), full), edge, edge],
    )(query, key, value, x, x, g, g)


def conv_kernel(
    lengths_ref,
    x_ref,
    g_ref,
    lo_ref,
    hi_ref,
    w_ref,
    proj_ref,
    attn_ref,
    log_ref,
    gs_ref,
    pk_ref,
    late_ref,
    xs,
    gm,
    gp,
    out_acc,
    attn_t,
    tmp,
):
    step = pl.program_id(0)
    first_row = lax.axis_index(SEQ) * ROWS
    length = record_length(lengths_ref)

    @pl.when(step == 0)
    def _():
        out_acc[...] = jnp.zeros_like(out_acc)
        attn_t[...] = attn_ref[0].T

    def mask(rows, offset):
        at = first_row + offset + lax.broadcasted_iota(jnp.int32, (rows, 128), 0)
        return jnp.where((at >= 0) & (at < length), 1.0, 0.0).astype(F32)

    mask_x = mask(256, -32)
    mask_g = mask(224, -16)
    for half in range(WIDTH // 128):
        cols = slice(half * 128, half * 128 + 128)
        xs[0:32, :] = lo_ref[0:32, cols].astype(F32) * mask_x[0:32]
        xs[32:224, :] = x_ref[0, :, cols].astype(F32) * mask_x[32:224]
        xs[224:256, :] = hi_ref[0:32, cols].astype(F32) * mask_x[224:256]
        gm[0:16, :] = lo_ref[32:48, cols].astype(F32) * mask_g[0:16]
        gm[16:208, :] = g_ref[0, :, cols].astype(F32) * mask_g[16:208]
        gm[208:224, :] = hi_ref[32:48, cols].astype(F32) * mask_g[208:224]
        pre = jnp.zeros((224, 128), F32)
        for j in range(TAPS):
            pre = pre + w_ref[j : j + 1, cols] * xs[1 + j : 225 + j, :]
        s = jax.nn.sigmoid(pre)
        gp[...] = (gm[...] * s * (1.0 + pre * (1.0 - s))).astype(BF).astype(F32)
        back = jnp.zeros((ROWS, 128), F32)
        for j in range(TAPS):
            back = back + w_ref[j : j + 1, cols] * gp[31 - j : 223 - j, :]
        gs = (gm[16:208, :] + mask_g[16:208] * back).astype(BF)
        gs_ref[0, :, cols] = gs
        out_acc[...] += lax.dot_general(
            gs, proj_ref[:, cols], NT, preferred_element_type=F32
        )
        pk_ref[half, 0:512, :] = lax.dot_general(
            attn_t[...], gs, NN, preferred_element_type=F32
        ).astype(BF)
        own = gp[16:208, :]
        rows = [
            jnp.sum(xs[17 + j : 209 + j, :] * own, axis=0, keepdims=True) for j in range(TAPS)
        ]
        rows.append(jnp.zeros((1, 128), F32))
        pk_ref[half, 512:544, :] = jnp.concatenate(rows, axis=0).astype(BF)

    @pl.when(step == pl.num_programs(0) - 1)
    def _():
        grad = out_acc[...].astype(BF)
        tmp[0:ROWS, :] = grad.astype(F32) * attn_ref[0].astype(F32)
        tmp[ROWS:256, :] = jnp.zeros((256 - ROWS, 512), F32)
        turned = tmp[...].T
        logs = jnp.concatenate(
            [log_ref[...].astype(F32), jnp.zeros((HEADS, 256 - ROWS), F32)], axis=1
        )
        for h in range(HEADS):
            delta = jnp.sum(turned[h * HSIZE : (h + 1) * HSIZE], axis=0, keepdims=True)
            log_row = logs[h : h + 1]
            part = grad[:, h * HSIZE : (h + 1) * HSIZE]
            late_ref[h, 0:HALF, 0:HSIZE] = part[:HALF]
            late_ref[h, 0:HALF, HSIZE:128] = part[HALF:]
            late_ref[h, HALF : HALF + 16, :] = jnp.concatenate(
                [
                    delta[:, 0:128],
                    delta[:, 128:256],
                    log_row[:, 0:128],
                    log_row[:, 128:256],
                    jnp.zeros((12, 128), F32),
                ],
                axis=0,
            ).astype(BF)


def conv_call(lengths, x, g, lo, hi, w, proj, attn, log):
    chunk = lambda i, *_: (0, 0, i)
    flat = lambda i, *_: (0, i)
    full3 = lambda i, *_: (0, 0, 0)
    full2 = lambda i, *_: (0, 0)
    return pl.pallas_call(
        conv_kernel,
        out_shape=(
            sds((1, ROWS, 1024)),
            sds((8, 544, 128)),
            sds((HEADS, HALF + 16, 128)),
        ),
        grid_spec=pltpu.PrefetchScalarGridSpec(
            num_scalar_prefetch=1,
            grid=(1024 // WIDTH,),
            in_specs=[
                pl.BlockSpec((1, ROWS, WIDTH), chunk),
                pl.BlockSpec((1, ROWS, WIDTH), chunk),
                pl.BlockSpec((48, WIDTH), flat),
                pl.BlockSpec((48, WIDTH), flat),
                pl.BlockSpec((TAPS, WIDTH), flat),
                pl.BlockSpec((512, WIDTH), flat),
                pl.BlockSpec((1, ROWS, 512), full3),
                pl.BlockSpec((HEADS, ROWS), full2),
            ],
            out_specs=[
                pl.BlockSpec((1, ROWS, WIDTH), chunk),
                pl.BlockSpec((WIDTH // 128, 544, 128), lambda i, *_: (i, 0, 0)),
                pl.BlockSpec((HEADS, HALF + 16, 128), full3),
            ],
            scratch_shapes=[
                pltpu.VMEM((256, 128), F32),
                pltpu.VMEM((224, 128), F32),
                pltpu.VMEM((224, 128), F32),
                pltpu.VMEM((ROWS, 512), F32),
                pltpu.VMEM((512, ROWS), BF),
                pltpu.VMEM((256, 512), F32),
            ],
        ),
        compiler_params=pltpu.CompilerParams(vmem_limit_bytes=FREE << 20),
        cost_estimate=cost(11),
    )(lengths, x, g, lo, hi, w, proj, attn, log)


CHUNK = HEADS * ROWS
BU = 512
BT = 1536


def key_rows(part, z, lanes):
    xh = lax.axis_index("xh")
    half = 1 - xh if part == 0 else xh
    row = ((half * 8 + z) * 2 + lax.axis_index("core")) * ROWS
    return row + lax.broadcasted_iota(jnp.int32, (ROWS, lanes), 0)


def unpack_rows(x, c, z, dst):
    left, right = x[:, 0:HSIZE], x[:, HSIZE:128]
    at = c * CHUNK + z * 128
    end = c * CHUNK + 1024 + z * 64
    dst[at : at + 96, :] = left
    dst[at + 96 : at + 128, :] = right[0:32]
    dst[end : end + 64, :] = right[32:96]


def turn_rows(dqt, dq, put):
    for b in range(3):
        dq[b * 512 : b * 512 + 512, :] = dqt[:, b * 512 : b * 512 + 512].T
    for z in range(8):
        at, end = z * 128, 1024 + z * 64
        put(z, slice(0, 96), slice(0, HSIZE), dq[at : at + 96, :])
        put(z, slice(0, 32), slice(HSIZE, 128), dq[at + 96 : at + 128, :])
        put(z, slice(32, 96), slice(HSIZE, 128), dq[end : end + 64, :])


def prep_early(lengths_ref, own_ref, qc_ref, kvx_ref, q_ref, k_ref, v_ref, kt_ref, kf):
    length = record_length(lengths_ref)
    for z in range(8):
        unpack_rows(own_ref[z, ROWS : ROWS + HALF, :], 0, z, q_ref)
        unpack_rows(qc_ref[z], 1, z, q_ref)
    for c in range(2):
        for z in range(8):
            kv = kvx_ref[z] if c == 0 else own_ref[z, 0:ROWS, :]
            at = c * CHUNK + z * ROWS
            k_ref[at : at + ROWS, :] = kv[:, 0:HSIZE]
            v_ref[at : at + ROWS, :] = kv[:, HSIZE:128]
            row = key_rows(c, z, 128)
            kf[at : at + ROWS, :] = jnp.where(row < length, kv.astype(F32) * 0.125, 0.0)
    for b in range(2 * CHUNK // 512):
        turned = kf[b * 512 : b * 512 + 512, :].T
        kt_ref[:, b * 512 : b * 512 + 512] = turned[0:HSIZE].astype(BF)


def prep_late(own_ref, core_ref, do_ref, st_ref):
    lane = lax.broadcasted_iota(jnp.int32, (1, 128), 1)
    for c, ref in enumerate((own_ref, core_ref)):
        stats = []
        for z in range(8):
            unpack_rows(ref[z, 0:HALF, :], c, z, do_ref)
            st = ref[z, HALF : HALF + 16, :].astype(F32)
            at = c * CHUNK + z * 128
            st_ref[0:1, at : at + 128] = st[0:1]
            st_ref[1:2, at : at + 128] = st[2:3]
            stats.append(st)
        for m in range(4):
            a, b = stats[2 * m], stats[2 * m + 1]
            at = c * CHUNK + 1024 + m * 128
            for row in range(2):
                src = 2 * row + 1
                st_ref[row : row + 1, at : at + 128] = jnp.where(
                    lane < 64, a[src : src + 1], pltpu.roll(b[src : src + 1], 64, 1)
                )


def score_tile(c, q, do, st, k, v, kt, dqt, dks, dvs):
    def key_block(ui, _):
        u0 = pl.multiple_of(ui * BU, BU)
        kb = k[pl.ds(u0, BU), :]
        vb = v[pl.ds(u0, BU), :]
        ktb = kt[:, pl.ds(u0, BU)]
        dk, dv = dks[pl.ds(u0, BU), :], dvs[pl.ds(u0, BU), :]
        for ti in range(CHUNK // BT):
            cols = slice(ti * BT, ti * BT + BT)
            at = slice(c * CHUNK + ti * BT, c * CHUNK + ti * BT + BT)
            qb = q[at, :]
            dob = do[at, :]
            s = lax.dot_general(kb, qb, NT, preferred_element_type=F32)
            p = jnp.exp(s - st[1:2, at])
            dp = lax.dot_general(vb, dob, NT, preferred_element_type=F32)
            ds = (p * (dp - st[0:1, at])).astype(BF)
            dv = dv + lax.dot_general(p.astype(BF), dob, NN, preferred_element_type=F32)
            dk = dk + lax.dot_general(ds, qb, NN, preferred_element_type=F32)
            dqt[:, cols] += lax.dot_general(ktb, ds, NN, preferred_element_type=F32)
        dks[pl.ds(u0, BU), :] = dk
        dvs[pl.ds(u0, BU), :] = dv
        return 0

    lax.fori_loop(0, CHUNK // BU, key_block, 0)


def tile_other_own(q, do, st, k, v, kt, dqo, dks, dvs):
    for ref in (dqo, dks, dvs):
        ref[...] = jnp.zeros_like(ref)
    score_tile(0, q, do, st, k, v, kt, dqo, dks, dvs)


def tile_other_core(lengths_ref, q, do, st, k, v, kt, dk_ref, dv_ref, dkv_ref, dqc, dks, dvs):
    dqc[...] = jnp.zeros_like(dqc)
    dks[...] = dk_ref[...]
    dvs[...] = dv_ref[...]
    score_tile(1, q, do, st, k, v, kt, dqc, dks, dvs)
    length = record_length(lengths_ref)
    for z in range(8):
        keep = key_rows(0, z, HSIZE) < length
        rows = slice(z * ROWS, z * ROWS + ROWS)
        dkv_ref[z, :, 0:HSIZE] = jnp.where(keep, dks[rows, :], 0.0).astype(BF)
        dkv_ref[z, :, HSIZE:128] = jnp.where(keep, dvs[rows, :], 0.0).astype(BF)


def tile_own_core(q, do, st, k, v, kt, dqc_ref, dq_ref, dks, dvs, dqt, dq):
    dks[...] = jnp.zeros_like(dks)
    dvs[...] = jnp.zeros_like(dvs)
    dqt[...] = dqc_ref[...]
    score_tile(1, q, do, st, k, v, kt, dqt, dks, dvs)

    def put(z, rows, cols, value):
        dq_ref[z, rows, cols] = value.astype(BF)

    turn_rows(dqt, dq, put)


def tile_own_own(q, do, st, k, v, kt, dqo_ref, dk_ref, dv_ref, dqt, dks, dvs):
    dqt[...] = dqo_ref[...]
    dks[...] = dk_ref[...]
    dvs[...] = dv_ref[...]
    score_tile(0, q, do, st, k, v, kt, dqt, dks, dvs)


def tile_call(body, part, lengths, tensors, extra, outs, scratch=()):
    full = lambda *_: (0, 0)
    whole = lambda x: pl.BlockSpec(x.shape, lambda *_: (0,) * len(x.shape))
    specs = [
        pl.BlockSpec((2 * CHUNK, HSIZE), full),
        pl.BlockSpec((2 * CHUNK, HSIZE), full),
        pl.BlockSpec((8, 2 * CHUNK), full),
        pl.BlockSpec((CHUNK, HSIZE), lambda *_: (part, 0)),
        pl.BlockSpec((CHUNK, HSIZE), lambda *_: (part, 0)),
        pl.BlockSpec((HSIZE, CHUNK), lambda *_: (0, part)),
    ] + [whole(e) for e in extra]
    args = list(tensors) + list(extra)
    if lengths is not None:
        specs.insert(0, pl.BlockSpec(memory_space=pltpu.SMEM))
        args.insert(0, lengths)
    return call(
        body,
        outs,
        7,
        40,
        grid=(1,),
        in_specs=specs,
        out_specs=tuple(whole(o) for o in outs),
        scratch_shapes=scratch,
    )(*args)


def combine(lengths_ref, dk_ref, dv_ref, got_ref, dqt_ref, dqgot_ref, o_ref, dq):
    length = record_length(lengths_ref)
    for z in range(8):
        keep = key_rows(1, z, HSIZE) < length
        rows = slice(z * ROWS, z * ROWS + ROWS)
        got = got_ref[z].astype(F32)
        dk = jnp.where(keep, dk_ref[rows, :], 0.0) + got[:, 0:HSIZE]
        dv = jnp.where(keep, dv_ref[rows, :], 0.0) + got[:, HSIZE:128]
        o_ref[z, 0:ROWS, 0:HSIZE] = dk.astype(BF)
        o_ref[z, 0:ROWS, HSIZE:128] = dv.astype(BF)

    def put(z, rows, cols, value):
        to = slice(ROWS + rows.start, ROWS + rows.stop)
        o_ref[z, to, cols] = (value + dqgot_ref[z, rows, cols].astype(F32)).astype(BF)

    turn_rows(dqt_ref, dq, put)


def unpack_final(x_ref, q_ref, k_ref, v_ref):
    for h in range(HEADS):
        cols = slice(h * HSIZE, (h + 1) * HSIZE)
        k_ref[0, :, cols] = x_ref[h, 0:ROWS, 0:HSIZE]
        v_ref[0, :, cols] = x_ref[h, 0:ROWS, HSIZE:128]
        q_ref[0, 0:HALF, cols] = x_ref[h, ROWS : ROWS + HALF, 0:HSIZE]
        q_ref[0, HALF:ROWS, cols] = x_ref[h, ROWS : ROWS + HALF, HSIZE:128]


def split_sums(x_ref, keep_ref, send_ref):
    core = lax.axis_index("core")
    keep_ref[...] = x_ref[pl.ds(core * 4, 4)]
    send_ref[...] = x_ref[pl.ds((1 - core) * 4, 4)]


def finish_sums(lengths_ref, own_ref, got_ref, proj_ref, taps_ref):
    total = lengths_ref[0]
    for r in range(1, 8):
        total = total + lengths_ref[r]
    scale = lax.rsqrt(jnp.full((1, 128), total, jnp.int32).astype(F32))
    core = lax.axis_index("core")
    for c in range(8):
        cols = slice(c * 128, c * 128 + 128)
        own, got = own_ref[c % 4].astype(F32), got_ref[c % 4].astype(F32)
        x = jnp.where(core == c // 4, own, got) * scale
        proj_ref[:, cols] = x[0:512]
        taps_ref[:, cols] = x[512:543]


def flip(x, axis, mask, size):
    return lax.ppermute(x, axis, [(i, i ^ mask) for i in range(size)])


def add(*terms):
    pair = [a.astype(F32) + b.astype(F32) for a, b in zip(terms[::2], terms[1::2])]
    return (pair[0] if len(pair) == 1 else pair[0] + pair[1]).astype(BF)


def reduce_dp(x, shift, count):
    me = (lax.axis_index("dp") >> shift) & (count - 1)
    pieces = x.reshape(count, x.shape[0] // count, 128)
    piece = lambda i: lax.dynamic_index_in_dim(pieces, i, 0, keepdims=False)
    got = [flip(piece(me ^ d), "dp", d << shift, 8) for d in range(1, count)]
    return add(piece(me), *got)


def sum_four(x, low, high):
    axes = ("xh", "z")
    return add(x, *[flip(x, axes, mask, 16) for mask in (low, high, low | high)])


def gather_y(x):
    y = lax.axis_index("dp") >> 1
    odd, upper = (y & 1) == 1, (y & 2) == 2
    a, b, c, d = (x, *[flip(x, "dp", m << 1, 8) for m in (1, 2, 3)])
    low = jnp.concatenate([jnp.where(odd, b, a), jnp.where(odd, a, b)], axis=0)
    high = jnp.concatenate([jnp.where(odd, d, c), jnp.where(odd, c, d)], axis=0)
    return jnp.concatenate([jnp.where(upper, high, low), jnp.where(upper, low, high)], axis=0)


def gather_x(x):
    odd = (lax.axis_index("dp") & 1) == 1
    got = flip(x, "dp", 1, 8)
    return jnp.concatenate([jnp.where(odd, got, x), jnp.where(odd, x, got)], axis=0)


def after(x, *first):
    return lax.optimization_barrier((x,) + first)[0]


def swap(x, axis):
    return lax.ppermute(x, axis, [(0, 1), (1, 0)])


def shards(query, key, value, attn, log, lengths, x, g, proj, taps):
    smem = pl.BlockSpec(memory_space=pltpu.SMEM)
    vmem = pl.BlockSpec(memory_space=pltpu.VMEM)
    up = [(i, i + 1) for i in range(31)]
    down = [(i + 1, i) for i in range(31)]
    packed, last, first = pack_call(query, key, value, x, g)
    lo = lax.ppermute(last, SEQ, up)
    hi = lax.ppermute(first, SEQ, down)
    early = lax.all_to_all(packed, "z", 0, 0, tiled=True)

    grad_state, sums, late = conv_call(lengths, x, g, lo, hi, taps, proj, attn, log[0].T)
    late = lax.all_to_all(after(late, early), "z", 0, 0, tiled=True)

    kvx = swap(early[:, :ROWS], "xh")
    qc = swap(early[:, ROWS:], "core")
    q, k, v, kt = call(
        prep_early,
        (sds((2 * CHUNK, HSIZE)),) * 3 + (sds((HSIZE, 2 * CHUNK)),),
        2,
        16,
        in_specs=[smem, vmem, vmem, vmem],
        scratch_shapes=[pltpu.VMEM((2 * CHUNK, 128), F32)],
    )(lengths, early, qc, kvx)

    keep, send = call(
        split_sums, (sds((4, 544, 128)),) * 2, 40, 8, in_specs=[vmem], out_specs=[vmem, vmem]
    )(after(sums, early))
    sums = add(keep, swap(send, "core")).reshape(2176, 128)
    sums = reduce_dp(after(sums, kvx), 0, 2)

    late_core = swap(late, "core")
    do, st = call(prep_late, (sds((2 * CHUNK, HSIZE)), sds((8, 2 * CHUNK), F32)), 1, 8)(
        late, late_core
    )
    do = after(do, sums)
    tensors = (q, do, st, k, v, kt)
    grad = sds((CHUNK, HSIZE), F32)
    turned = sds((HSIZE, CHUNK), F32)
    fgrad = pltpu.VMEM((CHUNK, HSIZE), F32)
    fturned = pltpu.VMEM((HSIZE, CHUNK), F32)
    sums = reduce_dp(sums, 1, 4)
    dqo, dk, dv = tile_call(tile_other_own, 0, None, tensors, (), (turned, grad, grad))
    dk = after(dk, sums)
    sums = sum_four(sums, 1, 8)
    dkv_other, dqc = tile_call(
        tile_other_core,
        0,
        lengths,
        tensors,
        (dk, dv),
        (sds((HEADS, ROWS, 128)), turned),
        [fgrad, fgrad],
    )
    dkv_got = swap(dkv_other, "xh")
    dqc = after(dqc, sums)
    sums = sum_four(sums, 2, 4)
    dq_core, dk, dv = tile_call(
        tile_own_core, 1, None, tensors, (dqc,), (sds((8, HALF, 128)), grad, grad), [fturned, fgrad]
    )
    dq_got = swap(dq_core, "core")
    dk = after(dk, sums, dkv_got)
    sums = gather_y(sums)
    dqo, dk, dv = tile_call(tile_own_own, 1, None, tensors, (dqo, dk, dv), (turned, grad, grad))
    dk = after(dk, sums)
    back = call(
        combine,
        sds((HEADS, ROWS + HALF, 128)),
        2,
        16,
        in_specs=[smem] + [vmem] * 5,
        scratch_shapes=[fgrad],
    )(lengths, dk, dv, dkv_got, dqo, dq_got)

    sums, back = lax.optimization_barrier((sums, back))
    back = lax.all_to_all(back, "z", 0, 0, tiled=True)
    sums = gather_x(sums).reshape(4, 544, 128)
    grad_proj, grad_taps = call(
        finish_sums,
        (sds((512, 1024), F32), sds((TAPS, 1024), F32)),
        2,
        8,
        in_specs=[smem, vmem, vmem],
    )(lengths, sums, swap(sums, "core"))
    grad_q, grad_k, grad_v = call(unpack_final, (sds((1, ROWS, 512)),) * 3, 2, 8)(back)
    return grad_q, grad_k, grad_v, grad_state, grad_proj, grad_taps


def solution(mesh):
    inner = Mesh(mesh.devices.reshape(8, 2, 8, 2), ALL)
    rows = P("dp", SEQ, None)
    in_specs = (rows,) * 5 + (P(), rows, rows, P(), P())
    out_specs = (rows,) * 4 + (P(), P())
    return jax.shard_map(
        shards, mesh=inner, in_specs=in_specs, out_specs=out_specs, check_vma=False
    )
```

time: 225 us -> 148 us (0.66)
  Pallas kernels: 81.1 us -> 49.8 us
  waiting for transfers between devices: 55 us -> 34.6 us
  starting transfers between devices: 70 us -> 56.6 us
  local copies, waits for them, and re-layouts: 9.92 us -> 4.44 us
  other arithmetic: 6.26 us -> 1.5 us
    pallas_call x13 -> x10, Pallas kernels: 66.5 us -> 36.7 us  [the longest x4 27.3 us: tile_call(): call(body, outs, 7, 40, grid=(1,), in_specs=specs, out_specs=tuple((whole...]
    ppermute x16 -> x14, waiting for transfers between devices: 29.9 us -> 12.8 us  [flip(): return lax.ppermute(x, axis, [(i, i ^ mask) for i in range(size)])]
    ppermute x16 -> x14, starting transfers between devices: 31 us -> 19.2 us  [flip(): return lax.ppermute(x, axis, [(i, i ^ mask) for i in range(size)])]
    all_to_all x1, waiting for transfers between devices: 0.01 us -> 4.37 us  [shards(): early = lax.all_to_all(packed, 'z', 0, 0, tiled=True)]
    all_to_all x2, waiting for transfers between devices: 15.1 us -> 10.9 us  [the longest x1 10.1 us: shards(): back = lax.all_to_all(back, 'z', 0, 0, tiled=True)]
    all_to_all x2, starting transfers between devices: 10.5 us -> 6.94 us  [the longest x1 3.54 us: shards(): back = lax.all_to_all(back, 'z', 0, 0, tiled=True)]
    all_to_all x1, starting transfers between devices: 3.79 us -> 7.3 us  [shards(): early = lax.all_to_all(packed, 'z', 0, 0, tiled=True)]
    ppermute x5 -> x7, waiting for transfers between devices: 9.89 us -> 6.52 us  [swap(): return lax.ppermute(x, axis, [(0, 1), (1, 0)])]
  transfers between devices with their start and end apart: 26 -> 26, of which waited for: 13 -> 10; matrix products, arithmetic and copies ran while one was open for 4% -> 1% of each run, Pallas kernels for 30% -> 29%
where the time goes in v2:
time: 148 us
  starting transfers between devices  56.6 us (38%)
  Pallas kernels  49.8 us (34%)
  waiting for transfers between devices  34.6 us (23%)
  local copies, waits for them, and re-layouts  4.44 us (3%)
  other arithmetic  1.5 us (1%)
    pallas_call x4, Pallas kernels, tile_call(): call(body, outs, 7, 40, grid=(1,), in_specs=specs, out_specs=tuple((whole...  27.3 us
    ppermute x14, starting transfers between devices, flip(): return lax.ppermute(x, axis, [(i, i ^ mask) for i in range(size)])  19.2 us
    ppermute x7, starting transfers between devices, swap(): return lax.ppermute(x, axis, [(0, 1), (1, 0)])  16.3 us
    ppermute x14, waiting for transfers between devices, flip(): return lax.ppermute(x, axis, [(i, i ^ mask) for i in range(size)])  12.8 us
    pallas_call x1, Pallas kernels, conv_call(): pl.pallas_call(conv_kernel, out_shape=(sds((1, ROWS, 1024)), sds((8, 544,...  11.6 us
    all_to_all x1, waiting for transfers between devices, shards(): back = lax.all_to_all(back, 'z', 0, 0, tiled=True)  10.1 us
    all_to_all x1, starting transfers between devices, shards(): early = lax.all_to_all(packed, 'z', 0, 0, tiled=True)  7.3 us
    ppermute x7, waiting for transfers between devices, swap(): return lax.ppermute(x, axis, [(0, 1), (1, 0)])  6.52 us
  transfers between devices with their start and end apart: 26, of which 10 were waited for; matrix products, arithmetic and copies ran while one was open for 1% of the time, Pallas kernels for 29%

profile of v2, /device:TPU:1, one launch (start us, length us, event | category | flops | bytes accessed | tf_op | source)
XLA Modules:
  0.0 147.9 jit_solution(8863296145111726013)
XLA Ops:
  3.0 4.9 %collective-permute-start = (bf16[48,1024]{1,0:T(8,128)(2,1)}, bf16[48,1024]{1,0:T(8,128)(2,1)S(1)}, u32[]{:S(2)}, u32[]{:S(2)}) collective-permute-start(bf16[48,1024]{1,0:T(8,128)(2,1)} %get-tuple-element.46), channel_id=1, source_target_pairs={{0,1},{1,2},{2,3},{3,4},{4,5},{5,6},{6,7},{7,8},{8,9},{9,10},{10,1... | collective-permute-start | bytes 294920 | tf_op jit(solution)/shard_map/ppermute | solution.py:474
  9.9 7.3 %all-to-all-start = ((bf16[8,288,128]{2,1,0:T(8,128)(2,1)}), bf16[8,288,128]{2,1,0:T(8,128)(2,1)S(1)}, u32[]{:S(2)}, u32[]{:S(2)}) async-start(bf16[8,288,128]{2,1,0:T(8,128)(2,1)} %get-tuple-element.49), calls=%async_computation | async-start | bytes 1179648 | tf_op jit(solution)/shard_map/all_to_all | solution.py:476
  17.8 11.6 %shard_map.146 = (bf16[1,192,1024]{2,1,0:T(8,128)(2,1)}, bf16[8,544,128]{2,1,0:T(8,128)(2,1)}, bf16[8,112,128]{2,1,0:T(8,128)(2,1)}) custom-call(s32[8]{0:T(128)} %lengths_ref.9, bf16[1,192,1024]{2,1,0:T(8,128)(2,1)} %x_ref.1, bf16[1,192,1024]{2,1,0:T(8,128)(2,1)} %g_ref.1, bf16[48,1024]{1,0:T(8,128)(2,1)} %copy-done.8, bf16[48,1024]{1,0:T(8,128)(2,1)} %copy-done.9, ...), custom_call_target="tpu_custom_call" | custom-call | flops 12650000384 | bytes 1048576 | tf_op jit(solution)/shard_map/pallas_call | solution.py:176
  29.4 4.4 %all-to-all-done.own_ref = bf16[8,288,128]{2,1,0:T(8,128)(2,1)S(1)} async-done(((bf16[8,288,128]{2,1,0:T(8,128)(2,1)}), bf16[8,288,128]{2,1,0:T(8,128)(2,1)S(1)}, u32[]{:S(2)}, u32[]{:S(2)}) %all-to-all-start) | async-done | bytes 589856 | tf_op jit(solution)/shard_map/all_to_all | solution.py:476
  35.1 3.3 %collective-permute-start.2 = (bf16[4,544,128]{2,1,0:T(8,128)(2,1)S(1)}, bf16[4,544,128]{2,1,0:T(8,128)(2,1)S(1)}, u32[]{:S(2)}, u32[]{:S(2)}) collective-permute-start(bf16[4,544,128]{2,1,0:T(8,128)(2,1)S(1)} %get-tuple-element.52), channel_id=1, source_target_pairs={{0,1},{1,0},{2,3},{3,2},{4,5},{5,4},{6,7},{7,6},{8,9},{9,8},{10,11... | collective-permute-start | bytes 1671176 | tf_op jit(solution)/shard_map/ppermute | solution.py:465
  38.5 2.8 %collective-permute-start.3 = (bf16[8,192,128]{2,1,0:T(8,128)(2,1)S(1)}, bf16[8,192,128]{2,1,0:T(8,128)(2,1)S(1)}, u32[]{:S(2)}, u32[]{:S(2)}) collective-permute-start(bf16[8,192,128]{2,1,0:T(8,128)(2,1)S(1)} %slice.8), channel_id=1, source_target_pairs={{0,16},{16,0},{1,17},{17,1},{2,18},{18,2},{3,19},{19,3},{4,20},{20... | collective-permute-start | bytes 1179656 | tf_op jit(solution)/shard_map/ppermute | solution.py:465
  41.3 3.4 %all-to-all-start.1 = ((bf16[8,112,128]{2,1,0:T(8,128)(2,1)}), bf16[8,112,128]{2,1,0:T(8,128)(2,1)S(1)}, u32[]{:S(2)}, u32[]{:S(2)}) async-start(bf16[8,112,128]{2,1,0:T(8,128)(2,1)} %get-tuple-element.56), calls=%async_computation.1 | async-start | bytes 458752 | tf_op jit(solution)/shard_map/all_to_all | solution.py:479
  45.9 4.9 %collective-permute-done.3.kvx_ref = bf16[8,192,128]{2,1,0:T(8,128)(2,1)S(1)} collective-permute-done((bf16[8,192,128]{2,1,0:T(8,128)(2,1)S(1)}, bf16[8,192,128]{2,1,0:T(8,128)(2,1)S(1)}, u32[]{:S(2)}, u32[]{:S(2)}) %collective-permute-start.3) | collective-permute-done | bytes 393248 | tf_op jit(solution)/shard_map/ppermute | solution.py:465
  60.8 2.6 %collective-permute-start.6 = (bf16[272,128]{1,0:T(8,128)(2,1)S(1)}, bf16[272,128]{1,0:T(8,128)(2,1)S(1)}, u32[]{:S(2)}, u32[]{:S(2)}) collective-permute-start(bf16[272,128]{1,0:T(8,128)(2,1)S(1)} %get-tuple-element.92), channel_id=1, source_target_pairs={{0,128},{32,160},{64,192},{96,224},{128,0},{160,32},{192,64},{224,... | collective-permute-start | bytes 208904 | tf_op jit(solution)/shard_map/ppermute | solution.py:424
  65.9 2.7 %collective-permute-done.7 = bf16[272,128]{1,0:T(8,128)(2,1)S(1)} collective-permute-done((bf16[272,128]{1,0:T(8,128)(2,1)S(1)}, bf16[272,128]{1,0:T(8,128)(2,1)S(1)}, u32[]{:S(2)}, u32[]{:S(2)}) %collective-permute-start.7) | collective-permute-done | bytes 69664 | tf_op jit(solution)/shard_map/ppermute | solution.py:424
  68.6 2.8 %collective-permute-start.10 = (bf16[272,128]{1,0:T(8,128)(2,1)S(1)}, bf16[272,128]{1,0:T(8,128)(2,1)S(1)}, u32[]{:S(2)}, u32[]{:S(2)}) collective-permute-start(bf16[272,128]{1,0:T(8,128)(2,1)S(1)} %fusion.2), channel_id=1, source_target_pairs={{0,18},{2,16},{4,22},{6,20},{8,26},{10,24},{12,30},{14,28},{16,2},... | collective-permute-start | bytes 208904 | tf_op jit(solution)/shard_map/ppermute | solution.py:424
  72.9 6.5 %shard_map.150 = (f32[64,1536]{1,0:T(8,128)S(1)}, f32[1536,64]{1,0:T(8,128)S(1)}, f32[1536,64]{1,0:T(8,128)S(1)}) custom-call(bf16[3072,64]{1,0:T(8,128)(2,1)S(1)} %get-tuple-element.54.q, bf16[3072,64]{1,0:T(8,128)(2,1)S(1)} %get-tuple-element.58.do, f32[8,3072]{1,0:T(8,128)S(1)} %get-tuple-element.59.st, bf16[3072,64]{1,0:T(8,128)(2,1)S(1)} %copy-done.2, ...), custom_call_target="tpu_custom_call" | custom-call | flops 8049999872 | bytes 1048576 | tf_op jit(solution)/shard_map/pallas_call | solution.py:364
  81.8 3.5 %collective-permute-start.13 = (bf16[272,128]{1,0:T(8,128)(2,1)S(1)}, bf16[272,128]{1,0:T(8,128)(2,1)S(1)}, u32[]{:S(2)}, u32[]{:S(2)}) collective-permute-start(bf16[272,128]{1,0:T(8,128)(2,1)S(1)} %add_convert_fusion.2), channel_id=1, source_target_pairs={{0,12},{2,14},{4,8},{6,10},{8,4},{10,6},{12,0},{14,2},{16,28},{18,... | collective-permute-start | bytes 208904 | tf_op jit(solution)/shard_map/ppermute | solution.py:424
  85.2 7.3 %shard_map.151 = (bf16[8,192,128]{2,1,0:T(8,128)(2,1)S(1)}, f32[64,1536]{1,0:T(8,128)S(1)}) custom-call(s32[8]{0:T(128)S(1)} %copy-done, bf16[3072,64]{1,0:T(8,128)(2,1)S(1)} %get-tuple-element.54.q, bf16[3072,64]{1,0:T(8,128)(2,1)S(1)} %get-tuple-element.58.do, f32[8,3072]{1,0:T(8,128)S(1)} %get-tuple-element.59.st, bf16[3072,64]{1,0:T(8,128)(2,1)S(1)} %copy-done.2, ...), custom_call_target="tpu_custom_call" | custom-call | flops 8049999872 | bytes 1048576 | tf_op jit(solution)/shard_map/pallas_call | solution.py:364
  92.6 2.8 %collective-permute-start.19 = (bf16[8,192,128]{2,1,0:T(8,128)(2,1)S(1)}, bf16[8,192,128]{2,1,0:T(8,128)(2,1)S(1)}, u32[]{:S(2)}, u32[]{:S(2)}) collective-permute-start(bf16[8,192,128]{2,1,0:T(8,128)(2,1)S(1)} %get-tuple-element.70), channel_id=1, source_target_pairs={{0,16},{16,0},{1,17},{17,1},{2,18},{18,2},{3,19},{19,3},{4,20},{20... | collective-permute-start | bytes 1179656 | tf_op jit(solution)/shard_map/ppermute | solution.py:465
  95.5 7.0 %shard_map.152 = (bf16[8,96,128]{2,1,0:T(8,128)(2,1)S(1)}, f32[1536,64]{1,0:T(8,128)S(1)}, f32[1536,64]{1,0:T(8,128)S(1)}) custom-call(bf16[3072,64]{1,0:T(8,128)(2,1)S(1)} %get-tuple-element.54.q, bf16[3072,64]{1,0:T(8,128)(2,1)S(1)} %get-tuple-element.58.do, f32[8,3072]{1,0:T(8,128)S(1)} %get-tuple-element.59.st, bf16[3072,64]{1,0:T(8,128)(2,1)S(1)} %copy-done.2, ...), custom_call_target="tpu_custom_call" | custom-call | flops 8049999872 | bytes 1048576 | tf_op jit(solution)/shard_map/pallas_call | solution.py:364
  102.5 4.7 %collective-permute-start.20 = (bf16[8,96,128]{2,1,0:T(8,128)(2,1)S(1)}, bf16[8,96,128]{2,1,0:T(8,128)(2,1)S(1)}, u32[]{:S(2)}, u32[]{:S(2)}) collective-permute-start(bf16[8,96,128]{2,1,0:T(8,128)(2,1)S(1)} %get-tuple-element.77), channel_id=1, source_target_pairs={{0,1},{1,0},{2,3},{3,2},{4,5},{5,4},{6,7},{7,6},{8,9},{9,8},{10,11... | collective-permute-start | bytes 589832 | tf_op jit(solution)/shard_map/ppermute | solution.py:465
  107.8 3.0 %collective-permute-start.15 = (bf16[272,128]{1,0:T(8,128)(2,1)S(1)}, bf16[272,128]{1,0:T(8,128)(2,1)S(1)}, u32[]{:S(2)}, u32[]{:S(2)}) collective-permute-start(bf16[272,128]{1,0:T(8,128)(2,1)S(1)} %add_convert_fusion.1), channel_id=1, source_target_pairs={{0,128},{32,160},{64,192},{96,224},{128,0},{160,32},{192,64},{224,... | collective-permute-start | bytes 208904 | tf_op jit(solution)/shard_map/ppermute | solution.py:424
  110.8 2.9 %collective-permute-done.14 = bf16[272,128]{1,0:T(8,128)(2,1)S(1)} collective-permute-done((bf16[272,128]{1,0:T(8,128)(2,1)S(1)}, bf16[272,128]{1,0:T(8,128)(2,1)S(1)}, u32[]{:S(2)}, u32[]{:S(2)}) %collective-permute-start.14) | collective-permute-done | bytes 69664 | tf_op jit(solution)/shard_map/ppermute | solution.py:424
  113.8 6.5 %shard_map.153 = (f32[64,1536]{1,0:T(8,128)S(1)}, f32[1536,64]{1,0:T(8,128)S(1)}, f32[1536,64]{1,0:T(8,128)S(1)}) custom-call(bf16[3072,64]{1,0:T(8,128)(2,1)S(1)} %get-tuple-element.54.q, bf16[3072,64]{1,0:T(8,128)(2,1)S(1)} %get-tuple-element.58.do, f32[8,3072]{1,0:T(8,128)S(1)} %get-tuple-element.59.st, bf16[3072,64]{1,0:T(8,128)(2,1)S(1)} %copy-done.2, ...), custom_call_target="tpu_custom_call" | custom-call | flops 8049999872 | bytes 1048576 | tf_op jit(solution)/shard_map/pallas_call | solution.py:364
  120.3 3.3 %shard_map.154 = bf16[8,288,128]{2,1,0:T(8,128)(2,1)} custom-call(s32[8]{0:T(128)S(1)} %copy-done, f32[1536,64]{1,0:T(8,128)S(1)} %get-tuple-element.74.dk_ref, f32[1536,64]{1,0:T(8,128)S(1)} %get-tuple-element.75.dv_ref, bf16[8,192,128]{2,1,0:T(8,128)(2,1)S(1)} %collective-permute-done.19.got_ref, f32[64,1536]{1,0:T(8,128)S(1)} %get-tuple-element.76.dqt_ref, ...), custom_call_target="tpu_custom_call" | custom-call | flops 2300000000 | bytes 1048576 | tf_op jit(solution)/shard_map/pallas_call | solution.py:532
  123.9 3.5 %all-to-all-start.2 = ((bf16[8,288,128]{2,1,0:T(8,128)(2,1)}), bf16[8,288,128]{2,1,0:T(8,128)(2,1)S(1)}, u32[]{:S(2)}, u32[]{:S(2)}) async-start(bf16[8,288,128]{2,1,0:T(8,128)(2,1)} %shard_map.154), calls=%async_computation.2 | async-start | bytes 1179648 | tf_op jit(solution)/shard_map/all_to_all | solution.py:542
  127.5 3.4 %collective-permute-done.21 = bf16[1088,128]{1,0:T(8,128)(2,1)S(1)} collective-permute-done((bf16[1088,128]{1,0:T(8,128)(2,1)S(1)}, bf16[1088,128]{1,0:T(8,128)(2,1)S(1)}, u32[]{:S(2)}, u32[]{:S(2)}) %collective-permute-start.21) | collective-permute-done | bytes 278560 | tf_op jit(solution)/shard_map/ppermute | solution.py:424
  136.7 10.1 %all-to-all-done.2.x_ref = bf16[8,288,128]{2,1,0:T(8,128)(2,1)S(1)} async-done(((bf16[8,288,128]{2,1,0:T(8,128)(2,1)}), bf16[8,288,128]{2,1,0:T(8,128)(2,1)S(1)}, u32[]{:S(2)}, u32[]{:S(2)}) %all-to-all-start.2) | async-done | bytes 589856 | tf_op jit(solution)/shard_map/all_to_all | solution.py:542
  (75 shorter events, 31.7 us)
Async XLA Ops:
  3.0 14.2 %collective-permute-start = (bf16[48,1024]{1,0:T(8,128)(2,1)}, bf16[48,1024]{1,0:T(8,128)(2,1)S(1)}, u32[]{:S(2)}, u32[]{:S(2)}) collective-permute-start(bf16[48,1024]{1,0:T(8,128)(2,1)} %get-tuple-element.46), channel_id=1, source_target_pairs={{0,1},{1,2},{2,3},{3,4},{4,5},{5,6},{6,7},{7,8},{8,9},{9,10},{10,1... | collective-permute-start | bytes 294920 | tf_op jit(solution)/shard_map/ppermute | solution.py:474
  7.9 9.2 %collective-permute-start.1 = (bf16[48,1024]{1,0:T(8,128)(2,1)}, bf16[48,1024]{1,0:T(8,128)(2,1)S(1)}, u32[]{:S(2)}, u32[]{:S(2)}) collective-permute-start(bf16[48,1024]{1,0:T(8,128)(2,1)} %get-tuple-element.47), channel_id=1, source_target_pairs={{1,0},{2,1},{3,2},{4,3},{5,4},{6,5},{7,6},{8,7},{9,8},{10,9},{11,1... | collective-permute-start | bytes 294920 | tf_op jit(solution)/shard_map/ppermute | solution.py:475
  9.9 23.9 %all-to-all-start = ((bf16[8,288,128]{2,1,0:T(8,128)(2,1)}), bf16[8,288,128]{2,1,0:T(8,128)(2,1)S(1)}, u32[]{:S(2)}, u32[]{:S(2)}) async-start(bf16[8,288,128]{2,1,0:T(8,128)(2,1)} %get-tuple-element.49), calls=%async_computation | async-start | bytes 1179648 | tf_op jit(solution)/shard_map/all_to_all | solution.py:476
  35.1 10.6 %collective-permute-start.2 = (bf16[4,544,128]{2,1,0:T(8,128)(2,1)S(1)}, bf16[4,544,128]{2,1,0:T(8,128)(2,1)S(1)}, u32[]{:S(2)}, u32[]{:S(2)}) collective-permute-start(bf16[4,544,128]{2,1,0:T(8,128)(2,1)S(1)} %get-tuple-element.52), channel_id=1, source_target_pairs={{0,1},{1,0},{2,3},{3,2},{4,5},{5,4},{6,7},{7,6},{8,9},{9,8},{10,11... | collective-permute-start | bytes 1671176 | tf_op jit(solution)/shard_map/ppermute | solution.py:465
  38.5 12.3 %collective-permute-start.3 = (bf16[8,192,128]{2,1,0:T(8,128)(2,1)S(1)}, bf16[8,192,128]{2,1,0:T(8,128)(2,1)S(1)}, u32[]{:S(2)}, u32[]{:S(2)}) collective-permute-start(bf16[8,192,128]{2,1,0:T(8,128)(2,1)S(1)} %slice.8), channel_id=1, source_target_pairs={{0,16},{16,0},{1,17},{17,1},{2,18},{18,2},{3,19},{19,3},{4,20},{20... | collective-permute-start | bytes 1179656 | tf_op jit(solution)/shard_map/ppermute | solution.py:465
  41.3 15.0 %all-to-all-start.1 = ((bf16[8,112,128]{2,1,0:T(8,128)(2,1)}), bf16[8,112,128]{2,1,0:T(8,128)(2,1)S(1)}, u32[]{:S(2)}, u32[]{:S(2)}) async-start(bf16[8,112,128]{2,1,0:T(8,128)(2,1)} %get-tuple-element.56), calls=%async_computation.1 | async-start | bytes 458752 | tf_op jit(solution)/shard_map/all_to_all | solution.py:479
  45.4 6.7 %collective-permute-start.17 = (bf16[8,96,128]{2,1,0:T(8,128)(2,1)}, bf16[8,96,128]{2,1,0:T(8,128)(2,1)S(1)}, u32[]{:S(2)}, u32[]{:S(2)}) collective-permute-start(bf16[8,96,128]{2,1,0:T(8,128)(2,1)} %slice.9), channel_id=1, source_target_pairs={{0,1},{1,0},{2,3},{3,2},{4,5},{5,4},{6,7},{7,6},{8,9},{9,8},{10,11... | collective-permute-start | bytes 589832 | tf_op jit(solution)/shard_map/ppermute | solution.py:465
  50.8 7.6 %collective-permute-start.4 = (bf16[1088,128]{1,0:T(8,128)(2,1)S(1)}, bf16[1088,128]{1,0:T(8,128)(2,1)}, u32[]{:S(2)}, u32[]{:S(2)}) collective-permute-start(bf16[1088,128]{1,0:T(8,128)(2,1)S(1)} %dynamic-slice_bitcast_fusion), channel_id=1, source_target_pairs={{0,32},{32,0},{64,96},{96,64},{128,160},{160,128},{192,224},{224,1... | collective-permute-start | bytes 835592 | tf_op jit(solution)/shard_map/ppermute | solution.py:424
  56.3 7.2 %collective-permute-start.18 = (bf16[8,112,128]{2,1,0:T(8,128)(2,1)S(1)}, bf16[8,112,128]{2,1,0:T(8,128)(2,1)S(1)}, u32[]{:S(2)}, u32[]{:S(2)}) collective-permute-start(bf16[8,112,128]{2,1,0:T(8,128)(2,1)S(1)} %all-to-all-done.1.own_ref), channel_id=1, source_target_pairs={{0,1},{1,0},{2,3},{3,2},{4,5},{5,4},{6,7},{7,6},{8,9},{9,8},{10,11... | collective-permute-start | bytes 688136 | tf_op jit(solution)/shard_map/ppermute | solution.py:465
  60.8 5.1 %collective-permute-start.6 = (bf16[272,128]{1,0:T(8,128)(2,1)S(1)}, bf16[272,128]{1,0:T(8,128)(2,1)S(1)}, u32[]{:S(2)}, u32[]{:S(2)}) collective-permute-start(bf16[272,128]{1,0:T(8,128)(2,1)S(1)} %get-tuple-element.92), channel_id=1, source_target_pairs={{0,128},{32,160},{64,192},{96,224},{128,0},{160,32},{192,64},{224,... | collective-permute-start | bytes 208904 | tf_op jit(solution)/shard_map/ppermute | solution.py:424
  63.5 5.1 %collective-permute-start.7 = (bf16[272,128]{1,0:T(8,128)(2,1)S(1)}, bf16[272,128]{1,0:T(8,128)(2,1)S(1)}, u32[]{:S(2)}, u32[]{:S(2)}) collective-permute-start(bf16[272,128]{1,0:T(8,128)(2,1)S(1)} %get-tuple-element.91), channel_id=1, source_target_pairs={{0,192},{32,224},{64,128},{96,160},{128,64},{160,96},{192,0},{224,... | collective-permute-start | bytes 208904 | tf_op jit(solution)/shard_map/ppermute | solution.py:424
  68.6 10.8 %collective-permute-start.10 = (bf16[272,128]{1,0:T(8,128)(2,1)S(1)}, bf16[272,128]{1,0:T(8,128)(2,1)S(1)}, u32[]{:S(2)}, u32[]{:S(2)}) collective-permute-start(bf16[272,128]{1,0:T(8,128)(2,1)S(1)} %fusion.2), channel_id=1, source_target_pairs={{0,18},{2,16},{4,22},{6,20},{8,26},{10,24},{12,30},{14,28},{16,2},... | collective-permute-start | bytes 208904 | tf_op jit(solution)/shard_map/ppermute | solution.py:424
  71.5 8.0 %collective-permute-start.8 = (bf16[272,128]{1,0:T(8,128)(2,1)S(1)}, bf16[272,128]{1,0:T(8,128)(2,1)S(1)}, u32[]{:S(2)}, u32[]{:S(2)}) collective-permute-start(bf16[272,128]{1,0:T(8,128)(2,1)S(1)} %fusion.2), channel_id=1, source_target_pairs={{0,2},{2,0},{4,6},{6,4},{8,10},{10,8},{12,14},{14,12},{16,18},{18,... | collective-permute-start | bytes 208904 | tf_op jit(solution)/shard_map/ppermute | solution.py:424
  72.6 6.8 %collective-permute-start.9 = (bf16[272,128]{1,0:T(8,128)(2,1)S(1)}, bf16[272,128]{1,0:T(8,128)(2,1)S(1)}, u32[]{:S(2)}, u32[]{:S(2)}) collective-permute-start(bf16[272,128]{1,0:T(8,128)(2,1)S(1)} %fusion.2), channel_id=1, source_target_pairs={{0,16},{2,18},{4,20},{6,22},{8,24},{10,26},{12,28},{14,30},{16,0},... | collective-permute-start | bytes 208904 | tf_op jit(solution)/shard_map/ppermute | solution.py:424
  79.5 15.9 %collective-permute-start.11 = (bf16[272,128]{1,0:T(8,128)(2,1)S(1)}, bf16[272,128]{1,0:T(8,128)(2,1)S(1)}, u32[]{:S(2)}, u32[]{:S(2)}) collective-permute-start(bf16[272,128]{1,0:T(8,128)(2,1)S(1)} %add_convert_fusion.2), channel_id=1, source_target_pairs={{0,4},{2,6},{4,0},{6,2},{8,12},{10,14},{12,8},{14,10},{16,20},{18,... | collective-permute-start | bytes 208904 | tf_op jit(solution)/shard_map/ppermute | solution.py:424
  79.6 15.8 %collective-permute-start.12 = (bf16[272,128]{1,0:T(8,128)(2,1)S(1)}, bf16[272,128]{1,0:T(8,128)(2,1)S(1)}, u32[]{:S(2)}, u32[]{:S(2)}) collective-permute-start(bf16[272,128]{1,0:T(8,128)(2,1)S(1)} %add_convert_fusion.2), channel_id=1, source_target_pairs={{0,8},{2,10},{4,12},{6,14},{8,0},{10,2},{12,4},{14,6},{16,24},{18,... | collective-permute-start | bytes 208904 | tf_op jit(solution)/shard_map/ppermute | solution.py:424
  81.8 13.6 %collective-permute-start.13 = (bf16[272,128]{1,0:T(8,128)(2,1)S(1)}, bf16[272,128]{1,0:T(8,128)(2,1)S(1)}, u32[]{:S(2)}, u32[]{:S(2)}) collective-permute-start(bf16[272,128]{1,0:T(8,128)(2,1)S(1)} %add_convert_fusion.2), channel_id=1, source_target_pairs={{0,12},{2,14},{4,8},{6,10},{8,4},{10,6},{12,0},{14,2},{16,28},{18,... | collective-permute-start | bytes 208904 | tf_op jit(solution)/shard_map/ppermute | solution.py:424
  92.6 21.2 %collective-permute-start.19 = (bf16[8,192,128]{2,1,0:T(8,128)(2,1)S(1)}, bf16[8,192,128]{2,1,0:T(8,128)(2,1)S(1)}, u32[]{:S(2)}, u32[]{:S(2)}) collective-permute-start(bf16[8,192,128]{2,1,0:T(8,128)(2,1)S(1)} %get-tuple-element.70), channel_id=1, source_target_pairs={{0,16},{16,0},{1,17},{17,1},{2,18},{18,2},{3,19},{19,3},{4,20},{20... | collective-permute-start | bytes 1179656 | tf_op jit(solution)/shard_map/ppermute | solution.py:465
  95.4 15.3 %collective-permute-start.16 = (bf16[272,128]{1,0:T(8,128)(2,1)S(1)}, bf16[272,128]{1,0:T(8,128)(2,1)S(1)}, u32[]{:S(2)}, u32[]{:S(2)}) collective-permute-start(bf16[272,128]{1,0:T(8,128)(2,1)S(1)} %add_convert_fusion.1), channel_id=1, source_target_pairs={{0,64},{32,96},{64,0},{96,32},{128,192},{160,224},{192,128},{224,1... | collective-permute-start | bytes 208904 | tf_op jit(solution)/shard_map/ppermute | solution.py:424
  102.5 17.8 %collective-permute-start.20 = (bf16[8,96,128]{2,1,0:T(8,128)(2,1)S(1)}, bf16[8,96,128]{2,1,0:T(8,128)(2,1)S(1)}, u32[]{:S(2)}, u32[]{:S(2)}) collective-permute-start(bf16[8,96,128]{2,1,0:T(8,128)(2,1)S(1)} %get-tuple-element.77), channel_id=1, source_target_pairs={{0,1},{1,0},{2,3},{3,2},{4,5},{5,4},{6,7},{7,6},{8,9},{9,8},{10,11... | collective-permute-start | bytes 589832 | tf_op jit(solution)/shard_map/ppermute | solution.py:465
  107.2 6.4 %collective-permute-start.14 = (bf16[272,128]{1,0:T(8,128)(2,1)S(1)}, bf16[272,128]{1,0:T(8,128)(2,1)S(1)}, u32[]{:S(2)}, u32[]{:S(2)}) collective-permute-start(bf16[272,128]{1,0:T(8,128)(2,1)S(1)} %add_convert_fusion.1), channel_id=1, source_target_pairs={{0,192},{32,224},{64,128},{96,160},{128,64},{160,96},{192,0},{224,... | collective-permute-start | bytes 208904 | tf_op jit(solution)/shard_map/ppermute | solution.py:424
  107.8 5.9 %collective-permute-start.15 = (bf16[272,128]{1,0:T(8,128)(2,1)S(1)}, bf16[272,128]{1,0:T(8,128)(2,1)S(1)}, u32[]{:S(2)}, u32[]{:S(2)}) collective-permute-start(bf16[272,128]{1,0:T(8,128)(2,1)S(1)} %add_convert_fusion.1), channel_id=1, source_target_pairs={{0,128},{32,160},{64,192},{96,224},{128,0},{160,32},{192,64},{224,... | collective-permute-start | bytes 208904 | tf_op jit(solution)/shard_map/ppermute | solution.py:424
  123.6 7.3 %collective-permute-start.21 = (bf16[1088,128]{1,0:T(8,128)(2,1)S(1)}, bf16[1088,128]{1,0:T(8,128)(2,1)S(1)}, u32[]{:S(2)}, u32[]{:S(2)}) collective-permute-start(bf16[1088,128]{1,0:T(8,128)(2,1)S(1)} %pad_maximum_fusion.1), channel_id=1, source_target_pairs={{0,32},{32,0},{64,96},{96,64},{128,160},{160,128},{192,224},{224,1... | collective-permute-start | bytes 835592 | tf_op jit(solution)/shard_map/ppermute | solution.py:424
  123.9 22.8 %all-to-all-start.2 = ((bf16[8,288,128]{2,1,0:T(8,128)(2,1)}), bf16[8,288,128]{2,1,0:T(8,128)(2,1)S(1)}, u32[]{:S(2)}, u32[]{:S(2)}) async-start(bf16[8,288,128]{2,1,0:T(8,128)(2,1)} %shard_map.154), calls=%async_computation.2 | async-start | bytes 1179648 | tf_op jit(solution)/shard_map/all_to_all | solution.py:542
  (12 other events, 48.5 us)

commit v3 on v2

v3 whole, which is shorter than its diff:
```python
import functools

import jax
import jax.numpy as jnp
from jax import lax
from jax.experimental import pallas as pl
from jax.experimental.pallas import tpu as pltpu
from jax.sharding import Mesh, PartitionSpec as P

BF = jnp.bfloat16
F32 = jnp.float32
NT = (((1,), (1,)), ((), ()))
NN = (((1,), (0,)), ((), ()))
TN = (((0,), (0,)), ((), ()))
ROWS = 192
HALF = 96
HEADS = 8
HSIZE = 64
TAPS = 31
FREE = 60
WIDTH = 256
ALL = ("dp", "xh", "z", "core")
SEQ = ("xh", "z", "core")


def cost(micros):
    return pl.CostEstimate(flops=int(micros * 1.15e9), transcendentals=0, bytes_accessed=1 << 20)


def call(kernel, out_shape, micros, vmem, **kw):
    return pl.pallas_call(
        kernel,
        out_shape=out_shape,
        compiler_params=pltpu.CompilerParams(vmem_limit_bytes=vmem << 20),
        cost_estimate=cost(micros),
        **kw,
    )


def record_length(lengths_ref):
    return lengths_ref[lax.axis_index("dp")]


def sds(shape, dtype=BF):
    return jax.ShapeDtypeStruct(shape, dtype)


def rims(xl_ref, xf_ref, gl_ref, gf_ref, last_ref, first_ref):
    last_ref[0:32, :] = xl_ref[0]
    last_ref[32:48, :] = gl_ref[0]
    first_ref[0:32, :] = xf_ref[0]
    first_ref[32:48, :] = gf_ref[0]


def rims_call(x, g):
    rim = lambda n, at: pl.BlockSpec((1, n, 1024), lambda i: (0, at, 0))
    edge = pl.BlockSpec((48, 1024), lambda i: (0, 0))
    return call(
        rims,
        (sds((48, 1024)), sds((48, 1024))),
        1,
        FREE,
        grid=(1,),
        in_specs=[rim(32, 5), rim(32, 0), rim(16, 11), rim(16, 0)],
        out_specs=[edge, edge],
    )(x, x, g, g)


def conv_kernel(
    lengths_ref,
    x_ref,
    g_ref,
    lo_ref,
    hi_ref,
    w_ref,
    proj_ref,
    attn_ref,
    log_ref,
    q_ref,
    k_ref,
    v_ref,
    gs_ref,
    pk_ref,
    pay_ref,
    xs,
    gm,
    gp,
    out_acc,
    attn_t,
    tmp,
):
    step = pl.program_id(0)
    first_row = lax.axis_index(SEQ) * ROWS
    length = record_length(lengths_ref)

    @pl.when(step == 0)
    def _():
        out_acc[...] = jnp.zeros_like(out_acc)
        attn_t[...] = attn_ref[0].T

    for i in range(2):
        cols = slice(i * HSIZE, (i + 1) * HSIZE)
        h = pl.ds(2 * step + i, 1)
        pay_ref[h, 0:ROWS, 0:HSIZE] = k_ref[:, :, cols]
        pay_ref[h, 0:ROWS, HSIZE:128] = v_ref[:, :, cols]
        q = q_ref[:, :, cols] * BF(0.125)
        pay_ref[h, ROWS : ROWS + HALF, 0:HSIZE] = q[:, :HALF]
        pay_ref[h, ROWS : ROWS + HALF, HSIZE:128] = q[:, HALF:]

    def mask(rows, offset):
        at = first_row + offset + lax.broadcasted_iota(jnp.int32, (rows, 128), 0)
        return jnp.where((at >= 0) & (at < length), 1.0, 0.0).astype(F32)

    mask_x = mask(256, -32)
    mask_g = mask(224, -16)
    for half in range(WIDTH // 128):
        cols = slice(half * 128, half * 128 + 128)
        xs[0:32, :] = lo_ref[0:32, cols].astype(F32) * mask_x[0:32]
        xs[32:224, :] = x_ref[0, :, cols].astype(F32) * mask_x[32:224]
        xs[224:256, :] = hi_ref[0:32, cols].astype(F32) * mask_x[224:256]
        gm[0:16, :] = lo_ref[32:48, cols].astype(F32) * mask_g[0:16]
        gm[16:208, :] = g_ref[0, :, cols].astype(F32) * mask_g[16:208]
        gm[208:224, :] = hi_ref[32:48, cols].astype(F32) * mask_g[208:224]
        pre = jnp.zeros((224, 128), F32)
        for j in range(TAPS):
            pre = pre + w_ref[j : j + 1, cols] * xs[1 + j : 225 + j, :]
        s = jax.nn.sigmoid(pre)
        gp[...] = (gm[...] * s * (1.0 + pre * (1.0 - s))).astype(BF).astype(F32)
        back = jnp.zeros((ROWS, 128), F32)
        for j in range(TAPS):
            back = back + w_ref[j : j + 1, cols] * gp[31 - j : 223 - j, :]
        gs = (gm[16:208, :] + mask_g[16:208] * back).astype(BF)
        gs_ref[0, :, cols] = gs
        out_acc[...] += lax.dot_general(
            gs, proj_ref[:, cols], NT, preferred_element_type=F32
        )
        pk_ref[half, 0:512, :] = lax.dot_general(
            attn_t[...], gs, NN, preferred_element_type=F32
        ).astype(BF)
        own = gp[16:208, :]
        rows = [
            jnp.sum(xs[17 + j : 209 + j, :] * own, axis=0, keepdims=True) for j in range(TAPS)
        ]
        rows.append(jnp.zeros((1, 128), F32))
        pk_ref[half, 512:544, :] = jnp.concatenate(rows, axis=0).astype(BF)

    @pl.when(step == pl.num_programs(0) - 1)
    def _():
        grad = out_acc[...].astype(BF)
        tmp[0:ROWS, :] = grad.astype(F32) * attn_ref[0].astype(F32)
        tmp[ROWS:256, :] = jnp.zeros((256 - ROWS, 512), F32)
        turned = tmp[...].T
        logs = jnp.concatenate(
            [log_ref[...].astype(F32), jnp.zeros((HEADS, 256 - ROWS), F32)], axis=1
        )
        for h in range(HEADS):
            delta = jnp.sum(turned[h * HSIZE : (h + 1) * HSIZE], axis=0, keepdims=True)
            log_row = logs[h : h + 1]
            part = grad[:, h * HSIZE : (h + 1) * HSIZE]
            pay_ref[h, 288:384, 0:HSIZE] = part[:HALF]
            pay_ref[h, 288:384, HSIZE:128] = part[HALF:]
            pay_ref[h, 384:400, :] = jnp.concatenate(
                [
                    delta[:, 0:128],
                    delta[:, 128:256],
                    log_row[:, 0:128],
                    log_row[:, 128:256],
                    jnp.zeros((12, 128), F32),
                ],
                axis=0,
            ).astype(BF)


def conv_call(lengths, x, g, lo, hi, w, proj, attn, log, q, k, v):
    chunk = lambda i, *_: (0, 0, i)
    flat = lambda i, *_: (0, i)
    full3 = lambda i, *_: (0, 0, 0)
    full2 = lambda i, *_: (0, 0)
    return pl.pallas_call(
        conv_kernel,
        out_shape=(
            sds((1, ROWS, 1024)),
            sds((8, 544, 128)),
            sds((HEADS, 400, 128)),
        ),
        grid_spec=pltpu.PrefetchScalarGridSpec(
            num_scalar_prefetch=1,
            grid=(1024 // WIDTH,),
            in_specs=[
                pl.BlockSpec((1, ROWS, WIDTH), chunk),
                pl.BlockSpec((1, ROWS, WIDTH), chunk),
                pl.BlockSpec((48, WIDTH), flat),
                pl.BlockSpec((48, WIDTH), flat),
                pl.BlockSpec((TAPS, WIDTH), flat),
                pl.BlockSpec((512, WIDTH), flat),
                pl.BlockSpec((1, ROWS, 512), full3),
                pl.BlockSpec((HEADS, ROWS), full2),
                pl.BlockSpec((1, ROWS, 128), chunk),
                pl.BlockSpec((1, ROWS, 128), chunk),
                pl.BlockSpec((1, ROWS, 128), chunk),
            ],
            out_specs=[
                pl.BlockSpec((1, ROWS, WIDTH), chunk),
                pl.BlockSpec((WIDTH // 128, 544, 128), lambda i, *_: (i, 0, 0)),
                pl.BlockSpec((HEADS, 400, 128), full3),
            ],
            scratch_shapes=[
                pltpu.VMEM((256, 128), F32),
                pltpu.VMEM((224, 128), F32),
                pltpu.VMEM((224, 128), F32),
                pltpu.VMEM((ROWS, 512), F32),
                pltpu.VMEM((512, ROWS), BF),
                pltpu.VMEM((256, 512), F32),
            ],
        ),
        compiler_params=pltpu.CompilerParams(vmem_limit_bytes=FREE << 20),
        cost_estimate=cost(11),
    )(lengths, x, g, lo, hi, w, proj, attn, log, q, k, v)


CHUNK = HEADS * ROWS
BU = 512


def key_rows(part, z, lanes):
    xh = lax.axis_index("xh")
    half = 1 - xh if part == 0 else xh
    row = ((half * 8 + z) * 2 + lax.axis_index("core")) * ROWS
    return row + lax.broadcasted_iota(jnp.int32, (ROWS, lanes), 0)


def unpack_rows(x, z, dst):
    left, right = x[:, 0:HSIZE], x[:, HSIZE:128]
    at, end = z * 128, 1024 + z * 64
    dst[at : at + 96, :] = left
    dst[at + 96 : at + 128, :] = right[0:32]
    dst[end : end + 64, :] = right[32:96]


def turn_rows(dqt, dq, put):
    for b in range(3):
        dq[b * 512 : b * 512 + 512, :] = dqt[:, b * 512 : b * 512 + 512].T
    for z in range(8):
        at, end = z * 128, 1024 + z * 64
        put(z, slice(0, 96), slice(0, HSIZE), dq[at : at + 96, :])
        put(z, slice(0, 32), slice(HSIZE, 128), dq[at + 96 : at + 128, :])
        put(z, slice(32, 96), slice(HSIZE, 128), dq[end : end + 64, :])


def prep_queries(x_ref, q_ref, do_ref, st_ref):
    lane = lax.broadcasted_iota(jnp.int32, (1, 128), 1)
    stats = []
    for z in range(8):
        unpack_rows(x_ref[z, 0:HALF, :], z, q_ref)
        unpack_rows(x_ref[z, HALF:ROWS, :], z, do_ref)
        st = x_ref[z, ROWS : ROWS + 16, :].astype(F32)
        st_ref[0:1, z * 128 : z * 128 + 128] = st[0:1]
        st_ref[1:2, z * 128 : z * 128 + 128] = st[2:3]
        stats.append(st)
    for m in range(4):
        a, b = stats[2 * m], stats[2 * m + 1]
        at = 1024 + m * 128
        for row in range(2):
            src = 2 * row + 1
            st_ref[row : row + 1, at : at + 128] = jnp.where(
                lane < 64, a[src : src + 1], pltpu.roll(b[src : src + 1], 64, 1)
            )


def prep_keys(part, lengths_ref, x_ref, k_ref, v_ref, kt_ref, kf):
    length = record_length(lengths_ref)
    for z in range(8):
        kv = x_ref[z]
        rows = slice(z * ROWS, z * ROWS + ROWS)
        k_ref[rows, :] = kv[:, 0:HSIZE]
        v_ref[rows, :] = kv[:, HSIZE:128]
        kf[rows, :] = jnp.where(key_rows(part, z, 128) < length, kv.astype(F32) * 0.125, 0.0)
    for b in range(3):
        turned = kf[b * 512 : b * 512 + 512, :].T
        kt_ref[:, b * 512 : b * 512 + 512] = turned[0:HSIZE].astype(BF)


def score_tile(q, do, st, k, v, kt, dqt, dks, dvs):
    def key_block(ui, _):
        u0 = pl.multiple_of(ui * BU, BU)
        kb = k[pl.ds(u0, BU), :]
        vb = v[pl.ds(u0, BU), :]
        ktb = kt[:, pl.ds(u0, BU)]
        qb, dob = q[...], do[...]
        s = lax.dot_general(kb, qb, NT, preferred_element_type=F32)
        p = jnp.exp(s - st[1:2, :])
        dp = lax.dot_general(vb, dob, NT, preferred_element_type=F32)
        ds = (p * (dp - st[0:1, :])).astype(BF)
        dvs[pl.ds(u0, BU), :] += lax.dot_general(p.astype(BF), dob, NN, preferred_element_type=F32)
        dks[pl.ds(u0, BU), :] += lax.dot_general(ds, qb, NN, preferred_element_type=F32)
        dqt[...] += lax.dot_general(ktb, ds, NN, preferred_element_type=F32)
        return 0

    lax.fori_loop(0, CHUNK // BU, key_block, 0)


def tile_1(q, do, st, k, v, kt, dqt, dks, dvs):
    for ref in (dqt, dks, dvs):
        ref[...] = jnp.zeros_like(ref)
    score_tile(q, do, st, k, v, kt, dqt, dks, dvs)


def tile_2(q, do, st, k, v, kt, dq_ref, dqt, dks, dvs):
    dqt[...] = dq_ref[...]
    dks[...] = jnp.zeros_like(dks)
    dvs[...] = jnp.zeros_like(dvs)
    score_tile(q, do, st, k, v, kt, dqt, dks, dvs)


def tile_3(lengths_ref, q, do, st, k, v, kt, dk_ref, dv_ref, dkv_ref, dqt, dks, dvs):
    dqt[...] = jnp.zeros_like(dqt)
    dks[...] = dk_ref[...]
    dvs[...] = dv_ref[...]
    score_tile(q, do, st, k, v, kt, dqt, dks, dvs)
    length = record_length(lengths_ref)
    for z in range(8):
        keep = key_rows(0, z, HSIZE) < length
        rows = slice(z * ROWS, z * ROWS + ROWS)
        dkv_ref[z, :, 0:HSIZE] = jnp.where(keep, dks[rows, :], 0.0).astype(BF)
        dkv_ref[z, :, HSIZE:128] = jnp.where(keep, dvs[rows, :], 0.0).astype(BF)


def tile_4(q, do, st, k, v, kt, dq_in, dk_ref, dv_ref, dq_ref, dks, dvs, dqt, dq):
    dqt[...] = dq_in[...]
    dks[...] = dk_ref[...]
    dvs[...] = dv_ref[...]
    score_tile(q, do, st, k, v, kt, dqt, dks, dvs)

    def put(z, rows, cols, value):
        dq_ref[z, rows, cols] = value.astype(BF)

    turn_rows(dqt, dq, put)


def tile_call(body, lengths, args, outs, scratch=()):
    whole = lambda x: pl.BlockSpec(x.shape, lambda *_: (0,) * len(x.shape))
    specs = [whole(a) for a in args]
    if lengths is not None:
        specs.insert(0, pl.BlockSpec(memory_space=pltpu.SMEM))
        args = (lengths,) + args
    return call(
        body,
        outs,
        7,
        40,
        grid=(1,),
        in_specs=specs,
        out_specs=tuple(whole(o) for o in outs),
        scratch_shapes=scratch,
    )(*args)


def combine(lengths_ref, dk_ref, dv_ref, got_ref, dqt_ref, dqgot_ref, o_ref, dq):
    length = record_length(lengths_ref)
    for z in range(8):
        keep = key_rows(1, z, HSIZE) < length
        rows = slice(z * ROWS, z * ROWS + ROWS)
        got = got_ref[z].astype(F32)
        dk = jnp.where(keep, dk_ref[rows, :], 0.0) + got[:, 0:HSIZE]
        dv = jnp.where(keep, dv_ref[rows, :], 0.0) + got[:, HSIZE:128]
        o_ref[z, 0:ROWS, 0:HSIZE] = dk.astype(BF)
        o_ref[z, 0:ROWS, HSIZE:128] = dv.astype(BF)

    def put(z, rows, cols, value):
        to = slice(ROWS + rows.start, ROWS + rows.stop)
        o_ref[z, to, cols] = (value + dqgot_ref[z, rows, cols].astype(F32)).astype(BF)

    turn_rows(dqt_ref, dq, put)


def unpack_final(x_ref, q_ref, k_ref, v_ref):
    for h in range(HEADS):
        cols = slice(h * HSIZE, (h + 1) * HSIZE)
        k_ref[0, :, cols] = x_ref[h, 0:ROWS, 0:HSIZE]
        v_ref[0, :, cols] = x_ref[h, 0:ROWS, HSIZE:128]
        q_ref[0, 0:HALF, cols] = x_ref[h, ROWS : ROWS + HALF, 0:HSIZE]
        q_ref[0, HALF:ROWS, cols] = x_ref[h, ROWS : ROWS + HALF, HSIZE:128]


def finish_sums(lengths_ref, own_ref, got_ref, proj_ref, taps_ref):
    total = lengths_ref[0]
    for r in range(1, 8):
        total = total + lengths_ref[r]
    scale = lax.rsqrt(jnp.full((1, 128), total, jnp.int32).astype(F32))
    core = lax.axis_index("core")
    for c in range(8):
        cols = slice(c * 128, c * 128 + 128)
        own, got = own_ref[c % 4].astype(F32), got_ref[c % 4].astype(F32)
        x = jnp.where(core == c // 4, own, got) * scale
        proj_ref[:, cols] = x[0:512]
        taps_ref[:, cols] = x[512:543]


def flip(x, axis, mask, size):
    return lax.ppermute(x, axis, [(i, i ^ mask) for i in range(size)])


def add(*terms):
    pair = [a.astype(F32) + b.astype(F32) for a, b in zip(terms[::2], terms[1::2])]
    return (pair[0] if len(pair) == 1 else pair[0] + pair[1]).astype(BF)


def reduce_dp(x, shift, count):
    me = (lax.axis_index("dp") >> shift) & (count - 1)
    pieces = x.reshape(count, x.shape[0] // count, 128)
    piece = lambda i: lax.dynamic_index_in_dim(pieces, i, 0, keepdims=False)
    got = [flip(piece(me ^ d), "dp", d << shift, 8) for d in range(1, count)]
    return add(piece(me), *got)


def sum_four(x, low, high, beside):
    got = [flip(x, ("xh", "z"), mask, 16) for mask in (low, high, low | high)]
    return add(after(x, beside), *got)


def gather_y(x, beside):
    y = lax.axis_index("dp") >> 1
    odd, upper = (y & 1) == 1, (y & 2) == 2
    b, c, d = [flip(x, "dp", m << 1, 8) for m in (1, 2, 3)]
    a = after(x, beside)
    low = jnp.concatenate([jnp.where(odd, b, a), jnp.where(odd, a, b)], axis=0)
    high = jnp.concatenate([jnp.where(odd, d, c), jnp.where(odd, c, d)], axis=0)
    return jnp.concatenate([jnp.where(upper, high, low), jnp.where(upper, low, high)], axis=0)


def gather_x(x, beside):
    odd = (lax.axis_index("dp") & 1) == 1
    got = flip(x, "dp", 1, 8)
    x = after(x, beside)
    return jnp.concatenate([jnp.where(odd, got, x), jnp.where(odd, x, got)], axis=0)


def after(x, *first):
    return lax.optimization_barrier((x,) + first)[0]


def swap(x, axis):
    return lax.ppermute(x, axis, [(0, 1), (1, 0)])


def shards(query, key, value, attn, log, lengths, x, g, proj, taps):
    smem = pl.BlockSpec(memory_space=pltpu.SMEM)
    vmem = pl.BlockSpec(memory_space=pltpu.VMEM)
    up = [(i, i + 1) for i in range(31)]
    down = [(i + 1, i) for i in range(31)]
    last, first = rims_call(x, g)
    lo = lax.ppermute(last, SEQ, up)
    hi = lax.ppermute(first, SEQ, down)
    grad_state, sums, pay = conv_call(
        lengths, x, g, lo, hi, taps, proj, attn, log[0].T, query, key, value
    )
    pay = lax.all_to_all(pay, "z", 0, 0, tiled=True)

    core = lax.axis_index("core")
    sums = sums.reshape(2, 2176, 128)
    send = lax.dynamic_index_in_dim(sums, 1 - core, 0, keepdims=False)
    keep = lax.dynamic_index_in_dim(sums, core, 0, keepdims=False)
    sums = add(keep, swap(send, "core"))
    sums = reduce_dp(sums, 0, 2)
    sums = reduce_dp(sums, 1, 4)

    queries, keys = pay[:, ROWS:], pay[:, :ROWS]
    core_queries, other_keys = swap(queries, "core"), swap(keys, "xh")

    half = sds((CHUNK, HSIZE))

    def prepared_queries(x):
        return call(prep_queries, (half, half, sds((8, CHUNK), F32)), 1, 8)(x)

    def prepared_keys(part, x):
        return call(
            functools.partial(prep_keys, part),
            (half, half, sds((HSIZE, CHUNK))),
            1,
            8,
            in_specs=[smem, vmem],
            scratch_shapes=[pltpu.VMEM((CHUNK, 128), F32)],
        )(lengths, x)

    qo = prepared_queries(queries)
    ko = prepared_keys(1, keys)
    grad = sds((CHUNK, HSIZE), F32)
    turned = sds((HSIZE, CHUNK), F32)
    fgrad = pltpu.VMEM((CHUNK, HSIZE), F32)
    fturned = pltpu.VMEM((HSIZE, CHUNK), F32)
    dqo, dk, dv = tile_call(tile_1, None, qo + ko, (turned, grad, grad))
    sums = sum_four(sums, 1, 8, dk)

    kx = prepared_keys(0, other_keys)
    dqo = after(dqo, sums)
    dqo, dkx, dvx = tile_call(tile_2, None, qo + kx + (dqo,), (turned, grad, grad))
    sums = sum_four(sums, 2, 4, dvx)

    qc = prepared_queries(core_queries)
    dkx = after(dkx, sums)
    dkv_other, dqc = tile_call(
        tile_3, lengths, qc + kx + (dkx, dvx), (sds((HEADS, ROWS, 128)), turned), [fgrad, fgrad]
    )
    dkv_got = swap(dkv_other, "xh")
    sums = gather_y(sums, dqc)
    dqc = after(dqc, sums)
    dq_core, dk, dv = tile_call(
        tile_4,
        None,
        qc + ko + (dqc, dk, dv),
        (sds((8, HALF, 128)), grad, grad),
        [fturned, fgrad],
    )
    dq_got = swap(dq_core, "core")
    sums = gather_x(sums, dk)
    back = call(
        combine,
        sds((HEADS, ROWS + HALF, 128)),
        2,
        16,
        in_specs=[smem] + [vmem] * 5,
        scratch_shapes=[fgrad],
    )(lengths, dk, dv, dkv_got, dqo, dq_got)

    back = lax.all_to_all(back, "z", 0, 0, tiled=True)
    sums = sums.reshape(4, 544, 128)
    grad_proj, grad_taps = call(
        finish_sums,
        (sds((512, 1024), F32), sds((TAPS, 1024), F32)),
        2,
        8,
        in_specs=[smem, vmem, vmem],
    )(lengths, sums, swap(sums, "core"))
    grad_q, grad_k, grad_v = call(unpack_final, (sds((1, ROWS, 512)),) * 3, 2, 8)(back)
    return grad_q, grad_k, grad_v, grad_state, grad_proj, grad_taps


def solution(mesh):
    inner = Mesh(mesh.devices.reshape(8, 2, 8, 2), ALL)
    rows = P("dp", SEQ, None)
    in_specs = (rows,) * 5 + (P(), rows, rows, P(), P())
    out_specs = (rows,) * 4 + (P(), P())
    return jax.shard_map(
        shards, mesh=inner, in_specs=in_specs, out_specs=out_specs, check_vma=False
    )
```

time: 148 us -> 141 us (0.953)
  starting transfers between devices: 56.6 us -> 49.4 us
  waiting for transfers between devices: 34.6 us -> 37.8 us
  local copies, waits for them, and re-layouts: 4.44 us -> 1.95 us
    ppermute x7 -> x6, starting transfers between devices: 16.3 us -> 8.21 us  [swap(): return lax.ppermute(x, axis, [(0, 1), (1, 0)])]
    ppermute x14, waiting for transfers between devices: 12.8 us -> 18.1 us  [flip(): return lax.ppermute(x, axis, [(i, i ^ mask) for i in range(size)])]
    ppermute x7 -> x6, waiting for transfers between devices: 6.52 us -> 1.6 us  [swap(): return lax.ppermute(x, axis, [(0, 1), (1, 0)])]
    ppermute x1, waiting for transfers between devices: 0.01 us -> 4.19 us  [shards(): hi = lax.ppermute(first, SEQ, down)]
    unnamed x20 -> x8, local copies, waits for them, and re-layouts: 3.68 us -> 0.65 us
    all_to_all x2 -> x1, waiting for transfers between devices: 5.24 us -> 2.73 us  [shards(): pay = lax.all_to_all(pay, 'z', 0, 0, tiled=True)]
    all_to_all x1, starting transfers between devices: 3.54 us -> 6.03 us  [shards(): back = lax.all_to_all(back, 'z', 0, 0, tiled=True)]
    all_to_all x2 -> x1, starting transfers between devices: 10.7 us -> 8.4 us  [shards(): pay = lax.all_to_all(pay, 'z', 0, 0, tiled=True)]
  transfers between devices with their start and end apart: 26 -> 24, of which waited for: 10 -> 8; matrix products, arithmetic and copies ran while one was open for 1% -> 0% of each run, Pallas kernels for 29% -> 22%
where the time goes in v3:
time: 141 us; the launch traced here: 140 us
  starting transfers between devices  49.4 us (35%)
  Pallas kernels  49.2 us (35%)
  waiting for transfers between devices  37.8 us (27%)
  local copies, waits for them, and re-layouts  1.95 us (1%)
    pallas_call x4, Pallas kernels, tile_call(): call(body, outs, 7, 40, grid=(1,), in_specs=specs, out_specs=tuple((whole...  26.5 us
    ppermute x14, starting transfers between devices, flip(): return lax.ppermute(x, axis, [(i, i ^ mask) for i in range(size)])  20 us
    ppermute x14, waiting for transfers between devices, flip(): return lax.ppermute(x, axis, [(i, i ^ mask) for i in range(size)])  18.1 us
    pallas_call x1, Pallas kernels, conv_call(): pl.pallas_call(conv_kernel, out_shape=(sds((1, ROWS, 1024)), sds((8, 544,...  11.9 us
    all_to_all x1, waiting for transfers between devices, shards(): back = lax.all_to_all(back, 'z', 0, 0, tiled=True)  11.2 us
    all_to_all x1, starting transfers between devices, shards(): pay = lax.all_to_all(pay, 'z', 0, 0, tiled=True)  8.4 us
    ppermute x6, starting transfers between devices, swap(): return lax.ppermute(x, axis, [(0, 1), (1, 0)])  8.21 us
    all_to_all x1, starting transfers between devices, shards(): back = lax.all_to_all(back, 'z', 0, 0, tiled=True)  6.03 us
  transfers between devices with their start and end apart: 24, of which 8 were waited for; matrix products, arithmetic and copies ran while one was open for 0% of the time, Pallas kernels for 22%

profile of v3, /device:TPU:1, one launch (start us, length us, event | category | flops | bytes accessed | tf_op | source)
XLA Modules:
  0.0 139.8 jit_solution(226546282366521693)
XLA Ops:
  2.2 4.9 %collective-permute-start = (bf16[48,1024]{1,0:T(8,128)(2,1)}, bf16[48,1024]{1,0:T(8,128)(2,1)S(1)}, u32[]{:S(2)}, u32[]{:S(2)}) collective-permute-start(bf16[48,1024]{1,0:T(8,128)(2,1)} %get-tuple-element.46), channel_id=1, source_target_pairs={{0,1},{1,2},{2,3},{3,4},{4,5},{5,6},{6,7},{7,8},{8,9},{9,10},{10,1... | collective-permute-start | bytes 294920 | tf_op jit(solution)/shard_map/ppermute | solution.py:452
  9.1 4.2 %collective-permute-done.1.hi_ref = bf16[48,1024]{1,0:T(8,128)(2,1)S(1)} collective-permute-done((bf16[48,1024]{1,0:T(8,128)(2,1)}, bf16[48,1024]{1,0:T(8,128)(2,1)S(1)}, u32[]{:S(2)}, u32[]{:S(2)}) %collective-permute-start.1) | collective-permute-done | bytes 98336 | tf_op jit(solution)/shard_map/ppermute | solution.py:453
  13.9 11.9 %shard_map.146 = (bf16[1,192,1024]{2,1,0:T(8,128)(2,1)}, bf16[8,544,128]{2,1,0:T(8,128)(2,1)}, bf16[8,400,128]{2,1,0:T(8,128)(2,1)}) custom-call(s32[8]{0:T(128)} %lengths_ref.11, bf16[1,192,1024]{2,1,0:T(8,128)(2,1)} %x_ref.1, bf16[1,192,1024]{2,1,0:T(8,128)(2,1)} %g_ref.1, bf16[48,1024]{1,0:T(8,128)(2,1)} %copy-done.2, bf16[48,1024]{1,0:T(8,128)(2,1)} %copy-done.3, ...), custom_call_target="tpu_custom_call" | custom-call | flops 12650000384 | bytes 1048576 | tf_op jit(solution)/shard_map/pallas_call | solution.py:179
  27.2 8.4 %all-to-all-start = ((bf16[8,400,128]{2,1,0:T(8,128)(2,1)}), bf16[8,400,128]{2,1,0:T(8,128)(2,1)S(1)}, u32[]{:S(2)}, u32[]{:S(2)}) async-start(bf16[8,400,128]{2,1,0:T(8,128)(2,1)} %get-tuple-element.48), calls=%async_computation | async-start | bytes 1638400 | tf_op jit(solution)/shard_map/all_to_all | solution.py:457
  37.0 6.3 %collective-permute-done.5 = bf16[1088,128]{1,0:T(8,128)(2,1)S(1)} collective-permute-done((bf16[1088,128]{1,0:T(8,128)(2,1)S(1)}, bf16[1088,128]{1,0:T(8,128)(2,1)S(1)}, u32[]{:S(2)}, u32[]{:S(2)}) %collective-permute-start.5) | collective-permute-done | bytes 278560 | tf_op jit(solution)/shard_map/ppermute | solution.py:400
  44.8 2.6 %collective-permute-start.7 = (bf16[272,128]{1,0:T(8,128)(2,1)S(1)}, bf16[272,128]{1,0:T(8,128)(2,1)S(1)}, u32[]{:S(2)}, u32[]{:S(2)}) collective-permute-start(bf16[272,128]{1,0:T(8,128)(2,1)S(1)} %get-tuple-element.92), channel_id=1, source_target_pairs={{0,128},{32,160},{64,192},{96,224},{128,0},{160,32},{192,64},{224,... | collective-permute-start | bytes 208904 | tf_op jit(solution)/shard_map/ppermute | solution.py:400
  47.4 2.7 %collective-permute-done.7 = bf16[272,128]{1,0:T(8,128)(2,1)S(1)} collective-permute-done((bf16[272,128]{1,0:T(8,128)(2,1)S(1)}, bf16[272,128]{1,0:T(8,128)(2,1)S(1)}, u32[]{:S(2)}, u32[]{:S(2)}) %collective-permute-start.7) | collective-permute-done | bytes 69664 | tf_op jit(solution)/shard_map/ppermute | solution.py:400
  50.2 2.7 %collective-permute-done.8 = bf16[272,128]{1,0:T(8,128)(2,1)S(1)} collective-permute-done((bf16[272,128]{1,0:T(8,128)(2,1)S(1)}, bf16[272,128]{1,0:T(8,128)(2,1)S(1)}, u32[]{:S(2)}, u32[]{:S(2)}) %collective-permute-start.8) | collective-permute-done | bytes 69664 | tf_op jit(solution)/shard_map/ppermute | solution.py:400
  52.9 2.5 %collective-permute-start.10 = (bf16[272,128]{1,0:T(8,128)(2,1)S(1)}, bf16[272,128]{1,0:T(8,128)(2,1)S(1)}, u32[]{:S(2)}, u32[]{:S(2)}) collective-permute-start(bf16[272,128]{1,0:T(8,128)(2,1)S(1)} %fusion.3), channel_id=1, source_target_pairs={{0,16},{2,18},{4,20},{6,22},{8,24},{10,26},{12,28},{14,30},{16,0},... | collective-permute-start | bytes 208904 | tf_op jit(solution)/shard_map/ppermute | solution.py:400
  57.1 2.7 %all-to-all-done = bf16[8,400,128]{2,1,0:T(8,128)(2,1)S(1)} async-done(((bf16[8,400,128]{2,1,0:T(8,128)(2,1)}), bf16[8,400,128]{2,1,0:T(8,128)(2,1)S(1)}, u32[]{:S(2)}, u32[]{:S(2)}) %all-to-all-start) | async-done | bytes 819232 | tf_op jit(solution)/shard_map/all_to_all | solution.py:457
  60.8 2.5 %collective-permute-start.3 = (bf16[8,192,128]{2,1,0:T(8,128)(2,1)S(1)}, bf16[8,192,128]{2,1,0:T(8,128)(2,1)S(1)}, u32[]{:S(2)}, u32[]{:S(2)}) collective-permute-start(bf16[8,192,128]{2,1,0:T(8,128)(2,1)S(1)} %slice.9.x_ref), channel_id=1, source_target_pairs={{0,16},{16,0},{1,17},{17,1},{2,18},{18,2},{3,19},{19,3},{4,20},{20... | collective-permute-start | bytes 1179656 | tf_op jit(solution)/shard_map/ppermute | solution.py:443
  63.6 6.3 %shard_map.151 = (f32[64,1536]{1,0:T(8,128)S(1)}, f32[1536,64]{1,0:T(8,128)S(1)}, f32[1536,64]{1,0:T(8,128)S(1)}) custom-call(bf16[1536,64]{1,0:T(8,128)(2,1)S(1)} %get-tuple-element.58.q, bf16[1536,64]{1,0:T(8,128)(2,1)S(1)} %get-tuple-element.59.do, f32[8,1536]{1,0:T(8,128)S(1)} %get-tuple-element.60.st, bf16[1536,64]{1,0:T(8,128)(2,1)S(1)} %get-tuple-element.52.k, ...), custom_call_target="tpu_custom_call" | custom-call | flops 8049999872 | bytes 1048576 | tf_op jit(solution)/shard_map/pallas_call | solution.py:346
  70.1 2.6 %collective-permute-start.13 = (bf16[272,128]{1,0:T(8,128)(2,1)S(1)}, bf16[272,128]{1,0:T(8,128)(2,1)S(1)}, u32[]{:S(2)}, u32[]{:S(2)}) collective-permute-start(bf16[272,128]{1,0:T(8,128)(2,1)S(1)} %add_convert_fusion.1), channel_id=1, source_target_pairs={{0,8},{2,10},{4,12},{6,14},{8,0},{10,2},{12,4},{14,6},{16,24},{18,... | collective-permute-start | bytes 208904 | tf_op jit(solution)/shard_map/ppermute | solution.py:400
  72.7 3.1 %collective-permute-start.14 = (bf16[272,128]{1,0:T(8,128)(2,1)S(1)}, bf16[272,128]{1,0:T(8,128)(2,1)S(1)}, u32[]{:S(2)}, u32[]{:S(2)}) collective-permute-start(bf16[272,128]{1,0:T(8,128)(2,1)S(1)} %add_convert_fusion.1), channel_id=1, source_target_pairs={{0,12},{2,14},{4,8},{6,10},{8,4},{10,6},{12,0},{14,2},{16,28},{18,... | collective-permute-start | bytes 208904 | tf_op jit(solution)/shard_map/ppermute | solution.py:400
  78.3 6.3 %shard_map.152 = (f32[64,1536]{1,0:T(8,128)S(1)}, f32[1536,64]{1,0:T(8,128)S(1)}, f32[1536,64]{1,0:T(8,128)S(1)}) custom-call(bf16[1536,64]{1,0:T(8,128)(2,1)S(1)} %get-tuple-element.58.q, bf16[1536,64]{1,0:T(8,128)(2,1)S(1)} %get-tuple-element.59.do, f32[8,1536]{1,0:T(8,128)S(1)} %get-tuple-element.60.st, bf16[1536,64]{1,0:T(8,128)(2,1)S(1)} %get-tuple-element.55.k, ...), custom_call_target="tpu_custom_call" | custom-call | flops 8049999872 | bytes 1048576 | tf_op jit(solution)/shard_map/pallas_call | solution.py:346
  84.7 2.9 %collective-permute-start.15 = (bf16[272,128]{1,0:T(8,128)(2,1)S(1)}, bf16[272,128]{1,0:T(8,128)(2,1)S(1)}, u32[]{:S(2)}, u32[]{:S(2)}) collective-permute-start(bf16[272,128]{1,0:T(8,128)(2,1)S(1)} %add_convert_fusion), channel_id=1, source_target_pairs={{0,192},{32,224},{64,128},{96,160},{128,64},{160,96},{192,0},{224,... | collective-permute-start | bytes 208904 | tf_op jit(solution)/shard_map/ppermute | solution.py:400
  88.6 7.1 %shard_map.153 = (bf16[8,192,128]{2,1,0:T(8,128)(2,1)S(1)}, f32[64,1536]{1,0:T(8,128)S(1)}) custom-call(s32[8]{0:T(128)S(1)} %copy-done, bf16[1536,64]{1,0:T(8,128)(2,1)S(1)} %get-tuple-element.49.q, bf16[1536,64]{1,0:T(8,128)(2,1)S(1)} %get-tuple-element.50.do, f32[8,1536]{1,0:T(8,128)S(1)} %get-tuple-element.51.st, ...), custom_call_target="tpu_custom_call" | custom-call | flops 8049999872 | bytes 1048576 | tf_op jit(solution)/shard_map/pallas_call | solution.py:346
  97.7 6.8 %shard_map.154 = (bf16[8,96,128]{2,1,0:T(8,128)(2,1)S(1)}, f32[1536,64]{1,0:T(8,128)S(1)}, f32[1536,64]{1,0:T(8,128)S(1)}) custom-call(bf16[1536,64]{1,0:T(8,128)(2,1)S(1)} %get-tuple-element.49.q, bf16[1536,64]{1,0:T(8,128)(2,1)S(1)} %get-tuple-element.50.do, f32[8,1536]{1,0:T(8,128)S(1)} %get-tuple-element.51.st, ...), custom_call_target="tpu_custom_call" | custom-call | flops 8049999872 | bytes 1048576 | tf_op jit(solution)/shard_map/pallas_call | solution.py:346
  105.7 6.3 %collective-permute-done.20 = bf16[1088,128]{1,0:T(8,128)(2,1)S(1)} collective-permute-done((bf16[1088,128]{1,0:T(8,128)(2,1)S(1)}, bf16[1088,128]{1,0:T(8,128)(2,1)S(1)}, u32[]{:S(2)}, u32[]{:S(2)}) %collective-permute-start.20) | collective-permute-done | bytes 278560 | tf_op jit(solution)/shard_map/ppermute | solution.py:400
  112.1 3.3 %shard_map.155 = bf16[8,288,128]{2,1,0:T(8,128)(2,1)} custom-call(s32[8]{0:T(128)S(1)} %copy-done, f32[1536,64]{1,0:T(8,128)S(1)} %get-tuple-element.74.dk_ref, f32[1536,64]{1,0:T(8,128)S(1)} %get-tuple-element.75.dv_ref, bf16[8,192,128]{2,1,0:T(8,128)(2,1)S(1)} %collective-permute-done.18.got_ref, f32[64,1536]{1,0:T(8,128)S(1)} %get-tuple-element.77.dqt_ref, ...), custom_call_target="tpu_custom_call" | custom-call | flops 2300000000 | bytes 1048576 | tf_op jit(solution)/shard_map/pallas_call | solution.py:516
  115.4 6.0 %all-to-all-start.1 = ((bf16[8,288,128]{2,1,0:T(8,128)(2,1)}), bf16[8,288,128]{2,1,0:T(8,128)(2,1)S(1)}, u32[]{:S(2)}, u32[]{:S(2)}) async-start(bf16[8,288,128]{2,1,0:T(8,128)(2,1)} %shard_map.155), calls=%async_computation.1 | async-start | bytes 1179648 | tf_op jit(solution)/shard_map/all_to_all | solution.py:525
  121.5 2.1 %collective-permute-start.21 = (bf16[4,544,128]{2,1,0:T(8,128)(2,1)S(1)}, bf16[4,544,128]{2,1,0:T(8,128)(2,1)S(1)}, u32[]{:S(2)}, u32[]{:S(2)}) collective-permute-start(bf16[4,544,128]{2,1,0:T(8,128)(2,1)S(1)} %bitcast.26), channel_id=1, source_target_pairs={{0,1},{1,0},{2,3},{3,2},{4,5},{5,4},{6,7},{7,6},{8,9},{9,8},{10,11... | collective-permute-start | bytes 1671176 | tf_op jit(solution)/shard_map/ppermute | solution.py:443
  125.2 2.3 %shard_map.157 = (f32[512,1024]{1,0:T(8,128)}, f32[31,1024]{1,0:T(8,128)}) custom-call(s32[8]{0:T(128)S(1)} %copy-done, bf16[4,544,128]{2,1,0:T(8,128)(2,1)S(1)} %bitcast.27, bf16[4,544,128]{2,1,0:T(8,128)(2,1)S(1)} %collective-permute-done.21.got_ref), custom_call_target="tpu_custom_call" | custom-call | flops 2300000000 | bytes 1048576 | tf_op jit(solution)/shard_map/pallas_call | solution.py:527
  127.5 11.2 %all-to-all-done.1.x_ref = bf16[8,288,128]{2,1,0:T(8,128)(2,1)S(1)} async-done(((bf16[8,288,128]{2,1,0:T(8,128)(2,1)}), bf16[8,288,128]{2,1,0:T(8,128)(2,1)S(1)}, u32[]{:S(2)}, u32[]{:S(2)}) %all-to-all-start.1) | async-done | bytes 589856 | tf_op jit(solution)/shard_map/all_to_all | solution.py:525
  (61 shorter events, 21.1 us)
Async XLA Ops:
  2.2 6.9 %collective-permute-start = (bf16[48,1024]{1,0:T(8,128)(2,1)}, bf16[48,1024]{1,0:T(8,128)(2,1)S(1)}, u32[]{:S(2)}, u32[]{:S(2)}) collective-permute-start(bf16[48,1024]{1,0:T(8,128)(2,1)} %get-tuple-element.46), channel_id=1, source_target_pairs={{0,1},{1,2},{2,3},{3,4},{4,5},{5,6},{6,7},{7,8},{8,9},{9,10},{10,1... | collective-permute-start | bytes 294920 | tf_op jit(solution)/shard_map/ppermute | solution.py:452
  7.1 6.1 %collective-permute-start.1 = (bf16[48,1024]{1,0:T(8,128)(2,1)}, bf16[48,1024]{1,0:T(8,128)(2,1)S(1)}, u32[]{:S(2)}, u32[]{:S(2)}) collective-permute-start(bf16[48,1024]{1,0:T(8,128)(2,1)} %get-tuple-element.47), channel_id=1, source_target_pairs={{1,0},{2,1},{3,2},{4,3},{5,4},{6,5},{7,6},{8,7},{9,8},{10,9},{11,1... | collective-permute-start | bytes 294920 | tf_op jit(solution)/shard_map/ppermute | solution.py:453
  27.1 8.5 %collective-permute-start.4 = (bf16[2176,128]{1,0:T(8,128)(2,1)S(1)}, bf16[2176,128]{1,0:T(8,128)(2,1)S(1)}, u32[]{:S(2)}, u32[]{:S(2)}) collective-permute-start(bf16[2176,128]{1,0:T(8,128)(2,1)S(1)} %dynamic-slice_bitcast_fusion), channel_id=1, source_target_pairs={{0,1},{1,0},{2,3},{3,2},{4,5},{5,4},{6,7},{7,6},{8,9},{9,8},{10,11... | collective-permute-start | bytes 1671176 | tf_op jit(solution)/shard_map/ppermute | solution.py:443
  27.2 32.7 %all-to-all-start = ((bf16[8,400,128]{2,1,0:T(8,128)(2,1)}), bf16[8,400,128]{2,1,0:T(8,128)(2,1)S(1)}, u32[]{:S(2)}, u32[]{:S(2)}) async-start(bf16[8,400,128]{2,1,0:T(8,128)(2,1)} %get-tuple-element.48), calls=%async_computation | async-start | bytes 1638400 | tf_op jit(solution)/shard_map/all_to_all | solution.py:457
  35.8 7.5 %collective-permute-start.5 = (bf16[1088,128]{1,0:T(8,128)(2,1)S(1)}, bf16[1088,128]{1,0:T(8,128)(2,1)S(1)}, u32[]{:S(2)}, u32[]{:S(2)}) collective-permute-start(bf16[1088,128]{1,0:T(8,128)(2,1)S(1)} %dynamic-slice_bitcast_fusion.1), channel_id=1, source_target_pairs={{0,32},{32,0},{64,96},{96,64},{128,160},{160,128},{192,224},{224,1... | collective-permute-start | bytes 835592 | tf_op jit(solution)/shard_map/ppermute | solution.py:400
  43.4 4.0 %collective-permute-start.6 = (bf16[272,128]{1,0:T(8,128)(2,1)S(1)}, bf16[272,128]{1,0:T(8,128)(2,1)S(1)}, u32[]{:S(2)}, u32[]{:S(2)}) collective-permute-start(bf16[272,128]{1,0:T(8,128)(2,1)S(1)} %get-tuple-element.90), channel_id=1, source_target_pairs={{0,64},{32,96},{64,0},{96,32},{128,192},{160,224},{192,128},{224,1... | collective-permute-start | bytes 208904 | tf_op jit(solution)/shard_map/ppermute | solution.py:400
  44.8 5.4 %collective-permute-start.7 = (bf16[272,128]{1,0:T(8,128)(2,1)S(1)}, bf16[272,128]{1,0:T(8,128)(2,1)S(1)}, u32[]{:S(2)}, u32[]{:S(2)}) collective-permute-start(bf16[272,128]{1,0:T(8,128)(2,1)S(1)} %get-tuple-element.92), channel_id=1, source_target_pairs={{0,128},{32,160},{64,192},{96,224},{128,0},{160,32},{192,64},{224,... | collective-permute-start | bytes 208904 | tf_op jit(solution)/shard_map/ppermute | solution.py:400
  47.4 5.4 %collective-permute-start.8 = (bf16[272,128]{1,0:T(8,128)(2,1)S(1)}, bf16[272,128]{1,0:T(8,128)(2,1)S(1)}, u32[]{:S(2)}, u32[]{:S(2)}) collective-permute-start(bf16[272,128]{1,0:T(8,128)(2,1)S(1)} %get-tuple-element.91), channel_id=1, source_target_pairs={{0,192},{32,224},{64,128},{96,160},{128,64},{160,96},{192,0},{224,... | collective-permute-start | bytes 208904 | tf_op jit(solution)/shard_map/ppermute | solution.py:400
  52.9 17.1 %collective-permute-start.10 = (bf16[272,128]{1,0:T(8,128)(2,1)S(1)}, bf16[272,128]{1,0:T(8,128)(2,1)S(1)}, u32[]{:S(2)}, u32[]{:S(2)}) collective-permute-start(bf16[272,128]{1,0:T(8,128)(2,1)S(1)} %fusion.3), channel_id=1, source_target_pairs={{0,16},{2,18},{4,20},{6,22},{8,24},{10,26},{12,28},{14,30},{16,0},... | collective-permute-start | bytes 208904 | tf_op jit(solution)/shard_map/ppermute | solution.py:400
  55.4 14.6 %collective-permute-start.11 = (bf16[272,128]{1,0:T(8,128)(2,1)S(1)}, bf16[272,128]{1,0:T(8,128)(2,1)S(1)}, u32[]{:S(2)}, u32[]{:S(2)}) collective-permute-start(bf16[272,128]{1,0:T(8,128)(2,1)S(1)} %fusion.3), channel_id=1, source_target_pairs={{0,18},{2,16},{4,22},{6,20},{8,26},{10,24},{12,30},{14,28},{16,2},... | collective-permute-start | bytes 208904 | tf_op jit(solution)/shard_map/ppermute | solution.py:400
  56.8 13.2 %collective-permute-start.9 = (bf16[272,128]{1,0:T(8,128)(2,1)S(1)}, bf16[272,128]{1,0:T(8,128)(2,1)S(1)}, u32[]{:S(2)}, u32[]{:S(2)}) collective-permute-start(bf16[272,128]{1,0:T(8,128)(2,1)S(1)} %fusion.3), channel_id=1, source_target_pairs={{0,2},{2,0},{4,6},{6,4},{8,10},{10,8},{12,14},{14,12},{16,18},{18,... | collective-permute-start | bytes 208904 | tf_op jit(solution)/shard_map/ppermute | solution.py:400
  60.8 16.6 %collective-permute-start.3 = (bf16[8,192,128]{2,1,0:T(8,128)(2,1)S(1)}, bf16[8,192,128]{2,1,0:T(8,128)(2,1)S(1)}, u32[]{:S(2)}, u32[]{:S(2)}) collective-permute-start(bf16[8,192,128]{2,1,0:T(8,128)(2,1)S(1)} %slice.9.x_ref), channel_id=1, source_target_pairs={{0,16},{16,0},{1,17},{17,1},{2,18},{18,2},{3,19},{19,3},{4,20},{20... | collective-permute-start | bytes 1179656 | tf_op jit(solution)/shard_map/ppermute | solution.py:443
  70.0 14.6 %collective-permute-start.12 = (bf16[272,128]{1,0:T(8,128)(2,1)S(1)}, bf16[272,128]{1,0:T(8,128)(2,1)S(1)}, u32[]{:S(2)}, u32[]{:S(2)}) collective-permute-start(bf16[272,128]{1,0:T(8,128)(2,1)S(1)} %add_convert_fusion.1), channel_id=1, source_target_pairs={{0,4},{2,6},{4,0},{6,2},{8,12},{10,14},{12,8},{14,10},{16,20},{18,... | collective-permute-start | bytes 208904 | tf_op jit(solution)/shard_map/ppermute | solution.py:400
  70.1 14.5 %collective-permute-start.13 = (bf16[272,128]{1,0:T(8,128)(2,1)S(1)}, bf16[272,128]{1,0:T(8,128)(2,1)S(1)}, u32[]{:S(2)}, u32[]{:S(2)}) collective-permute-start(bf16[272,128]{1,0:T(8,128)(2,1)S(1)} %add_convert_fusion.1), channel_id=1, source_target_pairs={{0,8},{2,10},{4,12},{6,14},{8,0},{10,2},{12,4},{14,6},{16,24},{18,... | collective-permute-start | bytes 208904 | tf_op jit(solution)/shard_map/ppermute | solution.py:400
  72.7 12.0 %collective-permute-start.14 = (bf16[272,128]{1,0:T(8,128)(2,1)S(1)}, bf16[272,128]{1,0:T(8,128)(2,1)S(1)}, u32[]{:S(2)}, u32[]{:S(2)}) collective-permute-start(bf16[272,128]{1,0:T(8,128)(2,1)S(1)} %add_convert_fusion.1), channel_id=1, source_target_pairs={{0,12},{2,14},{4,8},{6,10},{8,4},{10,6},{12,0},{14,2},{16,28},{18,... | collective-permute-start | bytes 208904 | tf_op jit(solution)/shard_map/ppermute | solution.py:400
  75.8 12.6 %collective-permute-start.2 = (bf16[8,208,128]{2,1,0:T(8,128)(2,1)S(1)}, bf16[8,208,128]{2,1,0:T(8,128)(2,1)S(1)}, u32[]{:S(2)}, u32[]{:S(2)}) collective-permute-start(bf16[8,208,128]{2,1,0:T(8,128)(2,1)S(1)} %slice.8.x_ref), channel_id=1, source_target_pairs={{0,1},{1,0},{2,3},{3,2},{4,5},{5,4},{6,7},{7,6},{8,9},{9,8},{10,11... | collective-permute-start | bytes 1277960 | tf_op jit(solution)/shard_map/ppermute | solution.py:443
  84.7 11.7 %collective-permute-start.15 = (bf16[272,128]{1,0:T(8,128)(2,1)S(1)}, bf16[272,128]{1,0:T(8,128)(2,1)S(1)}, u32[]{:S(2)}, u32[]{:S(2)}) collective-permute-start(bf16[272,128]{1,0:T(8,128)(2,1)S(1)} %add_convert_fusion), channel_id=1, source_target_pairs={{0,192},{32,224},{64,128},{96,160},{128,64},{160,96},{192,0},{224,... | collective-permute-start | bytes 208904 | tf_op jit(solution)/shard_map/ppermute | solution.py:400
  87.6 8.8 %collective-permute-start.16 = (bf16[272,128]{1,0:T(8,128)(2,1)S(1)}, bf16[272,128]{1,0:T(8,128)(2,1)S(1)}, u32[]{:S(2)}, u32[]{:S(2)}) collective-permute-start(bf16[272,128]{1,0:T(8,128)(2,1)S(1)} %add_convert_fusion), channel_id=1, source_target_pairs={{0,128},{32,160},{64,192},{96,224},{128,0},{160,32},{192,64},{224,... | collective-permute-start | bytes 208904 | tf_op jit(solution)/shard_map/ppermute | solution.py:400
  88.0 8.4 %collective-permute-start.17 = (bf16[272,128]{1,0:T(8,128)(2,1)S(1)}, bf16[272,128]{1,0:T(8,128)(2,1)S(1)}, u32[]{:S(2)}, u32[]{:S(2)}) collective-permute-start(bf16[272,128]{1,0:T(8,128)(2,1)S(1)} %add_convert_fusion), channel_id=1, source_target_pairs={{0,64},{32,96},{64,0},{96,32},{128,192},{160,224},{192,128},{224,1... | collective-permute-start | bytes 208904 | tf_op jit(solution)/shard_map/ppermute | solution.py:400
  95.7 16.4 %collective-permute-start.18 = (bf16[8,192,128]{2,1,0:T(8,128)(2,1)S(1)}, bf16[8,192,128]{2,1,0:T(8,128)(2,1)S(1)}, u32[]{:S(2)}, u32[]{:S(2)}) collective-permute-start(bf16[8,192,128]{2,1,0:T(8,128)(2,1)S(1)} %get-tuple-element.76), channel_id=1, source_target_pairs={{0,16},{16,0},{1,17},{17,1},{2,18},{18,2},{3,19},{19,3},{4,20},{20... | collective-permute-start | bytes 1179656 | tf_op jit(solution)/shard_map/ppermute | solution.py:443
  96.6 15.5 %collective-permute-start.20 = (bf16[1088,128]{1,0:T(8,128)(2,1)S(1)}, bf16[1088,128]{1,0:T(8,128)(2,1)S(1)}, u32[]{:S(2)}, u32[]{:S(2)}) collective-permute-start(bf16[1088,128]{1,0:T(8,128)(2,1)S(1)} %pad_maximum_fusion.1), channel_id=1, source_target_pairs={{0,32},{32,0},{64,96},{96,64},{128,160},{160,128},{192,224},{224,1... | collective-permute-start | bytes 835592 | tf_op jit(solution)/shard_map/ppermute | solution.py:400
  104.5 7.6 %collective-permute-start.19 = (bf16[8,96,128]{2,1,0:T(8,128)(2,1)S(1)}, bf16[8,96,128]{2,1,0:T(8,128)(2,1)S(1)}, u32[]{:S(2)}, u32[]{:S(2)}) collective-permute-start(bf16[8,96,128]{2,1,0:T(8,128)(2,1)S(1)} %get-tuple-element.78), channel_id=1, source_target_pairs={{0,1},{1,0},{2,3},{3,2},{4,5},{5,4},{6,7},{7,6},{8,9},{9,8},{10,11... | collective-permute-start | bytes 589832 | tf_op jit(solution)/shard_map/ppermute | solution.py:443
  115.4 23.2 %all-to-all-start.1 = ((bf16[8,288,128]{2,1,0:T(8,128)(2,1)}), bf16[8,288,128]{2,1,0:T(8,128)(2,1)S(1)}, u32[]{:S(2)}, u32[]{:S(2)}) async-start(bf16[8,288,128]{2,1,0:T(8,128)(2,1)} %shard_map.155), calls=%async_computation.1 | async-start | bytes 1179648 | tf_op jit(solution)/shard_map/all_to_all | solution.py:525
  121.5 3.7 %collective-permute-start.21 = (bf16[4,544,128]{2,1,0:T(8,128)(2,1)S(1)}, bf16[4,544,128]{2,1,0:T(8,128)(2,1)S(1)}, u32[]{:S(2)}, u32[]{:S(2)}) collective-permute-start(bf16[4,544,128]{2,1,0:T(8,128)(2,1)S(1)} %bitcast.26), channel_id=1, source_target_pairs={{0,1},{1,0},{2,3},{3,2},{4,5},{5,4},{6,7},{7,6},{8,9},{9,8},{10,11... | collective-permute-start | bytes 1671176 | tf_op jit(solution)/shard_map/ppermute | solution.py:443
  (4 other events, 37.5 us)

commit v4 on v3

--- a/solution.py
+++ b/solution.py
@@ -18,7 +18,7 @@
 HSIZE = 64
 TAPS = 31
 FREE = 60
-WIDTH = 256
+WIDTH = 512
 ALL = ("dp", "xh", "z", "core")
 SEQ = ("xh", "z", "core")
 
@@ -98,9 +98,10 @@
         out_acc[...] = jnp.zeros_like(out_acc)
         attn_t[...] = attn_ref[0].T
 
-    for i in range(2):
+    heads = WIDTH // 128
+    for i in range(heads):
         cols = slice(i * HSIZE, (i + 1) * HSIZE)
-        h = pl.ds(2 * step + i, 1)
+        h = pl.ds(heads * step + i, 1)
         pay_ref[h, 0:ROWS, 0:HSIZE] = k_ref[:, :, cols]
         pay_ref[h, 0:ROWS, HSIZE:128] = v_ref[:, :, cols]
         q = q_ref[:, :, cols] * BF(0.125)
@@ -195,9 +196,9 @@
                 pl.BlockSpec((512, WIDTH), flat),
                 pl.BlockSpec((1, ROWS, 512), full3),
                 pl.BlockSpec((HEADS, ROWS), full2),
-                pl.BlockSpec((1, ROWS, 128), chunk),
-                pl.BlockSpec((1, ROWS, 128), chunk),
-                pl.BlockSpec((1, ROWS, 128), chunk),
+                pl.BlockSpec((1, ROWS, WIDTH // 2), chunk),
+                pl.BlockSpec((1, ROWS, WIDTH // 2), chunk),
+                pl.BlockSpec((1, ROWS, WIDTH // 2), chunk),
             ],
             out_specs=[
                 pl.BlockSpec((1, ROWS, WIDTH), chunk),
@@ -305,11 +306,28 @@
     score_tile(q, do, st, k, v, kt, dqt, dks, dvs)
 
 
-def tile_2(q, do, st, k, v, kt, dq_ref, dqt, dks, dvs):
-    dqt[...] = dq_ref[...]
+def pack_queries(dqt, dq, dq_ref):
+    def put(z, rows, cols, value):
+        dq_ref[z, rows, cols] = value.astype(BF)
+
+    turn_rows(dqt, dq, put)
+
+
+def pack_keys(part, lengths_ref, dks, dvs, dkv_ref):
+    length = record_length(lengths_ref)
+    for z in range(8):
+        keep = key_rows(part, z, HSIZE) < length
+        rows = slice(z * ROWS, z * ROWS + ROWS)
+        dkv_ref[z, :, 0:HSIZE] = jnp.where(keep, dks[rows, :], 0.0).astype(BF)
+        dkv_ref[z, :, HSIZE:128] = jnp.where(keep, dvs[rows, :], 0.0).astype(BF)
+
+
+def tile_2(q, do, st, k, v, kt, dq_in, dq_ref, dks, dvs, dqt, dq):
+    dqt[...] = dq_in[...]
     dks[...] = jnp.zeros_like(dks)
     dvs[...] = jnp.zeros_like(dvs)
     score_tile(q, do, st, k, v, kt, dqt, dks, dvs)
+    pack_queries(dqt, dq, dq_ref)
 
 
 def tile_3(lengths_ref, q, do, st, k, v, kt, dk_ref, dv_ref, dkv_ref, dqt, dks, dvs):
@@ -317,24 +335,18 @@
     dks[...] = dk_ref[...]
     dvs[...] = dv_ref[...]
     score_tile(q, do, st, k, v, kt, dqt, dks, dvs)
-    length = record_length(lengths_ref)
-    for z in range(8):
-        keep = key_rows(0, z, HSIZE) < length
-        rows = slice(z * ROWS, z * ROWS + ROWS)
-        dkv_ref[z, :, 0:HSIZE] = jnp.where(keep, dks[rows, :], 0.0).astype(BF)
-        dkv_ref[z, :, HSIZE:128] = jnp.where(keep, dvs[rows, :], 0.0).astype(BF)
-
-
-def tile_4(q, do, st, k, v, kt, dq_in, dk_ref, dv_ref, dq_ref, dks, dvs, dqt, dq):
+    pack_keys(0, lengths_ref, dks, dvs, dkv_ref)
+
+
+def tile_4(
+    lengths_ref, q, do, st, k, v, kt, dq_in, dk_ref, dv_ref, dq_ref, dkv_ref, dks, dvs, dqt, dq
+):
     dqt[...] = dq_in[...]
     dks[...] = dk_ref[...]
     dvs[...] = dv_ref[...]
     score_tile(q, do, st, k, v, kt, dqt, dks, dvs)
-
-    def put(z, rows, cols, value):
-        dq_ref[z, rows, cols] = value.astype(BF)
-
-    turn_rows(dqt, dq, put)
+    pack_queries(dqt, dq, dq_ref)
+    pack_keys(1, lengths_ref, dks, dvs, dkv_ref)
 
 
 def tile_call(body, lengths, args, outs, scratch=()):
@@ -355,22 +367,9 @@
     )(*args)
 
 
-def combine(lengths_ref, dk_ref, dv_ref, got_ref, dqt_ref, dqgot_ref, o_ref, dq):
-    length = record_length(lengths_ref)
-    for z in range(8):
-        keep = key_rows(1, z, HSIZE) < length
-        rows = slice(z * ROWS, z * ROWS + ROWS)
-        got = got_ref[z].astype(F32)
-        dk = jnp.where(keep, dk_ref[rows, :], 0.0) + got[:, 0:HSIZE]
-        dv = jnp.where(keep, dv_ref[rows, :], 0.0) + got[:, HSIZE:128]
-        o_ref[z, 0:ROWS, 0:HSIZE] = dk.astype(BF)
-        o_ref[z, 0:ROWS, HSIZE:128] = dv.astype(BF)
-
-    def put(z, rows, cols, value):
-        to = slice(ROWS + rows.start, ROWS + rows.stop)
-        o_ref[z, to, cols] = (value + dqgot_ref[z, rows, cols].astype(F32)).astype(BF)
-
-    turn_rows(dqt_ref, dq, put)
+def combine(dkv_ref, dkv_got_ref, dq_ref, dq_got_ref, o_ref):
+    o_ref[:, 0:ROWS, :] = (dkv_ref[...].astype(F32) + dkv_got_ref[...].astype(F32)).astype(BF)
+    o_ref[:, ROWS:, :] = (dq_ref[...].astype(F32) + dq_got_ref[...].astype(F32)).astype(BF)
 
 
 def unpack_final(x_ref, q_ref, k_ref, v_ref):
@@ -493,35 +492,34 @@
 
     kx = prepared_keys(0, other_keys)
     dqo = after(dqo, sums)
-    dqo, dkx, dvx = tile_call(tile_2, None, qo + kx + (dqo,), (turned, grad, grad))
+    packed_q = sds((8, HALF, 128))
+    packed_k = sds((HEADS, ROWS, 128))
+    dqo, dkx, dvx = tile_call(
+        tile_2, None, qo + kx + (dqo,), (packed_q, grad, grad), [fturned, fgrad]
+    )
     sums = sum_four(sums, 2, 4, dvx)
 
     qc = prepared_queries(core_queries)
     dkx = after(dkx, sums)
     dkv_other, dqc = tile_call(
-        tile_3, lengths, qc + kx + (dkx, dvx), (sds((HEADS, ROWS, 128)), turned), [fgrad, fgrad]
+        tile_3, lengths, qc + kx + (dkx, dvx), (packed_k, turned), [fgrad, fgrad]
     )
     dkv_got = swap(dkv_other, "xh")
     sums = gather_y(sums, dqc)
     dqc = after(dqc, sums)
-    dq_core, dk, dv = tile_call(
+    dq_core, dkv_own = tile_call(
         tile_4,
-        None,
+        lengths,
         qc + ko + (dqc, dk, dv),
-        (sds((8, HALF, 128)), grad, grad),
-        [fturned, fgrad],
+        (packed_q, packed_k),
+        [fgrad, fgrad, fturned, fgrad],
     )
     dq_got = swap(dq_core, "core")
-    sums = gather_x(sums, dk)
     back = call(
-        combine,
-        sds((HEADS, ROWS + HALF, 128)),
-        2,
-        16,
-        in_specs=[smem] + [vmem] * 5,
-        scratch_shapes=[fgrad],
-    )(lengths, dk, dv, dkv_got, dqo, dq_got)
-
+        combine, sds((HEADS, ROWS + HALF, 128)), 1, 8, in_specs=[vmem] * 4
+    )(dkv_own, dkv_got, dqo, dq_got)
+
+    sums = gather_x(sums, back)
     back = lax.all_to_all(back, "z", 0, 0, tiled=True)
     sums = sums.reshape(4, 544, 128)
     grad_proj, grad_taps = call(

time: 141 us -> 134 us (0.950)
  waiting for transfers between devices: 37.8 us -> 32.6 us
  Pallas kernels: 49.2 us -> 47.6 us
    ppermute x14, waiting for transfers between devices: 18.1 us -> 11.8 us  [flip(): return lax.ppermute(x, axis, [(i, i ^ mask) for i in range(size)])]
    pallas_call x1, Pallas kernels: 3.3 us -> 0.96 us  [shards(): call(combine, sds((HEADS, ROWS + HALF, 128)), 1, 8, in_specs=[vmem] * 4)]
  transfers between devices with their start and end apart: 24 -> 24, of which waited for: 8 -> 8; matrix products, arithmetic and copies ran while one was open for 0% -> 1% of each run, Pallas kernels for 22% -> 25%
where the time goes in v4:
time: 134 us; the launch traced here: 133 us
  starting transfers between devices  49.5 us (37%)
  Pallas kernels  47.6 us (36%)
  waiting for transfers between devices  32.6 us (24%)
  local copies, waits for them, and re-layouts  1.95 us (1%)
    pallas_call x4, Pallas kernels, tile_call(): call(body, outs, 7, 40, grid=(1,), in_specs=specs, out_specs=tuple((whole...  27.9 us
    ppermute x14, starting transfers between devices, flip(): return lax.ppermute(x, axis, [(i, i ^ mask) for i in range(size)])  19.9 us
    ppermute x14, waiting for transfers between devices, flip(): return lax.ppermute(x, axis, [(i, i ^ mask) for i in range(size)])  11.8 us
    pallas_call x1, Pallas kernels, conv_call(): pl.pallas_call(conv_kernel, out_shape=(sds((1, ROWS, 1024)), sds((8, 544,...  11.4 us
    all_to_all x1, waiting for transfers between devices, shards(): back = lax.all_to_all(back, 'z', 0, 0, tiled=True)  11.1 us
    all_to_all x1, starting transfers between devices, shards(): pay = lax.all_to_all(pay, 'z', 0, 0, tiled=True)  8.4 us
    ppermute x6, starting transfers between devices, swap(): return lax.ppermute(x, axis, [(0, 1), (1, 0)])  8.32 us
    all_to_all x1, starting transfers between devices, shards(): back = lax.all_to_all(back, 'z', 0, 0, tiled=True)  6.04 us
  transfers between devices with their start and end apart: 24, of which 8 were waited for; matrix products, arithmetic and copies ran while one was open for 1% of the time, Pallas kernels for 25%

profile of v4, /device:TPU:1, one launch (start us, length us, event | category | flops | bytes accessed | tf_op | source)
XLA Modules:
  0.0 133.2 jit_solution(14186281764760849951)
XLA Ops:
  2.2 4.9 %collective-permute-start = (bf16[48,1024]{1,0:T(8,128)(2,1)}, bf16[48,1024]{1,0:T(8,128)(2,1)S(1)}, u32[]{:S(2)}, u32[]{:S(2)}) collective-permute-start(bf16[48,1024]{1,0:T(8,128)(2,1)} %get-tuple-element.45), channel_id=1, source_target_pairs={{0,1},{1,2},{2,3},{3,4},{4,5},{5,6},{6,7},{7,8},{8,9},{9,10},{10,1... | collective-permute-start | bytes 294920 | tf_op jit(solution)/shard_map/ppermute | solution.py:451
  7.1 1.9 %collective-permute-start.1 = (bf16[48,1024]{1,0:T(8,128)(2,1)}, bf16[48,1024]{1,0:T(8,128)(2,1)S(1)}, u32[]{:S(2)}, u32[]{:S(2)}) collective-permute-start(bf16[48,1024]{1,0:T(8,128)(2,1)} %get-tuple-element.46), channel_id=1, source_target_pairs={{1,0},{2,1},{3,2},{4,3},{5,4},{6,5},{7,6},{8,7},{9,8},{10,9},{11,1... | collective-permute-start | bytes 294920 | tf_op jit(solution)/shard_map/ppermute | solution.py:452
  9.1 4.2 %collective-permute-done.1.hi_ref = bf16[48,1024]{1,0:T(8,128)(2,1)S(1)} collective-permute-done((bf16[48,1024]{1,0:T(8,128)(2,1)}, bf16[48,1024]{1,0:T(8,128)(2,1)S(1)}, u32[]{:S(2)}, u32[]{:S(2)}) %collective-permute-start.1) | collective-permute-done | bytes 98336 | tf_op jit(solution)/shard_map/ppermute | solution.py:452
  13.9 11.4 %shard_map.146 = (bf16[1,192,1024]{2,1,0:T(8,128)(2,1)}, bf16[8,544,128]{2,1,0:T(8,128)(2,1)}, bf16[8,400,128]{2,1,0:T(8,128)(2,1)}) custom-call(s32[8]{0:T(128)} %lengths_ref.11, bf16[1,192,1024]{2,1,0:T(8,128)(2,1)} %x_ref.1, bf16[1,192,1024]{2,1,0:T(8,128)(2,1)} %g_ref.1, bf16[48,1024]{1,0:T(8,128)(2,1)} %copy-done.2, bf16[48,1024]{1,0:T(8,128)(2,1)} %copy-done.3, ...), custom_call_target="tpu_custom_call" | custom-call | flops 12650000384 | bytes 1048576 | tf_op jit(solution)/shard_map/pallas_call | solution.py:180
  26.6 8.4 %all-to-all-start = ((bf16[8,400,128]{2,1,0:T(8,128)(2,1)}), bf16[8,400,128]{2,1,0:T(8,128)(2,1)S(1)}, u32[]{:S(2)}, u32[]{:S(2)}) async-start(bf16[8,400,128]{2,1,0:T(8,128)(2,1)} %get-tuple-element.47), calls=%async_computation | async-start | bytes 1638400 | tf_op jit(solution)/shard_map/all_to_all | solution.py:456
  36.4 6.3 %collective-permute-done.5 = bf16[1088,128]{1,0:T(8,128)(2,1)S(1)} collective-permute-done((bf16[1088,128]{1,0:T(8,128)(2,1)S(1)}, bf16[1088,128]{1,0:T(8,128)(2,1)S(1)}, u32[]{:S(2)}, u32[]{:S(2)}) %collective-permute-start.5) | collective-permute-done | bytes 278560 | tf_op jit(solution)/shard_map/ppermute | solution.py:399
  44.2 2.6 %collective-permute-start.7 = (bf16[272,128]{1,0:T(8,128)(2,1)S(1)}, bf16[272,128]{1,0:T(8,128)(2,1)S(1)}, u32[]{:S(2)}, u32[]{:S(2)}) collective-permute-start(bf16[272,128]{1,0:T(8,128)(2,1)S(1)} %get-tuple-element.90), channel_id=1, source_target_pairs={{0,128},{32,160},{64,192},{96,224},{128,0},{160,32},{192,64},{224,... | collective-permute-start | bytes 208904 | tf_op jit(solution)/shard_map/ppermute | solution.py:399
  46.9 2.7 %collective-permute-done.7 = bf16[272,128]{1,0:T(8,128)(2,1)S(1)} collective-permute-done((bf16[272,128]{1,0:T(8,128)(2,1)S(1)}, bf16[272,128]{1,0:T(8,128)(2,1)S(1)}, u32[]{:S(2)}, u32[]{:S(2)}) %collective-permute-start.7) | collective-permute-done | bytes 69664 | tf_op jit(solution)/shard_map/ppermute | solution.py:399
  49.6 2.7 %collective-permute-done.8 = bf16[272,128]{1,0:T(8,128)(2,1)S(1)} collective-permute-done((bf16[272,128]{1,0:T(8,128)(2,1)S(1)}, bf16[272,128]{1,0:T(8,128)(2,1)S(1)}, u32[]{:S(2)}, u32[]{:S(2)}) %collective-permute-start.8) | collective-permute-done | bytes 69664 | tf_op jit(solution)/shard_map/ppermute | solution.py:399
  52.3 2.5 %collective-permute-start.10 = (bf16[272,128]{1,0:T(8,128)(2,1)S(1)}, bf16[272,128]{1,0:T(8,128)(2,1)S(1)}, u32[]{:S(2)}, u32[]{:S(2)}) collective-permute-start(bf16[272,128]{1,0:T(8,128)(2,1)S(1)} %fusion.3), channel_id=1, source_target_pairs={{0,16},{2,18},{4,20},{6,22},{8,24},{10,26},{12,28},{14,30},{16,0},... | collective-permute-start | bytes 208904 | tf_op jit(solution)/shard_map/ppermute | solution.py:399
  56.6 2.7 %all-to-all-done = bf16[8,400,128]{2,1,0:T(8,128)(2,1)S(1)} async-done(((bf16[8,400,128]{2,1,0:T(8,128)(2,1)}), bf16[8,400,128]{2,1,0:T(8,128)(2,1)S(1)}, u32[]{:S(2)}, u32[]{:S(2)}) %all-to-all-start) | async-done | bytes 819232 | tf_op jit(solution)/shard_map/all_to_all | solution.py:456
  60.3 2.7 %collective-permute-start.3 = (bf16[8,192,128]{2,1,0:T(8,128)(2,1)S(1)}, bf16[8,192,128]{2,1,0:T(8,128)(2,1)S(1)}, u32[]{:S(2)}, u32[]{:S(2)}) collective-permute-start(bf16[8,192,128]{2,1,0:T(8,128)(2,1)S(1)} %slice.9.x_ref), channel_id=1, source_target_pairs={{0,16},{16,0},{1,17},{17,1},{2,18},{18,2},{3,19},{19,3},{4,20},{20... | collective-permute-start | bytes 1179656 | tf_op jit(solution)/shard_map/ppermute | solution.py:442
  63.2 6.3 %shard_map.151 = (f32[64,1536]{1,0:T(8,128)S(1)}, f32[1536,64]{1,0:T(8,128)S(1)}, f32[1536,64]{1,0:T(8,128)S(1)}) custom-call(bf16[1536,64]{1,0:T(8,128)(2,1)S(1)} %get-tuple-element.57.q, bf16[1536,64]{1,0:T(8,128)(2,1)S(1)} %get-tuple-element.58.do, f32[8,1536]{1,0:T(8,128)S(1)} %get-tuple-element.59.st, bf16[1536,64]{1,0:T(8,128)(2,1)S(1)} %get-tuple-element.51.k, ...), custom_call_target="tpu_custom_call" | custom-call | flops 8049999872 | bytes 1048576 | tf_op jit(solution)/shard_map/pallas_call | solution.py:358
  69.8 2.6 %collective-permute-start.13 = (bf16[272,128]{1,0:T(8,128)(2,1)S(1)}, bf16[272,128]{1,0:T(8,128)(2,1)S(1)}, u32[]{:S(2)}, u32[]{:S(2)}) collective-permute-start(bf16[272,128]{1,0:T(8,128)(2,1)S(1)} %add_convert_fusion.1), channel_id=1, source_target_pairs={{0,8},{2,10},{4,12},{6,14},{8,0},{10,2},{12,4},{14,6},{16,24},{18,... | collective-permute-start | bytes 208904 | tf_op jit(solution)/shard_map/ppermute | solution.py:399
  72.4 3.1 %collective-permute-start.14 = (bf16[272,128]{1,0:T(8,128)(2,1)S(1)}, bf16[272,128]{1,0:T(8,128)(2,1)S(1)}, u32[]{:S(2)}, u32[]{:S(2)}) collective-permute-start(bf16[272,128]{1,0:T(8,128)(2,1)S(1)} %add_convert_fusion.1), channel_id=1, source_target_pairs={{0,12},{2,14},{4,8},{6,10},{8,4},{10,6},{12,0},{14,2},{16,28},{18,... | collective-permute-start | bytes 208904 | tf_op jit(solution)/shard_map/ppermute | solution.py:399
  75.4 1.6 %collective-permute-start.2 = (bf16[8,208,128]{2,1,0:T(8,128)(2,1)S(1)}, bf16[8,208,128]{2,1,0:T(8,128)(2,1)S(1)}, u32[]{:S(2)}, u32[]{:S(2)}) collective-permute-start(bf16[8,208,128]{2,1,0:T(8,128)(2,1)S(1)} %slice.8.x_ref), channel_id=1, source_target_pairs={{0,1},{1,0},{2,3},{3,2},{4,5},{5,4},{6,7},{7,6},{8,9},{9,8},{10,11... | collective-permute-start | bytes 1277960 | tf_op jit(solution)/shard_map/ppermute | solution.py:442
  78.0 6.8 %shard_map.152 = (bf16[8,96,128]{2,1,0:T(8,128)(2,1)S(1)}, f32[1536,64]{1,0:T(8,128)S(1)}, f32[1536,64]{1,0:T(8,128)S(1)}) custom-call(bf16[1536,64]{1,0:T(8,128)(2,1)S(1)} %get-tuple-element.57.q, bf16[1536,64]{1,0:T(8,128)(2,1)S(1)} %get-tuple-element.58.do, f32[8,1536]{1,0:T(8,128)S(1)} %get-tuple-element.59.st, ...), custom_call_target="tpu_custom_call" | custom-call | flops 8049999872 | bytes 1048576 | tf_op jit(solution)/shard_map/pallas_call | solution.py:358
  84.8 2.9 %collective-permute-start.15 = (bf16[272,128]{1,0:T(8,128)(2,1)S(1)}, bf16[272,128]{1,0:T(8,128)(2,1)S(1)}, u32[]{:S(2)}, u32[]{:S(2)}) collective-permute-start(bf16[272,128]{1,0:T(8,128)(2,1)S(1)} %add_convert_fusion), channel_id=1, source_target_pairs={{0,192},{32,224},{64,128},{96,160},{128,64},{160,96},{192,0},{224,... | collective-permute-start | bytes 208904 | tf_op jit(solution)/shard_map/ppermute | solution.py:399
  88.7 7.2 %shard_map.153 = (bf16[8,192,128]{2,1,0:T(8,128)(2,1)S(1)}, f32[64,1536]{1,0:T(8,128)S(1)}) custom-call(s32[8]{0:T(128)S(1)} %copy-done, bf16[1536,64]{1,0:T(8,128)(2,1)S(1)} %get-tuple-element.48.q, bf16[1536,64]{1,0:T(8,128)(2,1)S(1)} %get-tuple-element.49.do, f32[8,1536]{1,0:T(8,128)S(1)} %get-tuple-element.50.st, ...), custom_call_target="tpu_custom_call" | custom-call | flops 8049999872 | bytes 1048576 | tf_op jit(solution)/shard_map/pallas_call | solution.py:358
  97.0 7.6 %shard_map.154 = (bf16[8,96,128]{2,1,0:T(8,128)(2,1)S(1)}, bf16[8,192,128]{2,1,0:T(8,128)(2,1)S(1)}) custom-call(s32[8]{0:T(128)S(1)} %copy-done, bf16[1536,64]{1,0:T(8,128)(2,1)S(1)} %get-tuple-element.48.q, bf16[1536,64]{1,0:T(8,128)(2,1)S(1)} %get-tuple-element.49.do, f32[8,1536]{1,0:T(8,128)S(1)} %get-tuple-element.50.st, ...), custom_call_target="tpu_custom_call" | custom-call | flops 8049999872 | bytes 1048576 | tf_op jit(solution)/shard_map/pallas_call | solution.py:358
  108.7 6.0 %all-to-all-start.1 = ((bf16[8,288,128]{2,1,0:T(8,128)(2,1)}), bf16[8,288,128]{2,1,0:T(8,128)(2,1)S(1)}, u32[]{:S(2)}, u32[]{:S(2)}) async-start(bf16[8,288,128]{2,1,0:T(8,128)(2,1)} %shard_map.155), calls=%async_computation.1 | async-start | bytes 1179648 | tf_op jit(solution)/shard_map/all_to_all | solution.py:523
  114.9 2.1 %collective-permute-start.21 = (bf16[4,544,128]{2,1,0:T(8,128)(2,1)S(1)}, bf16[4,544,128]{2,1,0:T(8,128)(2,1)S(1)}, u32[]{:S(2)}, u32[]{:S(2)}) collective-permute-start(bf16[4,544,128]{2,1,0:T(8,128)(2,1)S(1)} %bitcast.26), channel_id=1, source_target_pairs={{0,1},{1,0},{2,3},{3,2},{4,5},{5,4},{6,7},{7,6},{8,9},{9,8},{10,11... | collective-permute-start | bytes 1671176 | tf_op jit(solution)/shard_map/ppermute | solution.py:442
  118.6 2.3 %shard_map.157 = (f32[512,1024]{1,0:T(8,128)}, f32[31,1024]{1,0:T(8,128)}) custom-call(s32[8]{0:T(128)S(1)} %copy-done, bf16[4,544,128]{2,1,0:T(8,128)(2,1)S(1)} %bitcast.27, bf16[4,544,128]{2,1,0:T(8,128)(2,1)S(1)} %collective-permute-done.21.got_ref), custom_call_target="tpu_custom_call" | custom-call | flops 2300000000 | bytes 1048576 | tf_op jit(solution)/shard_map/pallas_call | solution.py:525
  120.8 11.1 %all-to-all-done.1.x_ref = bf16[8,288,128]{2,1,0:T(8,128)(2,1)S(1)} async-done(((bf16[8,288,128]{2,1,0:T(8,128)(2,1)}), bf16[8,288,128]{2,1,0:T(8,128)(2,1)S(1)}, u32[]{:S(2)}, u32[]{:S(2)}) %all-to-all-start.1) | async-done | bytes 589856 | tf_op jit(solution)/shard_map/all_to_all | solution.py:523
  (61 shorter events, 19.6 us)
Async XLA Ops:
  2.2 6.9 %collective-permute-start = (bf16[48,1024]{1,0:T(8,128)(2,1)}, bf16[48,1024]{1,0:T(8,128)(2,1)S(1)}, u32[]{:S(2)}, u32[]{:S(2)}) collective-permute-start(bf16[48,1024]{1,0:T(8,128)(2,1)} %get-tuple-element.45), channel_id=1, source_target_pairs={{0,1},{1,2},{2,3},{3,4},{4,5},{5,6},{6,7},{7,8},{8,9},{9,10},{10,1... | collective-permute-start | bytes 294920 | tf_op jit(solution)/shard_map/ppermute | solution.py:451
  7.1 6.1 %collective-permute-start.1 = (bf16[48,1024]{1,0:T(8,128)(2,1)}, bf16[48,1024]{1,0:T(8,128)(2,1)S(1)}, u32[]{:S(2)}, u32[]{:S(2)}) collective-permute-start(bf16[48,1024]{1,0:T(8,128)(2,1)} %get-tuple-element.46), channel_id=1, source_target_pairs={{1,0},{2,1},{3,2},{4,3},{5,4},{6,5},{7,6},{8,7},{9,8},{10,9},{11,1... | collective-permute-start | bytes 294920 | tf_op jit(solution)/shard_map/ppermute | solution.py:452
  26.5 8.5 %collective-permute-start.4 = (bf16[2176,128]{1,0:T(8,128)(2,1)S(1)}, bf16[2176,128]{1,0:T(8,128)(2,1)S(1)}, u32[]{:S(2)}, u32[]{:S(2)}) collective-permute-start(bf16[2176,128]{1,0:T(8,128)(2,1)S(1)} %dynamic-slice_bitcast_fusion), channel_id=1, source_target_pairs={{0,1},{1,0},{2,3},{3,2},{4,5},{5,4},{6,7},{7,6},{8,9},{9,8},{10,11... | collective-permute-start | bytes 1671176 | tf_op jit(solution)/shard_map/ppermute | solution.py:442
  26.6 32.7 %all-to-all-start = ((bf16[8,400,128]{2,1,0:T(8,128)(2,1)}), bf16[8,400,128]{2,1,0:T(8,128)(2,1)S(1)}, u32[]{:S(2)}, u32[]{:S(2)}) async-start(bf16[8,400,128]{2,1,0:T(8,128)(2,1)} %get-tuple-element.47), calls=%async_computation | async-start | bytes 1638400 | tf_op jit(solution)/shard_map/all_to_all | solution.py:456
  35.2 7.5 %collective-permute-start.5 = (bf16[1088,128]{1,0:T(8,128)(2,1)S(1)}, bf16[1088,128]{1,0:T(8,128)(2,1)S(1)}, u32[]{:S(2)}, u32[]{:S(2)}) collective-permute-start(bf16[1088,128]{1,0:T(8,128)(2,1)S(1)} %dynamic-slice_bitcast_fusion.1), channel_id=1, source_target_pairs={{0,32},{32,0},{64,96},{96,64},{128,160},{160,128},{192,224},{224,1... | collective-permute-start | bytes 835592 | tf_op jit(solution)/shard_map/ppermute | solution.py:399
  42.9 4.0 %collective-permute-start.6 = (bf16[272,128]{1,0:T(8,128)(2,1)S(1)}, bf16[272,128]{1,0:T(8,128)(2,1)S(1)}, u32[]{:S(2)}, u32[]{:S(2)}) collective-permute-start(bf16[272,128]{1,0:T(8,128)(2,1)S(1)} %get-tuple-element.88), channel_id=1, source_target_pairs={{0,64},{32,96},{64,0},{96,32},{128,192},{160,224},{192,128},{224,1... | collective-permute-start | bytes 208904 | tf_op jit(solution)/shard_map/ppermute | solution.py:399
  44.2 5.4 %collective-permute-start.7 = (bf16[272,128]{1,0:T(8,128)(2,1)S(1)}, bf16[272,128]{1,0:T(8,128)(2,1)S(1)}, u32[]{:S(2)}, u32[]{:S(2)}) collective-permute-start(bf16[272,128]{1,0:T(8,128)(2,1)S(1)} %get-tuple-element.90), channel_id=1, source_target_pairs={{0,128},{32,160},{64,192},{96,224},{128,0},{160,32},{192,64},{224,... | collective-permute-start | bytes 208904 | tf_op jit(solution)/shard_map/ppermute | solution.py:399
  46.9 5.4 %collective-permute-start.8 = (bf16[272,128]{1,0:T(8,128)(2,1)S(1)}, bf16[272,128]{1,0:T(8,128)(2,1)S(1)}, u32[]{:S(2)}, u32[]{:S(2)}) collective-permute-start(bf16[272,128]{1,0:T(8,128)(2,1)S(1)} %get-tuple-element.89), channel_id=1, source_target_pairs={{0,192},{32,224},{64,128},{96,160},{128,64},{160,96},{192,0},{224,... | collective-permute-start | bytes 208904 | tf_op jit(solution)/shard_map/ppermute | solution.py:399
  52.3 17.3 %collective-permute-start.10 = (bf16[272,128]{1,0:T(8,128)(2,1)S(1)}, bf16[272,128]{1,0:T(8,128)(2,1)S(1)}, u32[]{:S(2)}, u32[]{:S(2)}) collective-permute-start(bf16[272,128]{1,0:T(8,128)(2,1)S(1)} %fusion.3), channel_id=1, source_target_pairs={{0,16},{2,18},{4,20},{6,22},{8,24},{10,26},{12,28},{14,30},{16,0},... | collective-permute-start | bytes 208904 | tf_op jit(solution)/shard_map/ppermute | solution.py:399
  54.8 14.8 %collective-permute-start.11 = (bf16[272,128]{1,0:T(8,128)(2,1)S(1)}, bf16[272,128]{1,0:T(8,128)(2,1)S(1)}, u32[]{:S(2)}, u32[]{:S(2)}) collective-permute-start(bf16[272,128]{1,0:T(8,128)(2,1)S(1)} %fusion.3), channel_id=1, source_target_pairs={{0,18},{2,16},{4,22},{6,20},{8,26},{10,24},{12,30},{14,28},{16,2},... | collective-permute-start | bytes 208904 | tf_op jit(solution)/shard_map/ppermute | solution.py:399
  56.2 13.4 %collective-permute-start.9 = (bf16[272,128]{1,0:T(8,128)(2,1)S(1)}, bf16[272,128]{1,0:T(8,128)(2,1)S(1)}, u32[]{:S(2)}, u32[]{:S(2)}) collective-permute-start(bf16[272,128]{1,0:T(8,128)(2,1)S(1)} %fusion.3), channel_id=1, source_target_pairs={{0,2},{2,0},{4,6},{6,4},{8,10},{10,8},{12,14},{14,12},{16,18},{18,... | collective-permute-start | bytes 208904 | tf_op jit(solution)/shard_map/ppermute | solution.py:399
  60.3 16.8 %collective-permute-start.3 = (bf16[8,192,128]{2,1,0:T(8,128)(2,1)S(1)}, bf16[8,192,128]{2,1,0:T(8,128)(2,1)S(1)}, u32[]{:S(2)}, u32[]{:S(2)}) collective-permute-start(bf16[8,192,128]{2,1,0:T(8,128)(2,1)S(1)} %slice.9.x_ref), channel_id=1, source_target_pairs={{0,16},{16,0},{1,17},{17,1},{2,18},{18,2},{3,19},{19,3},{4,20},{20... | collective-permute-start | bytes 1179656 | tf_op jit(solution)/shard_map/ppermute | solution.py:442
  69.7 15.1 %collective-permute-start.12 = (bf16[272,128]{1,0:T(8,128)(2,1)S(1)}, bf16[272,128]{1,0:T(8,128)(2,1)S(1)}, u32[]{:S(2)}, u32[]{:S(2)}) collective-permute-start(bf16[272,128]{1,0:T(8,128)(2,1)S(1)} %add_convert_fusion.1), channel_id=1, source_target_pairs={{0,4},{2,6},{4,0},{6,2},{8,12},{10,14},{12,8},{14,10},{16,20},{18,... | collective-permute-start | bytes 208904 | tf_op jit(solution)/shard_map/ppermute | solution.py:399
  69.8 15.0 %collective-permute-start.13 = (bf16[272,128]{1,0:T(8,128)(2,1)S(1)}, bf16[272,128]{1,0:T(8,128)(2,1)S(1)}, u32[]{:S(2)}, u32[]{:S(2)}) collective-permute-start(bf16[272,128]{1,0:T(8,128)(2,1)S(1)} %add_convert_fusion.1), channel_id=1, source_target_pairs={{0,8},{2,10},{4,12},{6,14},{8,0},{10,2},{12,4},{14,6},{16,24},{18,... | collective-permute-start | bytes 208904 | tf_op jit(solution)/shard_map/ppermute | solution.py:399
  72.4 12.4 %collective-permute-start.14 = (bf16[272,128]{1,0:T(8,128)(2,1)S(1)}, bf16[272,128]{1,0:T(8,128)(2,1)S(1)}, u32[]{:S(2)}, u32[]{:S(2)}) collective-permute-start(bf16[272,128]{1,0:T(8,128)(2,1)S(1)} %add_convert_fusion.1), channel_id=1, source_target_pairs={{0,12},{2,14},{4,8},{6,10},{8,4},{10,6},{12,0},{14,2},{16,28},{18,... | collective-permute-start | bytes 208904 | tf_op jit(solution)/shard_map/ppermute | solution.py:399
  75.4 13.0 %collective-permute-start.2 = (bf16[8,208,128]{2,1,0:T(8,128)(2,1)S(1)}, bf16[8,208,128]{2,1,0:T(8,128)(2,1)S(1)}, u32[]{:S(2)}, u32[]{:S(2)}) collective-permute-start(bf16[8,208,128]{2,1,0:T(8,128)(2,1)S(1)} %slice.8.x_ref), channel_id=1, source_target_pairs={{0,1},{1,0},{2,3},{3,2},{4,5},{5,4},{6,7},{7,6},{8,9},{9,8},{10,11... | collective-permute-start | bytes 1277960 | tf_op jit(solution)/shard_map/ppermute | solution.py:442
  84.8 11.9 %collective-permute-start.15 = (bf16[272,128]{1,0:T(8,128)(2,1)S(1)}, bf16[272,128]{1,0:T(8,128)(2,1)S(1)}, u32[]{:S(2)}, u32[]{:S(2)}) collective-permute-start(bf16[272,128]{1,0:T(8,128)(2,1)S(1)} %add_convert_fusion), channel_id=1, source_target_pairs={{0,192},{32,224},{64,128},{96,160},{128,64},{160,96},{192,0},{224,... | collective-permute-start | bytes 208904 | tf_op jit(solution)/shard_map/ppermute | solution.py:399
  87.8 9.0 %collective-permute-start.16 = (bf16[272,128]{1,0:T(8,128)(2,1)S(1)}, bf16[272,128]{1,0:T(8,128)(2,1)S(1)}, u32[]{:S(2)}, u32[]{:S(2)}) collective-permute-start(bf16[272,128]{1,0:T(8,128)(2,1)S(1)} %add_convert_fusion), channel_id=1, source_target_pairs={{0,128},{32,160},{64,192},{96,224},{128,0},{160,32},{192,64},{224,... | collective-permute-start | bytes 208904 | tf_op jit(solution)/shard_map/ppermute | solution.py:399
  88.1 8.7 %collective-permute-start.17 = (bf16[272,128]{1,0:T(8,128)(2,1)S(1)}, bf16[272,128]{1,0:T(8,128)(2,1)S(1)}, u32[]{:S(2)}, u32[]{:S(2)}) collective-permute-start(bf16[272,128]{1,0:T(8,128)(2,1)S(1)} %add_convert_fusion), channel_id=1, source_target_pairs={{0,64},{32,96},{64,0},{96,32},{128,192},{160,224},{192,128},{224,1... | collective-permute-start | bytes 208904 | tf_op jit(solution)/shard_map/ppermute | solution.py:399
  95.9 11.9 %collective-permute-start.18 = (bf16[8,192,128]{2,1,0:T(8,128)(2,1)S(1)}, bf16[8,192,128]{2,1,0:T(8,128)(2,1)S(1)}, u32[]{:S(2)}, u32[]{:S(2)}) collective-permute-start(bf16[8,192,128]{2,1,0:T(8,128)(2,1)S(1)} %get-tuple-element.74), channel_id=1, source_target_pairs={{0,16},{16,0},{1,17},{17,1},{2,18},{18,2},{3,19},{19,3},{4,20},{20... | collective-permute-start | bytes 1179656 | tf_op jit(solution)/shard_map/ppermute | solution.py:442
  104.5 2.1 %collective-permute-start.19 = (bf16[8,96,128]{2,1,0:T(8,128)(2,1)S(1)}, bf16[8,96,128]{2,1,0:T(8,128)(2,1)S(1)}, u32[]{:S(2)}, u32[]{:S(2)}) collective-permute-start(bf16[8,96,128]{2,1,0:T(8,128)(2,1)S(1)} %get-tuple-element.76), channel_id=1, source_target_pairs={{0,1},{1,0},{2,3},{3,2},{4,5},{5,4},{6,7},{7,6},{8,9},{9,8},{10,11... | collective-permute-start | bytes 589832 | tf_op jit(solution)/shard_map/ppermute | solution.py:442
  105.5 9.3 %collective-permute-start.20 = (bf16[1088,128]{1,0:T(8,128)(2,1)S(1)}, bf16[1088,128]{1,0:T(8,128)(2,1)S(1)}, u32[]{:S(2)}, u32[]{:S(2)}) collective-permute-start(bf16[1088,128]{1,0:T(8,128)(2,1)S(1)} %pad_maximum_fusion.1), channel_id=1, source_target_pairs={{0,32},{32,0},{64,96},{96,64},{128,160},{160,128},{192,224},{224,1... | collective-permute-start | bytes 835592 | tf_op jit(solution)/shard_map/ppermute | solution.py:399
  108.7 23.2 %all-to-all-start.1 = ((bf16[8,288,128]{2,1,0:T(8,128)(2,1)}), bf16[8,288,128]{2,1,0:T(8,128)(2,1)S(1)}, u32[]{:S(2)}, u32[]{:S(2)}) async-start(bf16[8,288,128]{2,1,0:T(8,128)(2,1)} %shard_map.155), calls=%async_computation.1 | async-start | bytes 1179648 | tf_op jit(solution)/shard_map/all_to_all | solution.py:523
  114.9 3.7 %collective-permute-start.21 = (bf16[4,544,128]{2,1,0:T(8,128)(2,1)S(1)}, bf16[4,544,128]{2,1,0:T(8,128)(2,1)S(1)}, u32[]{:S(2)}, u32[]{:S(2)}) collective-permute-start(bf16[4,544,128]{2,1,0:T(8,128)(2,1)S(1)} %bitcast.26), channel_id=1, source_target_pairs={{0,1},{1,0},{2,3},{3,2},{4,5},{5,4},{6,7},{7,6},{8,9},{9,8},{10,11... | collective-permute-start | bytes 1671176 | tf_op jit(solution)/shard_map/ppermute | solution.py:442
  (4 other events, 37.5 us)

commit v5 on v4

--- a/solution.py
+++ b/solution.py
@@ -417,6 +417,10 @@
     return add(after(x, beside), *got)
 
 
+def sum_two(x, mask, beside):
+    return add(after(x, beside), flip(x, ("xh", "z"), mask, 16))
+
+
 def gather_y(x, beside):
     y = lax.axis_index("dp") >> 1
     odd, upper = (y & 1) == 1, (y & 2) == 2
@@ -497,7 +501,7 @@
     dqo, dkx, dvx = tile_call(
         tile_2, None, qo + kx + (dqo,), (packed_q, grad, grad), [fturned, fgrad]
     )
-    sums = sum_four(sums, 2, 4, dvx)
+    sums = sum_two(sums, 2, dvx)
 
     qc = prepared_queries(core_queries)
     dkx = after(dkx, sums)
@@ -505,7 +509,7 @@
         tile_3, lengths, qc + kx + (dkx, dvx), (packed_k, turned), [fgrad, fgrad]
     )
     dkv_got = swap(dkv_other, "xh")
-    sums = gather_y(sums, dqc)
+    sums = sum_two(sums, 4, dqc)
     dqc = after(dqc, sums)
     dq_core, dkv_own = tile_call(
         tile_4,
@@ -519,7 +523,7 @@
         combine, sds((HEADS, ROWS + HALF, 128)), 1, 8, in_specs=[vmem] * 4
     )(dkv_own, dkv_got, dqo, dq_got)
 
-    sums = gather_x(sums, back)
+    sums = gather_x(gather_y(sums, dkv_own), back)
     back = lax.all_to_all(back, "z", 0, 0, tiled=True)
     sums = sums.reshape(4, 544, 128)
     grad_proj, grad_taps = call(

time: 134 us -> 133 us (level)
  starting transfers between devices: 49.5 us -> 46.9 us
  waiting for transfers between devices: 32.6 us -> 34.9 us
    ppermute x14 -> x13, waiting for transfers between devices: 11.8 us -> 14.3 us  [flip(): return lax.ppermute(x, axis, [(i, i ^ mask) for i in range(size)])]
    all_to_all x1, starting transfers between devices: 6.04 us -> 3.96 us  [shards(): back = lax.all_to_all(back, 'z', 0, 0, tiled=True)]
    ppermute x14 -> x13, starting transfers between devices: 19.9 us -> 19.3 us  [flip(): return lax.ppermute(x, axis, [(i, i ^ mask) for i in range(size)])]
  transfers between devices with their start and end apart: 24 -> 23, of which waited for: 8 -> 9; matrix products, arithmetic and copies ran while one was open for 1% -> 1% of each run, Pallas kernels for 25% -> 25%
where the time goes in v5:
time: 133 us
  Pallas kernels  47.6 us (36%)
  starting transfers between devices  46.9 us (35%)
  waiting for transfers between devices  34.9 us (26%)
  local copies, waits for them, and re-layouts  1.95 us (1%)
    pallas_call x4, Pallas kernels, tile_call(): call(body, outs, 7, 40, grid=(1,), in_specs=specs, out_specs=tuple((whole...  27.9 us
    ppermute x13, starting transfers between devices, flip(): return lax.ppermute(x, axis, [(i, i ^ mask) for i in range(size)])  19.3 us
    ppermute x13, waiting for transfers between devices, flip(): return lax.ppermute(x, axis, [(i, i ^ mask) for i in range(size)])  14.3 us
    all_to_all x1, waiting for transfers between devices, shards(): back = lax.all_to_all(back, 'z', 0, 0, tiled=True)  12 us
    pallas_call x1, Pallas kernels, conv_call(): pl.pallas_call(conv_kernel, out_shape=(sds((1, ROWS, 1024)), sds((8, 544,...  11.4 us
    all_to_all x1, starting transfers between devices, shards(): pay = lax.all_to_all(pay, 'z', 0, 0, tiled=True)  8.4 us
    ppermute x6, starting transfers between devices, swap(): return lax.ppermute(x, axis, [(0, 1), (1, 0)])  8.36 us
    ppermute x1, starting transfers between devices, shards(): lo = lax.ppermute(last, SEQ, up)  4.92 us
  transfers between devices with their start and end apart: 23, of which 9 were waited for; matrix products, arithmetic and copies ran while one was open for 1% of the time, Pallas kernels for 25%

profile of v5, /device:TPU:1, one launch (start us, length us, event | category | flops | bytes accessed | tf_op | source)
XLA Modules:
  0.0 132.8 jit_solution(9928096919819986885)
XLA Ops:
  2.2 4.9 %collective-permute-start = (bf16[48,1024]{1,0:T(8,128)(2,1)}, bf16[48,1024]{1,0:T(8,128)(2,1)S(1)}, u32[]{:S(2)}, u32[]{:S(2)}) collective-permute-start(bf16[48,1024]{1,0:T(8,128)(2,1)} %get-tuple-element.46), channel_id=1, source_target_pairs={{0,1},{1,2},{2,3},{3,4},{4,5},{5,6},{6,7},{7,8},{8,9},{9,10},{10,1... | collective-permute-start | bytes 294920 | tf_op jit(solution)/shard_map/ppermute | solution.py:455
  7.1 1.9 %collective-permute-start.1 = (bf16[48,1024]{1,0:T(8,128)(2,1)}, bf16[48,1024]{1,0:T(8,128)(2,1)S(1)}, u32[]{:S(2)}, u32[]{:S(2)}) collective-permute-start(bf16[48,1024]{1,0:T(8,128)(2,1)} %get-tuple-element.47), channel_id=1, source_target_pairs={{1,0},{2,1},{3,2},{4,3},{5,4},{6,5},{7,6},{8,7},{9,8},{10,9},{11,1... | collective-permute-start | bytes 294920 | tf_op jit(solution)/shard_map/ppermute | solution.py:456
  9.1 4.2 %collective-permute-done.1.hi_ref = bf16[48,1024]{1,0:T(8,128)(2,1)S(1)} collective-permute-done((bf16[48,1024]{1,0:T(8,128)(2,1)}, bf16[48,1024]{1,0:T(8,128)(2,1)S(1)}, u32[]{:S(2)}, u32[]{:S(2)}) %collective-permute-start.1) | collective-permute-done | bytes 98336 | tf_op jit(solution)/shard_map/ppermute | solution.py:456
  13.9 11.4 %shard_map.146 = (bf16[1,192,1024]{2,1,0:T(8,128)(2,1)}, bf16[8,544,128]{2,1,0:T(8,128)(2,1)}, bf16[8,400,128]{2,1,0:T(8,128)(2,1)}) custom-call(s32[8]{0:T(128)} %lengths_ref.11, bf16[1,192,1024]{2,1,0:T(8,128)(2,1)} %x_ref.1, bf16[1,192,1024]{2,1,0:T(8,128)(2,1)} %g_ref.1, bf16[48,1024]{1,0:T(8,128)(2,1)} %copy-done.2, bf16[48,1024]{1,0:T(8,128)(2,1)} %copy-done.3, ...), custom_call_target="tpu_custom_call" | custom-call | flops 12650000384 | bytes 1048576 | tf_op jit(solution)/shard_map/pallas_call | solution.py:180
  26.6 8.4 %all-to-all-start = ((bf16[8,400,128]{2,1,0:T(8,128)(2,1)}), bf16[8,400,128]{2,1,0:T(8,128)(2,1)S(1)}, u32[]{:S(2)}, u32[]{:S(2)}) async-start(bf16[8,400,128]{2,1,0:T(8,128)(2,1)} %get-tuple-element.48), calls=%async_computation | async-start | bytes 1638400 | tf_op jit(solution)/shard_map/all_to_all | solution.py:460
  36.4 6.3 %collective-permute-done.5 = bf16[1088,128]{1,0:T(8,128)(2,1)S(1)} collective-permute-done((bf16[1088,128]{1,0:T(8,128)(2,1)S(1)}, bf16[1088,128]{1,0:T(8,128)(2,1)S(1)}, u32[]{:S(2)}, u32[]{:S(2)}) %collective-permute-start.5) | collective-permute-done | bytes 278560 | tf_op jit(solution)/shard_map/ppermute | solution.py:399
  44.3 2.6 %collective-permute-start.7 = (bf16[272,128]{1,0:T(8,128)(2,1)S(1)}, bf16[272,128]{1,0:T(8,128)(2,1)S(1)}, u32[]{:S(2)}, u32[]{:S(2)}) collective-permute-start(bf16[272,128]{1,0:T(8,128)(2,1)S(1)} %get-tuple-element.92), channel_id=1, source_target_pairs={{0,128},{32,160},{64,192},{96,224},{128,0},{160,32},{192,64},{224,... | collective-permute-start | bytes 208904 | tf_op jit(solution)/shard_map/ppermute | solution.py:399
  46.9 2.7 %collective-permute-done.7 = bf16[272,128]{1,0:T(8,128)(2,1)S(1)} collective-permute-done((bf16[272,128]{1,0:T(8,128)(2,1)S(1)}, bf16[272,128]{1,0:T(8,128)(2,1)S(1)}, u32[]{:S(2)}, u32[]{:S(2)}) %collective-permute-start.7) | collective-permute-done | bytes 69664 | tf_op jit(solution)/shard_map/ppermute | solution.py:399
  49.6 2.7 %collective-permute-done.8 = bf16[272,128]{1,0:T(8,128)(2,1)S(1)} collective-permute-done((bf16[272,128]{1,0:T(8,128)(2,1)S(1)}, bf16[272,128]{1,0:T(8,128)(2,1)S(1)}, u32[]{:S(2)}, u32[]{:S(2)}) %collective-permute-start.8) | collective-permute-done | bytes 69664 | tf_op jit(solution)/shard_map/ppermute | solution.py:399
  52.3 2.5 %collective-permute-start.10 = (bf16[272,128]{1,0:T(8,128)(2,1)S(1)}, bf16[272,128]{1,0:T(8,128)(2,1)S(1)}, u32[]{:S(2)}, u32[]{:S(2)}) collective-permute-start(bf16[272,128]{1,0:T(8,128)(2,1)S(1)} %fusion.3), channel_id=1, source_target_pairs={{0,16},{2,18},{4,20},{6,22},{8,24},{10,26},{12,28},{14,30},{16,0},... | collective-permute-start | bytes 208904 | tf_op jit(solution)/shard_map/ppermute | solution.py:399
  56.6 2.7 %all-to-all-done = bf16[8,400,128]{2,1,0:T(8,128)(2,1)S(1)} async-done(((bf16[8,400,128]{2,1,0:T(8,128)(2,1)}), bf16[8,400,128]{2,1,0:T(8,128)(2,1)S(1)}, u32[]{:S(2)}, u32[]{:S(2)}) %all-to-all-start) | async-done | bytes 819232 | tf_op jit(solution)/shard_map/all_to_all | solution.py:460
  60.3 2.5 %collective-permute-start.3 = (bf16[8,192,128]{2,1,0:T(8,128)(2,1)S(1)}, bf16[8,192,128]{2,1,0:T(8,128)(2,1)S(1)}, u32[]{:S(2)}, u32[]{:S(2)}) collective-permute-start(bf16[8,192,128]{2,1,0:T(8,128)(2,1)S(1)} %slice.9.x_ref), channel_id=1, source_target_pairs={{0,16},{16,0},{1,17},{17,1},{2,18},{18,2},{3,19},{19,3},{4,20},{20... | collective-permute-start | bytes 1179656 | tf_op jit(solution)/shard_map/ppermute | solution.py:446
  64.1 6.3 %shard_map.151 = (f32[64,1536]{1,0:T(8,128)S(1)}, f32[1536,64]{1,0:T(8,128)S(1)}, f32[1536,64]{1,0:T(8,128)S(1)}) custom-call(bf16[1536,64]{1,0:T(8,128)(2,1)S(1)} %get-tuple-element.58.q, bf16[1536,64]{1,0:T(8,128)(2,1)S(1)} %get-tuple-element.59.do, f32[8,1536]{1,0:T(8,128)S(1)} %get-tuple-element.60.st, bf16[1536,64]{1,0:T(8,128)(2,1)S(1)} %get-tuple-element.52.k, ...), custom_call_target="tpu_custom_call" | custom-call | flops 8049999872 | bytes 1048576 | tf_op jit(solution)/shard_map/pallas_call | solution.py:358
  70.5 2.4 %collective-permute-start.12 = (bf16[272,128]{1,0:T(8,128)(2,1)S(1)}, bf16[272,128]{1,0:T(8,128)(2,1)S(1)}, u32[]{:S(2)}, u32[]{:S(2)}) collective-permute-start(bf16[272,128]{1,0:T(8,128)(2,1)S(1)} %add_convert_fusion.2), channel_id=1, source_target_pairs={{0,4},{2,6},{4,0},{6,2},{8,12},{10,14},{12,8},{14,10},{16,20},{18,... | collective-permute-start | bytes 208904 | tf_op jit(solution)/shard_map/ppermute | solution.py:399
  73.9 6.8 %shard_map.152 = (bf16[8,96,128]{2,1,0:T(8,128)(2,1)S(1)}, f32[1536,64]{1,0:T(8,128)S(1)}, f32[1536,64]{1,0:T(8,128)S(1)}) custom-call(bf16[1536,64]{1,0:T(8,128)(2,1)S(1)} %get-tuple-element.58.q, bf16[1536,64]{1,0:T(8,128)(2,1)S(1)} %get-tuple-element.59.do, f32[8,1536]{1,0:T(8,128)S(1)} %get-tuple-element.60.st, ...), custom_call_target="tpu_custom_call" | custom-call | flops 8049999872 | bytes 1048576 | tf_op jit(solution)/shard_map/pallas_call | solution.py:358
  80.7 3.4 %collective-permute-start.13 = (bf16[272,128]{1,0:T(8,128)(2,1)S(1)}, bf16[272,128]{1,0:T(8,128)(2,1)S(1)}, u32[]{:S(2)}, u32[]{:S(2)}) collective-permute-start(bf16[272,128]{1,0:T(8,128)(2,1)S(1)} %add_convert_fusion.1), channel_id=1, source_target_pairs={{0,8},{2,10},{4,12},{6,14},{8,0},{10,2},{12,4},{14,6},{16,24},{18,... | collective-permute-start | bytes 208904 | tf_op jit(solution)/shard_map/ppermute | solution.py:399
  84.3 7.2 %shard_map.153 = (bf16[8,192,128]{2,1,0:T(8,128)(2,1)S(1)}, f32[64,1536]{1,0:T(8,128)S(1)}) custom-call(s32[8]{0:T(128)S(1)} %copy-done, bf16[1536,64]{1,0:T(8,128)(2,1)S(1)} %get-tuple-element.49.q, bf16[1536,64]{1,0:T(8,128)(2,1)S(1)} %get-tuple-element.50.do, f32[8,1536]{1,0:T(8,128)S(1)} %get-tuple-element.51.st, ...), custom_call_target="tpu_custom_call" | custom-call | flops 8049999872 | bytes 1048576 | tf_op jit(solution)/shard_map/pallas_call | solution.py:358
  93.0 2.6 %collective-permute-start.18 = (bf16[272,128]{1,0:T(8,128)(2,1)S(1)}, bf16[272,128]{1,0:T(8,128)(2,1)S(1)}, u32[]{:S(2)}, u32[]{:S(2)}) collective-permute-start(bf16[272,128]{1,0:T(8,128)(2,1)S(1)} %add_convert_fusion), channel_id=1, source_target_pairs={{0,64},{32,96},{64,0},{96,32},{128,192},{160,224},{192,128},{224,1... | collective-permute-start | bytes 208904 | tf_op jit(solution)/shard_map/ppermute | solution.py:399
  95.6 7.5 %shard_map.154 = (bf16[8,96,128]{2,1,0:T(8,128)(2,1)S(1)}, bf16[8,192,128]{2,1,0:T(8,128)(2,1)S(1)}) custom-call(s32[8]{0:T(128)S(1)} %copy-done, bf16[1536,64]{1,0:T(8,128)(2,1)S(1)} %get-tuple-element.49.q, bf16[1536,64]{1,0:T(8,128)(2,1)S(1)} %get-tuple-element.50.do, f32[8,1536]{1,0:T(8,128)S(1)} %get-tuple-element.51.st, ...), custom_call_target="tpu_custom_call" | custom-call | flops 8049999872 | bytes 1048576 | tf_op jit(solution)/shard_map/pallas_call | solution.py:358
  103.1 3.2 %collective-permute-start.15 = (bf16[8,96,128]{2,1,0:T(8,128)(2,1)S(1)}, bf16[8,96,128]{2,1,0:T(8,128)(2,1)S(1)}, u32[]{:S(2)}, u32[]{:S(2)}) collective-permute-start(bf16[8,96,128]{2,1,0:T(8,128)(2,1)S(1)} %get-tuple-element.77), channel_id=1, source_target_pairs={{0,1},{1,0},{2,3},{3,2},{4,5},{5,4},{6,7},{7,6},{8,9},{9,8},{10,11... | collective-permute-start | bytes 589832 | tf_op jit(solution)/shard_map/ppermute | solution.py:446
  108.3 4.0 %all-to-all-start.1 = ((bf16[8,288,128]{2,1,0:T(8,128)(2,1)}), bf16[8,288,128]{2,1,0:T(8,128)(2,1)S(1)}, u32[]{:S(2)}, u32[]{:S(2)}) async-start(bf16[8,288,128]{2,1,0:T(8,128)(2,1)} %shard_map.155), calls=%async_computation.1 | async-start | bytes 1179648 | tf_op jit(solution)/shard_map/all_to_all | solution.py:527
  112.3 2.5 %collective-permute-done.19 = bf16[1088,128]{1,0:T(8,128)(2,1)S(1)} collective-permute-done((bf16[1088,128]{1,0:T(8,128)(2,1)S(1)}, bf16[1088,128]{1,0:T(8,128)(2,1)S(1)}, u32[]{:S(2)}, u32[]{:S(2)}) %collective-permute-start.19) | collective-permute-done | bytes 278560 | tf_op jit(solution)/shard_map/ppermute | solution.py:399
  117.4 2.3 %shard_map.157 = (f32[512,1024]{1,0:T(8,128)}, f32[31,1024]{1,0:T(8,128)}) custom-call(s32[8]{0:T(128)S(1)} %copy-done, bf16[4,544,128]{2,1,0:T(8,128)(2,1)S(1)} %bitcast.27, bf16[4,544,128]{2,1,0:T(8,128)(2,1)S(1)} %collective-permute-done.20.got_ref), custom_call_target="tpu_custom_call" | custom-call | flops 2300000000 | bytes 1048576 | tf_op jit(solution)/shard_map/pallas_call | solution.py:529
  119.6 12.0 %all-to-all-done.1.x_ref = bf16[8,288,128]{2,1,0:T(8,128)(2,1)S(1)} async-done(((bf16[8,288,128]{2,1,0:T(8,128)(2,1)}), bf16[8,288,128]{2,1,0:T(8,128)(2,1)S(1)}, u32[]{:S(2)}, u32[]{:S(2)}) %all-to-all-start.1) | async-done | bytes 589856 | tf_op jit(solution)/shard_map/all_to_all | solution.py:527
  (60 shorter events, 18.9 us)
Async XLA Ops:
  2.2 6.9 %collective-permute-start = (bf16[48,1024]{1,0:T(8,128)(2,1)}, bf16[48,1024]{1,0:T(8,128)(2,1)S(1)}, u32[]{:S(2)}, u32[]{:S(2)}) collective-permute-start(bf16[48,1024]{1,0:T(8,128)(2,1)} %get-tuple-element.46), channel_id=1, source_target_pairs={{0,1},{1,2},{2,3},{3,4},{4,5},{5,6},{6,7},{7,8},{8,9},{9,10},{10,1... | collective-permute-start | bytes 294920 | tf_op jit(solution)/shard_map/ppermute | solution.py:455
  7.1 6.1 %collective-permute-start.1 = (bf16[48,1024]{1,0:T(8,128)(2,1)}, bf16[48,1024]{1,0:T(8,128)(2,1)S(1)}, u32[]{:S(2)}, u32[]{:S(2)}) collective-permute-start(bf16[48,1024]{1,0:T(8,128)(2,1)} %get-tuple-element.47), channel_id=1, source_target_pairs={{1,0},{2,1},{3,2},{4,3},{5,4},{6,5},{7,6},{8,7},{9,8},{10,9},{11,1... | collective-permute-start | bytes 294920 | tf_op jit(solution)/shard_map/ppermute | solution.py:456
  26.5 8.5 %collective-permute-start.4 = (bf16[2176,128]{1,0:T(8,128)(2,1)S(1)}, bf16[2176,128]{1,0:T(8,128)(2,1)S(1)}, u32[]{:S(2)}, u32[]{:S(2)}) collective-permute-start(bf16[2176,128]{1,0:T(8,128)(2,1)S(1)} %dynamic-slice_bitcast_fusion), channel_id=1, source_target_pairs={{0,1},{1,0},{2,3},{3,2},{4,5},{5,4},{6,7},{7,6},{8,9},{9,8},{10,11... | collective-permute-start | bytes 1671176 | tf_op jit(solution)/shard_map/ppermute | solution.py:446
  26.6 32.7 %all-to-all-start = ((bf16[8,400,128]{2,1,0:T(8,128)(2,1)}), bf16[8,400,128]{2,1,0:T(8,128)(2,1)S(1)}, u32[]{:S(2)}, u32[]{:S(2)}) async-start(bf16[8,400,128]{2,1,0:T(8,128)(2,1)} %get-tuple-element.48), calls=%async_computation | async-start | bytes 1638400 | tf_op jit(solution)/shard_map/all_to_all | solution.py:460
  35.2 7.5 %collective-permute-start.5 = (bf16[1088,128]{1,0:T(8,128)(2,1)S(1)}, bf16[1088,128]{1,0:T(8,128)(2,1)S(1)}, u32[]{:S(2)}, u32[]{:S(2)}) collective-permute-start(bf16[1088,128]{1,0:T(8,128)(2,1)S(1)} %dynamic-slice_bitcast_fusion.1), channel_id=1, source_target_pairs={{0,32},{32,0},{64,96},{96,64},{128,160},{160,128},{192,224},{224,1... | collective-permute-start | bytes 835592 | tf_op jit(solution)/shard_map/ppermute | solution.py:399
  36.4 22.9 %copy-start = (s32[8]{0:T(128)S(1)}, s32[8]{0:T(128)}, u32[]{:S(2)}) copy-start(s32[8]{0:T(128)} %lengths_ref.11) | copy-start | bytes 100
  42.9 4.0 %collective-permute-start.6 = (bf16[272,128]{1,0:T(8,128)(2,1)S(1)}, bf16[272,128]{1,0:T(8,128)(2,1)S(1)}, u32[]{:S(2)}, u32[]{:S(2)}) collective-permute-start(bf16[272,128]{1,0:T(8,128)(2,1)S(1)} %get-tuple-element.90), channel_id=1, source_target_pairs={{0,64},{32,96},{64,0},{96,32},{128,192},{160,224},{192,128},{224,1... | collective-permute-start | bytes 208904 | tf_op jit(solution)/shard_map/ppermute | solution.py:399
  44.3 5.4 %collective-permute-start.7 = (bf16[272,128]{1,0:T(8,128)(2,1)S(1)}, bf16[272,128]{1,0:T(8,128)(2,1)S(1)}, u32[]{:S(2)}, u32[]{:S(2)}) collective-permute-start(bf16[272,128]{1,0:T(8,128)(2,1)S(1)} %get-tuple-element.92), channel_id=1, source_target_pairs={{0,128},{32,160},{64,192},{96,224},{128,0},{160,32},{192,64},{224,... | collective-permute-start | bytes 208904 | tf_op jit(solution)/shard_map/ppermute | solution.py:399
  46.9 5.4 %collective-permute-start.8 = (bf16[272,128]{1,0:T(8,128)(2,1)S(1)}, bf16[272,128]{1,0:T(8,128)(2,1)S(1)}, u32[]{:S(2)}, u32[]{:S(2)}) collective-permute-start(bf16[272,128]{1,0:T(8,128)(2,1)S(1)} %get-tuple-element.91), channel_id=1, source_target_pairs={{0,192},{32,224},{64,128},{96,160},{128,64},{160,96},{192,0},{224,... | collective-permute-start | bytes 208904 | tf_op jit(solution)/shard_map/ppermute | solution.py:399
  52.3 18.1 %collective-permute-start.10 = (bf16[272,128]{1,0:T(8,128)(2,1)S(1)}, bf16[272,128]{1,0:T(8,128)(2,1)S(1)}, u32[]{:S(2)}, u32[]{:S(2)}) collective-permute-start(bf16[272,128]{1,0:T(8,128)(2,1)S(1)} %fusion.3), channel_id=1, source_target_pairs={{0,16},{2,18},{4,20},{6,22},{8,24},{10,26},{12,28},{14,30},{16,0},... | collective-permute-start | bytes 208904 | tf_op jit(solution)/shard_map/ppermute | solution.py:399
  54.8 15.7 %collective-permute-start.11 = (bf16[272,128]{1,0:T(8,128)(2,1)S(1)}, bf16[272,128]{1,0:T(8,128)(2,1)S(1)}, u32[]{:S(2)}, u32[]{:S(2)}) collective-permute-start(bf16[272,128]{1,0:T(8,128)(2,1)S(1)} %fusion.3), channel_id=1, source_target_pairs={{0,18},{2,16},{4,22},{6,20},{8,26},{10,24},{12,30},{14,28},{16,2},... | collective-permute-start | bytes 208904 | tf_op jit(solution)/shard_map/ppermute | solution.py:399
  56.2 14.2 %collective-permute-start.9 = (bf16[272,128]{1,0:T(8,128)(2,1)S(1)}, bf16[272,128]{1,0:T(8,128)(2,1)S(1)}, u32[]{:S(2)}, u32[]{:S(2)}) collective-permute-start(bf16[272,128]{1,0:T(8,128)(2,1)S(1)} %fusion.3), channel_id=1, source_target_pairs={{0,2},{2,0},{4,6},{6,4},{8,10},{10,8},{12,14},{14,12},{16,18},{18,... | collective-permute-start | bytes 208904 | tf_op jit(solution)/shard_map/ppermute | solution.py:399
  60.3 12.6 %collective-permute-start.3 = (bf16[8,192,128]{2,1,0:T(8,128)(2,1)S(1)}, bf16[8,192,128]{2,1,0:T(8,128)(2,1)S(1)}, u32[]{:S(2)}, u32[]{:S(2)}) collective-permute-start(bf16[8,192,128]{2,1,0:T(8,128)(2,1)S(1)} %slice.9.x_ref), channel_id=1, source_target_pairs={{0,16},{16,0},{1,17},{17,1},{2,18},{18,2},{3,19},{19,3},{4,20},{20... | collective-permute-start | bytes 1179656 | tf_op jit(solution)/shard_map/ppermute | solution.py:446
  63.1 21.0 %collective-permute-start.2 = (bf16[8,208,128]{2,1,0:T(8,128)(2,1)S(1)}, bf16[8,208,128]{2,1,0:T(8,128)(2,1)S(1)}, u32[]{:S(2)}, u32[]{:S(2)}) collective-permute-start(bf16[8,208,128]{2,1,0:T(8,128)(2,1)S(1)} %slice.8.x_ref), channel_id=1, source_target_pairs={{0,1},{1,0},{2,3},{3,2},{4,5},{5,4},{6,7},{7,6},{8,9},{9,8},{10,11... | collective-permute-start | bytes 1277960 | tf_op jit(solution)/shard_map/ppermute | solution.py:446
  70.5 10.1 %collective-permute-start.12 = (bf16[272,128]{1,0:T(8,128)(2,1)S(1)}, bf16[272,128]{1,0:T(8,128)(2,1)S(1)}, u32[]{:S(2)}, u32[]{:S(2)}) collective-permute-start(bf16[272,128]{1,0:T(8,128)(2,1)S(1)} %add_convert_fusion.2), channel_id=1, source_target_pairs={{0,4},{2,6},{4,0},{6,2},{8,12},{10,14},{12,8},{14,10},{16,20},{18,... | collective-permute-start | bytes 208904 | tf_op jit(solution)/shard_map/ppermute | solution.py:399
  80.7 11.5 %collective-permute-start.13 = (bf16[272,128]{1,0:T(8,128)(2,1)S(1)}, bf16[272,128]{1,0:T(8,128)(2,1)S(1)}, u32[]{:S(2)}, u32[]{:S(2)}) collective-permute-start(bf16[272,128]{1,0:T(8,128)(2,1)S(1)} %add_convert_fusion.1), channel_id=1, source_target_pairs={{0,8},{2,10},{4,12},{6,14},{8,0},{10,2},{12,4},{14,6},{16,24},{18,... | collective-permute-start | bytes 208904 | tf_op jit(solution)/shard_map/ppermute | solution.py:399
  91.5 15.8 %collective-permute-start.14 = (bf16[8,192,128]{2,1,0:T(8,128)(2,1)S(1)}, bf16[8,192,128]{2,1,0:T(8,128)(2,1)S(1)}, u32[]{:S(2)}, u32[]{:S(2)}) collective-permute-start(bf16[8,192,128]{2,1,0:T(8,128)(2,1)S(1)} %get-tuple-element.75), channel_id=1, source_target_pairs={{0,16},{16,0},{1,17},{17,1},{2,18},{18,2},{3,19},{19,3},{4,20},{20... | collective-permute-start | bytes 1179656 | tf_op jit(solution)/shard_map/ppermute | solution.py:446
  92.2 14.1 %collective-permute-start.16 = (bf16[272,128]{1,0:T(8,128)(2,1)S(1)}, bf16[272,128]{1,0:T(8,128)(2,1)S(1)}, u32[]{:S(2)}, u32[]{:S(2)}) collective-permute-start(bf16[272,128]{1,0:T(8,128)(2,1)S(1)} %add_convert_fusion), channel_id=1, source_target_pairs={{0,192},{32,224},{64,128},{96,160},{128,64},{160,96},{192,0},{224,... | collective-permute-start | bytes 208904 | tf_op jit(solution)/shard_map/ppermute | solution.py:399
  92.6 13.7 %collective-permute-start.17 = (bf16[272,128]{1,0:T(8,128)(2,1)S(1)}, bf16[272,128]{1,0:T(8,128)(2,1)S(1)}, u32[]{:S(2)}, u32[]{:S(2)}) collective-permute-start(bf16[272,128]{1,0:T(8,128)(2,1)S(1)} %add_convert_fusion), channel_id=1, source_target_pairs={{0,128},{32,160},{64,192},{96,224},{128,0},{160,32},{192,64},{224,... | collective-permute-start | bytes 208904 | tf_op jit(solution)/shard_map/ppermute | solution.py:399
  93.0 13.3 %collective-permute-start.18 = (bf16[272,128]{1,0:T(8,128)(2,1)S(1)}, bf16[272,128]{1,0:T(8,128)(2,1)S(1)}, u32[]{:S(2)}, u32[]{:S(2)}) collective-permute-start(bf16[272,128]{1,0:T(8,128)(2,1)S(1)} %add_convert_fusion), channel_id=1, source_target_pairs={{0,64},{32,96},{64,0},{96,32},{128,192},{160,224},{192,128},{224,1... | collective-permute-start | bytes 208904 | tf_op jit(solution)/shard_map/ppermute | solution.py:399
  103.1 4.3 %collective-permute-start.15 = (bf16[8,96,128]{2,1,0:T(8,128)(2,1)S(1)}, bf16[8,96,128]{2,1,0:T(8,128)(2,1)S(1)}, u32[]{:S(2)}, u32[]{:S(2)}) collective-permute-start(bf16[8,96,128]{2,1,0:T(8,128)(2,1)S(1)} %get-tuple-element.77), channel_id=1, source_target_pairs={{0,1},{1,0},{2,3},{3,2},{4,5},{5,4},{6,7},{7,6},{8,9},{9,8},{10,11... | collective-permute-start | bytes 589832 | tf_op jit(solution)/shard_map/ppermute | solution.py:446
  106.5 8.3 %collective-permute-start.19 = (bf16[1088,128]{1,0:T(8,128)(2,1)S(1)}, bf16[1088,128]{1,0:T(8,128)(2,1)S(1)}, u32[]{:S(2)}, u32[]{:S(2)}) collective-permute-start(bf16[1088,128]{1,0:T(8,128)(2,1)S(1)} %pad_maximum_fusion.1), channel_id=1, source_target_pairs={{0,32},{32,0},{64,96},{96,64},{128,160},{160,128},{192,224},{224,1... | collective-permute-start | bytes 835592 | tf_op jit(solution)/shard_map/ppermute | solution.py:399
  108.3 23.3 %all-to-all-start.1 = ((bf16[8,288,128]{2,1,0:T(8,128)(2,1)}), bf16[8,288,128]{2,1,0:T(8,128)(2,1)S(1)}, u32[]{:S(2)}, u32[]{:S(2)}) async-start(bf16[8,288,128]{2,1,0:T(8,128)(2,1)} %shard_map.155), calls=%async_computation.1 | async-start | bytes 1179648 | tf_op jit(solution)/shard_map/all_to_all | solution.py:527
  114.9 2.5 %collective-permute-start.20 = (bf16[4,544,128]{2,1,0:T(8,128)(2,1)S(1)}, bf16[4,544,128]{2,1,0:T(8,128)(2,1)S(1)}, u32[]{:S(2)}, u32[]{:S(2)}) collective-permute-start(bf16[4,544,128]{2,1,0:T(8,128)(2,1)S(1)} %bitcast.26), channel_id=1, source_target_pairs={{0,1},{1,0},{2,3},{3,2},{4,5},{5,4},{6,7},{7,6},{8,9},{9,8},{10,11... | collective-permute-start | bytes 1671176 | tf_op jit(solution)/shard_map/ppermute | solution.py:446
  (3 other events, 14.6 us)

commit v6 on v5

--- a/solution.py
+++ b/solution.py
@@ -18,7 +18,7 @@
 HSIZE = 64
 TAPS = 31
 FREE = 60
-WIDTH = 512
+WIDTH = 1024
 ALL = ("dp", "xh", "z", "core")
 SEQ = ("xh", "z", "core")
 

time: 133 us -> 133 us (level)
  no operation moved by 1% of the time
where the time goes in v6:
time: 133 us
  Pallas kernels  47.2 us (35%)
  starting transfers between devices  47 us (35%)
  waiting for transfers between devices  34.9 us (26%)
  local copies, waits for them, and re-layouts  1.94 us (1%)
    pallas_call x4, Pallas kernels, tile_call(): call(body, outs, 7, 40, grid=(1,), in_specs=specs, out_specs=tuple((whole...  27.9 us
    ppermute x13, starting transfers between devices, flip(): return lax.ppermute(x, axis, [(i, i ^ mask) for i in range(size)])  19.3 us
    ppermute x13, waiting for transfers between devices, flip(): return lax.ppermute(x, axis, [(i, i ^ mask) for i in range(size)])  14.2 us
    all_to_all x1, waiting for transfers between devices, shards(): back = lax.all_to_all(back, 'z', 0, 0, tiled=True)  12.1 us
    pallas_call x1, Pallas kernels, conv_call(): pl.pallas_call(conv_kernel, out_shape=(sds((1, ROWS, 1024)), sds((8, 544,...  11 us
    all_to_all x1, starting transfers between devices, shards(): pay = lax.all_to_all(pay, 'z', 0, 0, tiled=True)  8.4 us
    ppermute x6, starting transfers between devices, swap(): return lax.ppermute(x, axis, [(0, 1), (1, 0)])  8.37 us
    ppermute x1, starting transfers between devices, shards(): lo = lax.ppermute(last, SEQ, up)  4.92 us
  transfers between devices with their start and end apart: 23, of which 9 were waited for; matrix products, arithmetic and copies ran while one was open for 1% of the time, Pallas kernels for 25%

profile of v6, /device:TPU:1, one launch (start us, length us, event | category | flops | bytes accessed | tf_op | source)
XLA Modules:
  0.0 132.5 jit_solution(14088580646591479321)
XLA Ops:
  2.2 4.9 %collective-permute-start = (bf16[48,1024]{1,0:T(8,128)(2,1)}, bf16[48,1024]{1,0:T(8,128)(2,1)S(1)}, u32[]{:S(2)}, u32[]{:S(2)}) collective-permute-start(bf16[48,1024]{1,0:T(8,128)(2,1)} %get-tuple-element.46), channel_id=1, source_target_pairs={{0,1},{1,2},{2,3},{3,4},{4,5},{5,6},{6,7},{7,8},{8,9},{9,10},{10,1... | collective-permute-start | bytes 294920 | tf_op jit(solution)/shard_map/ppermute | solution.py:455
  7.1 1.9 %collective-permute-start.1 = (bf16[48,1024]{1,0:T(8,128)(2,1)}, bf16[48,1024]{1,0:T(8,128)(2,1)S(1)}, u32[]{:S(2)}, u32[]{:S(2)}) collective-permute-start(bf16[48,1024]{1,0:T(8,128)(2,1)} %get-tuple-element.47), channel_id=1, source_target_pairs={{1,0},{2,1},{3,2},{4,3},{5,4},{6,5},{7,6},{8,7},{9,8},{10,9},{11,1... | collective-permute-start | bytes 294920 | tf_op jit(solution)/shard_map/ppermute | solution.py:456
  9.1 4.2 %collective-permute-done.1.hi_ref = bf16[48,1024]{1,0:T(8,128)(2,1)S(1)} collective-permute-done((bf16[48,1024]{1,0:T(8,128)(2,1)}, bf16[48,1024]{1,0:T(8,128)(2,1)S(1)}, u32[]{:S(2)}, u32[]{:S(2)}) %collective-permute-start.1) | collective-permute-done | bytes 98336 | tf_op jit(solution)/shard_map/ppermute | solution.py:456
  13.9 11.0 %shard_map.146 = (bf16[1,192,1024]{2,1,0:T(8,128)(2,1)}, bf16[8,544,128]{2,1,0:T(8,128)(2,1)}, bf16[8,400,128]{2,1,0:T(8,128)(2,1)}) custom-call(s32[8]{0:T(128)} %lengths_ref.11, bf16[1,192,1024]{2,1,0:T(8,128)(2,1)} %x_ref.1, bf16[1,192,1024]{2,1,0:T(8,128)(2,1)} %g_ref.1, bf16[48,1024]{1,0:T(8,128)(2,1)} %copy-done.2, bf16[48,1024]{1,0:T(8,128)(2,1)} %copy-done.3, ...), custom_call_target="tpu_custom_call" | custom-call | flops 12650000384 | bytes 1048576 | tf_op jit(solution)/shard_map/pallas_call | solution.py:180
  26.2 8.4 %all-to-all-start = ((bf16[8,400,128]{2,1,0:T(8,128)(2,1)}), bf16[8,400,128]{2,1,0:T(8,128)(2,1)S(1)}, u32[]{:S(2)}, u32[]{:S(2)}) async-start(bf16[8,400,128]{2,1,0:T(8,128)(2,1)} %get-tuple-element.48), calls=%async_computation | async-start | bytes 1638400 | tf_op jit(solution)/shard_map/all_to_all | solution.py:460
  36.0 6.3 %collective-permute-done.5 = bf16[1088,128]{1,0:T(8,128)(2,1)S(1)} collective-permute-done((bf16[1088,128]{1,0:T(8,128)(2,1)S(1)}, bf16[1088,128]{1,0:T(8,128)(2,1)S(1)}, u32[]{:S(2)}, u32[]{:S(2)}) %collective-permute-start.5) | collective-permute-done | bytes 278560 | tf_op jit(solution)/shard_map/ppermute | solution.py:399
  43.8 2.6 %collective-permute-start.7 = (bf16[272,128]{1,0:T(8,128)(2,1)S(1)}, bf16[272,128]{1,0:T(8,128)(2,1)S(1)}, u32[]{:S(2)}, u32[]{:S(2)}) collective-permute-start(bf16[272,128]{1,0:T(8,128)(2,1)S(1)} %get-tuple-element.92), channel_id=1, source_target_pairs={{0,128},{32,160},{64,192},{96,224},{128,0},{160,32},{192,64},{224,... | collective-permute-start | bytes 208904 | tf_op jit(solution)/shard_map/ppermute | solution.py:399
  46.5 2.7 %collective-permute-done.7 = bf16[272,128]{1,0:T(8,128)(2,1)S(1)} collective-permute-done((bf16[272,128]{1,0:T(8,128)(2,1)S(1)}, bf16[272,128]{1,0:T(8,128)(2,1)S(1)}, u32[]{:S(2)}, u32[]{:S(2)}) %collective-permute-start.7) | collective-permute-done | bytes 69664 | tf_op jit(solution)/shard_map/ppermute | solution.py:399
  49.2 2.7 %collective-permute-done.8 = bf16[272,128]{1,0:T(8,128)(2,1)S(1)} collective-permute-done((bf16[272,128]{1,0:T(8,128)(2,1)S(1)}, bf16[272,128]{1,0:T(8,128)(2,1)S(1)}, u32[]{:S(2)}, u32[]{:S(2)}) %collective-permute-start.8) | collective-permute-done | bytes 69664 | tf_op jit(solution)/shard_map/ppermute | solution.py:399
  51.9 2.5 %collective-permute-start.10 = (bf16[272,128]{1,0:T(8,128)(2,1)S(1)}, bf16[272,128]{1,0:T(8,128)(2,1)S(1)}, u32[]{:S(2)}, u32[]{:S(2)}) collective-permute-start(bf16[272,128]{1,0:T(8,128)(2,1)S(1)} %fusion.3), channel_id=1, source_target_pairs={{0,16},{2,18},{4,20},{6,22},{8,24},{10,26},{12,28},{14,30},{16,0},... | collective-permute-start | bytes 208904 | tf_op jit(solution)/shard_map/ppermute | solution.py:399
  56.2 2.7 %all-to-all-done = bf16[8,400,128]{2,1,0:T(8,128)(2,1)S(1)} async-done(((bf16[8,400,128]{2,1,0:T(8,128)(2,1)}), bf16[8,400,128]{2,1,0:T(8,128)(2,1)S(1)}, u32[]{:S(2)}, u32[]{:S(2)}) %all-to-all-start) | async-done | bytes 819232 | tf_op jit(solution)/shard_map/all_to_all | solution.py:460
  59.9 2.5 %collective-permute-start.3 = (bf16[8,192,128]{2,1,0:T(8,128)(2,1)S(1)}, bf16[8,192,128]{2,1,0:T(8,128)(2,1)S(1)}, u32[]{:S(2)}, u32[]{:S(2)}) collective-permute-start(bf16[8,192,128]{2,1,0:T(8,128)(2,1)S(1)} %slice.9.x_ref), channel_id=1, source_target_pairs={{0,16},{16,0},{1,17},{17,1},{2,18},{18,2},{3,19},{19,3},{4,20},{20... | collective-permute-start | bytes 1179656 | tf_op jit(solution)/shard_map/ppermute | solution.py:446
  63.5 6.3 %shard_map.151 = (f32[64,1536]{1,0:T(8,128)S(1)}, f32[1536,64]{1,0:T(8,128)S(1)}, f32[1536,64]{1,0:T(8,128)S(1)}) custom-call(bf16[1536,64]{1,0:T(8,128)(2,1)S(1)} %get-tuple-element.58.q, bf16[1536,64]{1,0:T(8,128)(2,1)S(1)} %get-tuple-element.59.do, f32[8,1536]{1,0:T(8,128)S(1)} %get-tuple-element.60.st, bf16[1536,64]{1,0:T(8,128)(2,1)S(1)} %get-tuple-element.52.k, ...), custom_call_target="tpu_custom_call" | custom-call | flops 8049999872 | bytes 1048576 | tf_op jit(solution)/shard_map/pallas_call | solution.py:358
  70.0 2.4 %collective-permute-start.12 = (bf16[272,128]{1,0:T(8,128)(2,1)S(1)}, bf16[272,128]{1,0:T(8,128)(2,1)S(1)}, u32[]{:S(2)}, u32[]{:S(2)}) collective-permute-start(bf16[272,128]{1,0:T(8,128)(2,1)S(1)} %add_convert_fusion.2), channel_id=1, source_target_pairs={{0,4},{2,6},{4,0},{6,2},{8,12},{10,14},{12,8},{14,10},{16,20},{18,... | collective-permute-start | bytes 208904 | tf_op jit(solution)/shard_map/ppermute | solution.py:399
  73.3 6.8 %shard_map.152 = (bf16[8,96,128]{2,1,0:T(8,128)(2,1)S(1)}, f32[1536,64]{1,0:T(8,128)S(1)}, f32[1536,64]{1,0:T(8,128)S(1)}) custom-call(bf16[1536,64]{1,0:T(8,128)(2,1)S(1)} %get-tuple-element.58.q, bf16[1536,64]{1,0:T(8,128)(2,1)S(1)} %get-tuple-element.59.do, f32[8,1536]{1,0:T(8,128)S(1)} %get-tuple-element.60.st, ...), custom_call_target="tpu_custom_call" | custom-call | flops 8049999872 | bytes 1048576 | tf_op jit(solution)/shard_map/pallas_call | solution.py:358
  80.1 3.4 %collective-permute-start.13 = (bf16[272,128]{1,0:T(8,128)(2,1)S(1)}, bf16[272,128]{1,0:T(8,128)(2,1)S(1)}, u32[]{:S(2)}, u32[]{:S(2)}) collective-permute-start(bf16[272,128]{1,0:T(8,128)(2,1)S(1)} %add_convert_fusion.1), channel_id=1, source_target_pairs={{0,8},{2,10},{4,12},{6,14},{8,0},{10,2},{12,4},{14,6},{16,24},{18,... | collective-permute-start | bytes 208904 | tf_op jit(solution)/shard_map/ppermute | solution.py:399
  83.7 7.2 %shard_map.153 = (bf16[8,192,128]{2,1,0:T(8,128)(2,1)S(1)}, f32[64,1536]{1,0:T(8,128)S(1)}) custom-call(s32[8]{0:T(128)S(1)} %copy-done, bf16[1536,64]{1,0:T(8,128)(2,1)S(1)} %get-tuple-element.49.q, bf16[1536,64]{1,0:T(8,128)(2,1)S(1)} %get-tuple-element.50.do, f32[8,1536]{1,0:T(8,128)S(1)} %get-tuple-element.51.st, ...), custom_call_target="tpu_custom_call" | custom-call | flops 8049999872 | bytes 1048576 | tf_op jit(solution)/shard_map/pallas_call | solution.py:358
  92.7 2.3 %collective-permute-start.18 = (bf16[272,128]{1,0:T(8,128)(2,1)S(1)}, bf16[272,128]{1,0:T(8,128)(2,1)S(1)}, u32[]{:S(2)}, u32[]{:S(2)}) collective-permute-start(bf16[272,128]{1,0:T(8,128)(2,1)S(1)} %add_convert_fusion), channel_id=1, source_target_pairs={{0,64},{32,96},{64,0},{96,32},{128,192},{160,224},{192,128},{224,1... | collective-permute-start | bytes 208904 | tf_op jit(solution)/shard_map/ppermute | solution.py:399
  95.0 7.5 %shard_map.154 = (bf16[8,96,128]{2,1,0:T(8,128)(2,1)S(1)}, bf16[8,192,128]{2,1,0:T(8,128)(2,1)S(1)}) custom-call(s32[8]{0:T(128)S(1)} %copy-done, bf16[1536,64]{1,0:T(8,128)(2,1)S(1)} %get-tuple-element.49.q, bf16[1536,64]{1,0:T(8,128)(2,1)S(1)} %get-tuple-element.50.do, f32[8,1536]{1,0:T(8,128)S(1)} %get-tuple-element.51.st, ...), custom_call_target="tpu_custom_call" | custom-call | flops 8049999872 | bytes 1048576 | tf_op jit(solution)/shard_map/pallas_call | solution.py:358
  102.5 3.4 %collective-permute-start.15 = (bf16[8,96,128]{2,1,0:T(8,128)(2,1)S(1)}, bf16[8,96,128]{2,1,0:T(8,128)(2,1)S(1)}, u32[]{:S(2)}, u32[]{:S(2)}) collective-permute-start(bf16[8,96,128]{2,1,0:T(8,128)(2,1)S(1)} %get-tuple-element.77), channel_id=1, source_target_pairs={{0,1},{1,0},{2,3},{3,2},{4,5},{5,4},{6,7},{7,6},{8,9},{9,8},{10,11... | collective-permute-start | bytes 589832 | tf_op jit(solution)/shard_map/ppermute | solution.py:446
  107.9 4.1 %all-to-all-start.1 = ((bf16[8,288,128]{2,1,0:T(8,128)(2,1)}), bf16[8,288,128]{2,1,0:T(8,128)(2,1)S(1)}, u32[]{:S(2)}, u32[]{:S(2)}) async-start(bf16[8,288,128]{2,1,0:T(8,128)(2,1)} %shard_map.155), calls=%async_computation.1 | async-start | bytes 1179648 | tf_op jit(solution)/shard_map/all_to_all | solution.py:527
  112.0 2.4 %collective-permute-done.19 = bf16[1088,128]{1,0:T(8,128)(2,1)S(1)} collective-permute-done((bf16[1088,128]{1,0:T(8,128)(2,1)S(1)}, bf16[1088,128]{1,0:T(8,128)(2,1)S(1)}, u32[]{:S(2)}, u32[]{:S(2)}) %collective-permute-start.19) | collective-permute-done | bytes 278560 | tf_op jit(solution)/shard_map/ppermute | solution.py:399
  117.0 2.3 %shard_map.157 = (f32[512,1024]{1,0:T(8,128)}, f32[31,1024]{1,0:T(8,128)}) custom-call(s32[8]{0:T(128)S(1)} %copy-done, bf16[4,544,128]{2,1,0:T(8,128)(2,1)S(1)} %bitcast.27, bf16[4,544,128]{2,1,0:T(8,128)(2,1)S(1)} %collective-permute-done.20.got_ref), custom_call_target="tpu_custom_call" | custom-call | flops 2300000000 | bytes 1048576 | tf_op jit(solution)/shard_map/pallas_call | solution.py:529
  119.2 12.1 %all-to-all-done.1.x_ref = bf16[8,288,128]{2,1,0:T(8,128)(2,1)S(1)} async-done(((bf16[8,288,128]{2,1,0:T(8,128)(2,1)}), bf16[8,288,128]{2,1,0:T(8,128)(2,1)S(1)}, u32[]{:S(2)}, u32[]{:S(2)}) %all-to-all-start.1) | async-done | bytes 589856 | tf_op jit(solution)/shard_map/all_to_all | solution.py:527
  (60 shorter events, 19.1 us)
Async XLA Ops:
  2.2 6.9 %collective-permute-start = (bf16[48,1024]{1,0:T(8,128)(2,1)}, bf16[48,1024]{1,0:T(8,128)(2,1)S(1)}, u32[]{:S(2)}, u32[]{:S(2)}) collective-permute-start(bf16[48,1024]{1,0:T(8,128)(2,1)} %get-tuple-element.46), channel_id=1, source_target_pairs={{0,1},{1,2},{2,3},{3,4},{4,5},{5,6},{6,7},{7,8},{8,9},{9,10},{10,1... | collective-permute-start | bytes 294920 | tf_op jit(solution)/shard_map/ppermute | solution.py:455
  7.1 6.1 %collective-permute-start.1 = (bf16[48,1024]{1,0:T(8,128)(2,1)}, bf16[48,1024]{1,0:T(8,128)(2,1)S(1)}, u32[]{:S(2)}, u32[]{:S(2)}) collective-permute-start(bf16[48,1024]{1,0:T(8,128)(2,1)} %get-tuple-element.47), channel_id=1, source_target_pairs={{1,0},{2,1},{3,2},{4,3},{5,4},{6,5},{7,6},{8,7},{9,8},{10,9},{11,1... | collective-permute-start | bytes 294920 | tf_op jit(solution)/shard_map/ppermute | solution.py:456
  26.1 8.5 %collective-permute-start.4 = (bf16[2176,128]{1,0:T(8,128)(2,1)S(1)}, bf16[2176,128]{1,0:T(8,128)(2,1)S(1)}, u32[]{:S(2)}, u32[]{:S(2)}) collective-permute-start(bf16[2176,128]{1,0:T(8,128)(2,1)S(1)} %dynamic-slice_bitcast_fusion), channel_id=1, source_target_pairs={{0,1},{1,0},{2,3},{3,2},{4,5},{5,4},{6,7},{7,6},{8,9},{9,8},{10,11... | collective-permute-start | bytes 1671176 | tf_op jit(solution)/shard_map/ppermute | solution.py:446
  26.2 32.7 %all-to-all-start = ((bf16[8,400,128]{2,1,0:T(8,128)(2,1)}), bf16[8,400,128]{2,1,0:T(8,128)(2,1)S(1)}, u32[]{:S(2)}, u32[]{:S(2)}) async-start(bf16[8,400,128]{2,1,0:T(8,128)(2,1)} %get-tuple-element.48), calls=%async_computation | async-start | bytes 1638400 | tf_op jit(solution)/shard_map/all_to_all | solution.py:460
  34.8 7.5 %collective-permute-start.5 = (bf16[1088,128]{1,0:T(8,128)(2,1)S(1)}, bf16[1088,128]{1,0:T(8,128)(2,1)S(1)}, u32[]{:S(2)}, u32[]{:S(2)}) collective-permute-start(bf16[1088,128]{1,0:T(8,128)(2,1)S(1)} %dynamic-slice_bitcast_fusion.1), channel_id=1, source_target_pairs={{0,32},{32,0},{64,96},{96,64},{128,160},{160,128},{192,224},{224,1... | collective-permute-start | bytes 835592 | tf_op jit(solution)/shard_map/ppermute | solution.py:399
  36.0 22.9 %copy-start = (s32[8]{0:T(128)S(1)}, s32[8]{0:T(128)}, u32[]{:S(2)}) copy-start(s32[8]{0:T(128)} %lengths_ref.11) | copy-start | bytes 100
  42.5 4.0 %collective-permute-start.6 = (bf16[272,128]{1,0:T(8,128)(2,1)S(1)}, bf16[272,128]{1,0:T(8,128)(2,1)S(1)}, u32[]{:S(2)}, u32[]{:S(2)}) collective-permute-start(bf16[272,128]{1,0:T(8,128)(2,1)S(1)} %get-tuple-element.90), channel_id=1, source_target_pairs={{0,64},{32,96},{64,0},{96,32},{128,192},{160,224},{192,128},{224,1... | collective-permute-start | bytes 208904 | tf_op jit(solution)/shard_map/ppermute | solution.py:399
  43.8 5.4 %collective-permute-start.7 = (bf16[272,128]{1,0:T(8,128)(2,1)S(1)}, bf16[272,128]{1,0:T(8,128)(2,1)S(1)}, u32[]{:S(2)}, u32[]{:S(2)}) collective-permute-start(bf16[272,128]{1,0:T(8,128)(2,1)S(1)} %get-tuple-element.92), channel_id=1, source_target_pairs={{0,128},{32,160},{64,192},{96,224},{128,0},{160,32},{192,64},{224,... | collective-permute-start | bytes 208904 | tf_op jit(solution)/shard_map/ppermute | solution.py:399
  46.5 5.4 %collective-permute-start.8 = (bf16[272,128]{1,0:T(8,128)(2,1)S(1)}, bf16[272,128]{1,0:T(8,128)(2,1)S(1)}, u32[]{:S(2)}, u32[]{:S(2)}) collective-permute-start(bf16[272,128]{1,0:T(8,128)(2,1)S(1)} %get-tuple-element.91), channel_id=1, source_target_pairs={{0,192},{32,224},{64,128},{96,160},{128,64},{160,96},{192,0},{224,... | collective-permute-start | bytes 208904 | tf_op jit(solution)/shard_map/ppermute | solution.py:399
  51.9 18.0 %collective-permute-start.10 = (bf16[272,128]{1,0:T(8,128)(2,1)S(1)}, bf16[272,128]{1,0:T(8,128)(2,1)S(1)}, u32[]{:S(2)}, u32[]{:S(2)}) collective-permute-start(bf16[272,128]{1,0:T(8,128)(2,1)S(1)} %fusion.3), channel_id=1, source_target_pairs={{0,16},{2,18},{4,20},{6,22},{8,24},{10,26},{12,28},{14,30},{16,0},... | collective-permute-start | bytes 208904 | tf_op jit(solution)/shard_map/ppermute | solution.py:399
  54.4 15.5 %collective-permute-start.11 = (bf16[272,128]{1,0:T(8,128)(2,1)S(1)}, bf16[272,128]{1,0:T(8,128)(2,1)S(1)}, u32[]{:S(2)}, u32[]{:S(2)}) collective-permute-start(bf16[272,128]{1,0:T(8,128)(2,1)S(1)} %fusion.3), channel_id=1, source_target_pairs={{0,18},{2,16},{4,22},{6,20},{8,26},{10,24},{12,30},{14,28},{16,2},... | collective-permute-start | bytes 208904 | tf_op jit(solution)/shard_map/ppermute | solution.py:399
  55.8 14.1 %collective-permute-start.9 = (bf16[272,128]{1,0:T(8,128)(2,1)S(1)}, bf16[272,128]{1,0:T(8,128)(2,1)S(1)}, u32[]{:S(2)}, u32[]{:S(2)}) collective-permute-start(bf16[272,128]{1,0:T(8,128)(2,1)S(1)} %fusion.3), channel_id=1, source_target_pairs={{0,2},{2,0},{4,6},{6,4},{8,10},{10,8},{12,14},{14,12},{16,18},{18,... | collective-permute-start | bytes 208904 | tf_op jit(solution)/shard_map/ppermute | solution.py:399
  59.9 12.5 %collective-permute-start.3 = (bf16[8,192,128]{2,1,0:T(8,128)(2,1)S(1)}, bf16[8,192,128]{2,1,0:T(8,128)(2,1)S(1)}, u32[]{:S(2)}, u32[]{:S(2)}) collective-permute-start(bf16[8,192,128]{2,1,0:T(8,128)(2,1)S(1)} %slice.9.x_ref), channel_id=1, source_target_pairs={{0,16},{16,0},{1,17},{17,1},{2,18},{18,2},{3,19},{19,3},{4,20},{20... | collective-permute-start | bytes 1179656 | tf_op jit(solution)/shard_map/ppermute | solution.py:446
  62.7 20.8 %collective-permute-start.2 = (bf16[8,208,128]{2,1,0:T(8,128)(2,1)S(1)}, bf16[8,208,128]{2,1,0:T(8,128)(2,1)S(1)}, u32[]{:S(2)}, u32[]{:S(2)}) collective-permute-start(bf16[8,208,128]{2,1,0:T(8,128)(2,1)S(1)} %slice.8.x_ref), channel_id=1, source_target_pairs={{0,1},{1,0},{2,3},{3,2},{4,5},{5,4},{6,7},{7,6},{8,9},{9,8},{10,11... | collective-permute-start | bytes 1277960 | tf_op jit(solution)/shard_map/ppermute | solution.py:446
  70.0 10.1 %collective-permute-start.12 = (bf16[272,128]{1,0:T(8,128)(2,1)S(1)}, bf16[272,128]{1,0:T(8,128)(2,1)S(1)}, u32[]{:S(2)}, u32[]{:S(2)}) collective-permute-start(bf16[272,128]{1,0:T(8,128)(2,1)S(1)} %add_convert_fusion.2), channel_id=1, source_target_pairs={{0,4},{2,6},{4,0},{6,2},{8,12},{10,14},{12,8},{14,10},{16,20},{18,... | collective-permute-start | bytes 208904 | tf_op jit(solution)/shard_map/ppermute | solution.py:399
  80.1 11.5 %collective-permute-start.13 = (bf16[272,128]{1,0:T(8,128)(2,1)S(1)}, bf16[272,128]{1,0:T(8,128)(2,1)S(1)}, u32[]{:S(2)}, u32[]{:S(2)}) collective-permute-start(bf16[272,128]{1,0:T(8,128)(2,1)S(1)} %add_convert_fusion.1), channel_id=1, source_target_pairs={{0,8},{2,10},{4,12},{6,14},{8,0},{10,2},{12,4},{14,6},{16,24},{18,... | collective-permute-start | bytes 208904 | tf_op jit(solution)/shard_map/ppermute | solution.py:399
  90.9 16.0 %collective-permute-start.14 = (bf16[8,192,128]{2,1,0:T(8,128)(2,1)S(1)}, bf16[8,192,128]{2,1,0:T(8,128)(2,1)S(1)}, u32[]{:S(2)}, u32[]{:S(2)}) collective-permute-start(bf16[8,192,128]{2,1,0:T(8,128)(2,1)S(1)} %get-tuple-element.75), channel_id=1, source_target_pairs={{0,16},{16,0},{1,17},{17,1},{2,18},{18,2},{3,19},{19,3},{4,20},{20... | collective-permute-start | bytes 1179656 | tf_op jit(solution)/shard_map/ppermute | solution.py:446
  91.6 14.3 %collective-permute-start.16 = (bf16[272,128]{1,0:T(8,128)(2,1)S(1)}, bf16[272,128]{1,0:T(8,128)(2,1)S(1)}, u32[]{:S(2)}, u32[]{:S(2)}) collective-permute-start(bf16[272,128]{1,0:T(8,128)(2,1)S(1)} %add_convert_fusion), channel_id=1, source_target_pairs={{0,192},{32,224},{64,128},{96,160},{128,64},{160,96},{192,0},{224,... | collective-permute-start | bytes 208904 | tf_op jit(solution)/shard_map/ppermute | solution.py:399
  92.2 13.7 %collective-permute-start.17 = (bf16[272,128]{1,0:T(8,128)(2,1)S(1)}, bf16[272,128]{1,0:T(8,128)(2,1)S(1)}, u32[]{:S(2)}, u32[]{:S(2)}) collective-permute-start(bf16[272,128]{1,0:T(8,128)(2,1)S(1)} %add_convert_fusion), channel_id=1, source_target_pairs={{0,128},{32,160},{64,192},{96,224},{128,0},{160,32},{192,64},{224,... | collective-permute-start | bytes 208904 | tf_op jit(solution)/shard_map/ppermute | solution.py:399
  92.7 13.2 %collective-permute-start.18 = (bf16[272,128]{1,0:T(8,128)(2,1)S(1)}, bf16[272,128]{1,0:T(8,128)(2,1)S(1)}, u32[]{:S(2)}, u32[]{:S(2)}) collective-permute-start(bf16[272,128]{1,0:T(8,128)(2,1)S(1)} %add_convert_fusion), channel_id=1, source_target_pairs={{0,64},{32,96},{64,0},{96,32},{128,192},{160,224},{192,128},{224,1... | collective-permute-start | bytes 208904 | tf_op jit(solution)/shard_map/ppermute | solution.py:399
  102.5 4.4 %collective-permute-start.15 = (bf16[8,96,128]{2,1,0:T(8,128)(2,1)S(1)}, bf16[8,96,128]{2,1,0:T(8,128)(2,1)S(1)}, u32[]{:S(2)}, u32[]{:S(2)}) collective-permute-start(bf16[8,96,128]{2,1,0:T(8,128)(2,1)S(1)} %get-tuple-element.77), channel_id=1, source_target_pairs={{0,1},{1,0},{2,3},{3,2},{4,5},{5,4},{6,7},{7,6},{8,9},{9,8},{10,11... | collective-permute-start | bytes 589832 | tf_op jit(solution)/shard_map/ppermute | solution.py:446
  106.1 8.3 %collective-permute-start.19 = (bf16[1088,128]{1,0:T(8,128)(2,1)S(1)}, bf16[1088,128]{1,0:T(8,128)(2,1)S(1)}, u32[]{:S(2)}, u32[]{:S(2)}) collective-permute-start(bf16[1088,128]{1,0:T(8,128)(2,1)S(1)} %pad_maximum_fusion.1), channel_id=1, source_target_pairs={{0,32},{32,0},{64,96},{96,64},{128,160},{160,128},{192,224},{224,1... | collective-permute-start | bytes 835592 | tf_op jit(solution)/shard_map/ppermute | solution.py:399
  107.9 23.4 %all-to-all-start.1 = ((bf16[8,288,128]{2,1,0:T(8,128)(2,1)}), bf16[8,288,128]{2,1,0:T(8,128)(2,1)S(1)}, u32[]{:S(2)}, u32[]{:S(2)}) async-start(bf16[8,288,128]{2,1,0:T(8,128)(2,1)} %shard_map.155), calls=%async_computation.1 | async-start | bytes 1179648 | tf_op jit(solution)/shard_map/all_to_all | solution.py:527
  114.5 2.5 %collective-permute-start.20 = (bf16[4,544,128]{2,1,0:T(8,128)(2,1)S(1)}, bf16[4,544,128]{2,1,0:T(8,128)(2,1)S(1)}, u32[]{:S(2)}, u32[]{:S(2)}) collective-permute-start(bf16[4,544,128]{2,1,0:T(8,128)(2,1)S(1)} %bitcast.26), channel_id=1, source_target_pairs={{0,1},{1,0},{2,3},{3,2},{4,5},{5,4},{6,7},{7,6},{8,9},{9,8},{10,11... | collective-permute-start | bytes 1671176 | tf_op jit(solution)/shard_map/ppermute | solution.py:446
  (3 other events, 14.6 us)
